TPU v7x, 128 devices: a whole 4x4x4 slice. The times are simulated.
128 devices in a mesh: seq: 16 (over y_lo, x, core), head: 8 (over z, y_hi).
Axes of the slice: x: 4, y: 4 (y_hi: 2, y_lo: 2; y = y_hi * 2 + y_lo), z: 4, core: 2. Of those that a mesh axis runs over, the one named last changes fastest.
Arguments:
- queries: bfloat16 [3072, 8192], P('seq', 'head'), may hold values from -1024 to 1024
- image_keys: bfloat16 [25616, 1024], P('seq', 'head'), may hold values from -8 to 8
- image_values: bfloat16 [25616, 1024], P('seq', 'head'), may hold values from -6 to 6
- layer_input: bfloat16 [3072, 8192], P('seq', 'head'), may hold values from -6 to 6
- out_weight: bfloat16 [8192, 8192], P('head'), may hold values from -0.09375 to 0.09375
- tile_counts: int32 [8], replicated, may hold values from 1 to 4, as said below
- image_range: int32 [2, 3072], P(None, 'seq'), may hold values from 0 to 8, as said below
- attn_gate: float32 [1], replicated, may hold values from 0.5 to 1.5
Outputs:
- layer_out: bfloat16 [3072, 8192], P('seq', 'head')
Inputs may be any that keep to these rules, and one draw needn't show every extreme that they name: `tile_counts`: each image has 1 to 4 tiles and together they have 16; some image has exactly 4. Images are numbered in text order. For every token t, image_range[0, t] <= image_range[1, t]; image_range[1, t] never decreases as t grows; image_range[1, 0] = 0, so tokens before the first image attend to none.
All inputs are finite; a program needn't handle non-finite values.
Results may differ from a plain program's by a relative error of at most 0.0055.
Values may be sent and summed in bfloat16 or wider, within the bound.
No kernel may reach another device: no remote copies, remote signals or barrier semaphores. Data moves between devices by JAX's collectives and lax.ppermute only.
A program may use at most 512 MiB of HBM per device.

v0:
```python
import math

import jax
import jax.numpy as jnp
from jax import lax
from jax.experimental import pallas as pl
from jax.experimental.pallas import tpu as pltpu
from jax.sharding import Mesh
from jax.sharding import PartitionSpec as P

SEQ = ("y", "x", "core")
HEAD = ("z", "yh")
CHUNK = 32
LOWEST = -1e30
BLOCKED = 1e30
GROUPS = ((2, 1, 3, 0),)
BF16 = jnp.bfloat16
F32 = jnp.float32


def shifted(value, axis, steps):
    count = lax.axis_size(axis)
    return lax.ppermute(value, axis, [(s, (s + steps) % count) for s in range(count)])


def head_shifted(value, dz, dy):
    nz, ny = lax.axis_size("z"), lax.axis_size("yh")
    pairs = []
    for z in range(nz):
        for y in range(ny):
            pairs.append((z * ny + y, (z + dz) % nz * ny + (y + dy) % ny))
    return lax.ppermute(value, HEAD, pairs)


def attend_kernel(items, count, images, *refs, scale, hd, group, blocks, keys, padded):
    q_refs = refs[:blocks]
    bounds_ref = refs[blocks]
    key_refs = refs[blocks + 1 : blocks + 5]
    value_refs = refs[blocks + 5 : blocks + 9]
    out_refs = refs[blocks + 9 : 2 * blocks + 9]
    q_all, key_all, value_all, first_s, second_s, first_b, second_b, top_ref, acc_ref, sems = refs[
        2 * blocks + 9 :
    ]
    tokens = out_refs[0].shape[0]
    rows = CHUNK * group
    factor = scale * math.log2(math.e)
    copies = []
    for j in range(4):
        copies.append(pltpu.make_async_copy(key_refs[j], key_all.at[j], sems.at[2 * j]))
        copies.append(
            pltpu.make_async_copy(value_refs[j], value_all.at[j, :, pl.ds(0, hd)], sems.at[2 * j + 1])
        )
    for i in range(blocks):
        copies.append(
            pltpu.make_async_copy(
                q_refs[i].at[pl.ds(0, tokens)], q_all.at[pl.ds(i * tokens, tokens)], sems.at[8 + i]
            )
        )
    for copy in copies:
        copy.start()
    place = lax.broadcasted_iota(jnp.int32, (padded, hd), 0)
    ones = jnp.where(place < keys, 1.0, 0.0).astype(BF16)
    for j in range(4):
        value_all[j, :, hd:] = ones
    top_ref[...] = jnp.full(top_ref.shape, LOWEST, F32)
    acc_ref[...] = jnp.zeros(acc_ref.shape, F32)
    for copy in copies:
        copy.wait()

    def where_is(i):
        item = items[i]
        return item // 8, item % 4, jnp.where(item % 8 < 4, images[item % 4], -1)

    def score(i, scores_ref, best_ref):
        chunk, j, _ = where_is(i)
        at = pl.ds(pl.multiple_of(chunk * CHUNK, CHUNK), CHUNK)
        q = jnp.concatenate([q_all[at, h * hd : (h + 1) * hd] for h in range(group)], axis=0)
        best = None
        for k in range(0, padded, 128):
            part = jnp.dot(q, key_all[j, :, k : k + 128], preferred_element_type=F32)
            scores_ref[:, k : k + 128] = part
            best = part if best is None else jnp.maximum(best, part)
        best_ref[...] = jnp.broadcast_to(jnp.max(best, axis=1, keepdims=True), best_ref.shape)

    def absorb(i, scores_ref, best_ref):
        chunk, j, image = where_is(i)
        at = pl.ds(pl.multiple_of(chunk * rows, rows), rows)
        near = pl.ds(pl.multiple_of(chunk * CHUNK, CHUNK), CHUNK)
        low = jnp.concatenate([bounds_ref[near, 0:1]] * group, axis=0)
        high = jnp.concatenate([bounds_ref[near, 1:2]] * group, axis=0)
        allowed = (low <= image) & (image < high)
        old = top_ref[at, 0:1]
        new = jnp.where(allowed, jnp.maximum(old, best_ref[:, 0:1]), old)
        anchor = jnp.where(allowed, new, BLOCKED)
        rescale = jnp.exp2((old - new) * factor)
        top_ref[at, :] = jnp.broadcast_to(new, (rows, hd))
        weights = jnp.exp2((scores_ref[...] - anchor) * factor).astype(BF16)
        mixed = jnp.dot(weights, value_all[j], preferred_element_type=F32)
        acc_ref[at, :] = acc_ref[at, :] * rescale + mixed

    def pair(k, carry):
        i = 2 * k
        score(i + 1, second_s, second_b)
        absorb(i, first_s, first_b)
        score(i + 2, first_s, first_b)
        absorb(i + 1, second_s, second_b)
        return carry

    score(0, first_s, first_b)
    lax.fori_loop(0, (count[0] + 1) // 2, pair, 0)

    lane = lax.broadcasted_iota(jnp.int32, (CHUNK, hd), 1)
    for c in range(blocks * tokens // CHUNK):
        at = pl.ds(c * rows, rows)
        out_ref = out_refs[c * CHUNK // tokens]
        near = pl.ds(c * CHUNK % tokens, CHUNK)
        total = acc_ref[at, hd:]
        seen = total > 0
        safe = jnp.where(seen, total, 1.0)
        mean = (acc_ref[at, :hd] / safe).astype(BF16)
        logsum = jnp.where(seen, top_ref[at, :] * scale + jnp.log(safe), LOWEST)
        spread = jnp.zeros((CHUNK, hd), F32)
        for h in range(group):
            mine = slice(h * CHUNK, (h + 1) * CHUNK)
            out_ref[near, h * hd : (h + 1) * hd] = mean[mine]
            hi = logsum[mine].astype(BF16).astype(F32)
            mid = (logsum[mine] - hi).astype(BF16).astype(F32)
            lo = logsum[mine] - hi - mid
            spread = jnp.where(lane == h, hi, spread)
            spread = jnp.where(lane == h + group, mid, spread)
            spread = jnp.where(lane == h + 2 * group, lo, spread)
        out_ref[near, group * hd :] = spread.astype(BF16)


def attend(payloads, bounds, items, count, images, keys_t, values, keys, tokens):
    blocks = len(payloads)
    width = payloads[0].shape[1]
    hd, padded = keys_t[0].shape
    group = width // hd
    rows = CHUNK * group
    apart = pl.BlockSpec(memory_space=pl.ANY)
    here = pl.BlockSpec(memory_space=pltpu.VMEM)
    result = jax.ShapeDtypeStruct((tokens, width + hd), BF16)
    return pl.pallas_call(
        lambda *refs: attend_kernel(
            *refs, scale=1.0 / math.sqrt(hd), hd=hd, group=group, blocks=blocks, keys=keys, padded=padded
        ),
        out_shape=[result] * blocks,
        grid_spec=pltpu.PrefetchScalarGridSpec(
            num_scalar_prefetch=3,
            grid=(),
            in_specs=[apart] * blocks + [here] + [apart] * 8,
            out_specs=[here] * blocks,
            scratch_shapes=[
                pltpu.VMEM((blocks * tokens, width), BF16),
                pltpu.VMEM((4, hd, padded), BF16),
                pltpu.VMEM((4, padded, 2 * hd), BF16),
                pltpu.VMEM((rows, padded), F32),
                pltpu.VMEM((rows, padded), F32),
                pltpu.VMEM((rows, hd), F32),
                pltpu.VMEM((rows, hd), F32),
                pltpu.VMEM((blocks * tokens * group, hd), F32),
                pltpu.VMEM((blocks * tokens * group, 2 * hd), F32),
                pltpu.SemaphoreType.DMA((8 + blocks,)),
            ],
        ),
        compiler_params=pltpu.CompilerParams(vmem_limit_bytes=40 << 20),
        cost_estimate=pl.CostEstimate(
            flops=2 * blocks * tokens * group * padded * 2 * hd,
            bytes_accessed=blocks * tokens * width * 4 + padded * hd * 16,
            transcendentals=blocks * tokens * group * padded * 2,
        ),
        name="attend",
    )(items, count, images, *payloads, bounds, *keys_t, *values)


def work_list(hits, images):
    tokens, tiles = hits.shape
    flags = jnp.any(hits.reshape(tokens // CHUNK, CHUNK, tiles), axis=1).reshape(-1)
    size = flags.shape[0]
    place = jnp.arange(size, dtype=jnp.int32)
    rank = jnp.sum((place[None, :] < place[:, None]) & flags[None, :], axis=1)
    count = jnp.sum(flags.astype(jnp.int32))
    code = place // tiles * 8 + place % tiles + 1
    slot = jnp.arange(size + 3, dtype=jnp.int32)
    chosen = (rank[None, :] == slot[:, None]) & flags[None, :]
    items = jnp.sum(jnp.where(chosen, code[None, :], 0), axis=1)
    items = jnp.where(items > 0, items - 1, 4)
    return items.astype(jnp.int32), count.reshape(1)


def combine_kernel(order_ref, a_ref, b_ref, c_ref, d_ref, out_ref, *, hd, group):
    parts = (a_ref, b_ref, c_ref, d_ref)
    width = group * hd
    sums = []
    for ref in parts:
        pieces = ref[:, width:].astype(F32)
        sums.append(pieces[:, :group] + pieces[:, group : 2 * group] + pieces[:, 2 * group : 3 * group])
    top = jnp.maximum(jnp.maximum(sums[0], sums[1]), jnp.maximum(sums[2], sums[3]))
    shares = [jnp.exp(s - top) for s in sums]
    total = shares[0] + shares[1] + shares[2] + shares[3]
    shares = [s / total for s in shares]
    for h in range(group):
        at = slice(h * hd, (h + 1) * hd)
        mixed = parts[0][:, at].astype(F32) * shares[0][:, h : h + 1]
        for ref, share in zip(parts[1:], shares[1:]):
            mixed = mixed + ref[:, at].astype(F32) * share[:, h : h + 1]
        mixed = lax.dot_general(
            order_ref[...], mixed.astype(BF16), (((0,), (0,)), ((), ())), preferred_element_type=F32
        )
        out_ref[:, at] = mixed.astype(BF16)


def combine(order, parts, hd):
    tokens, wide = parts[0].shape
    width = wide - hd
    return pl.pallas_call(
        lambda *refs: combine_kernel(*refs, hd=hd, group=width // hd),
        out_shape=jax.ShapeDtypeStruct((tokens, width), BF16),
        cost_estimate=pl.CostEstimate(
            flops=8 * tokens * width, bytes_accessed=10 * tokens * width, transcendentals=tokens * 32
        ),
        compiler_params=pltpu.CompilerParams(vmem_limit_bytes=32 << 20),
        name="combine",
    )(order, *parts)


def project_kernel(block, a_ref, w_ref, out_ref):
    out_ref[...] = jnp.dot(a_ref[...], w_ref[...], preferred_element_type=F32).astype(BF16)


def project(attended, weight, block, width):
    tokens, depth = attended.shape
    cuts = 4
    step = width // cuts
    return pl.pallas_call(
        project_kernel,
        out_shape=jax.ShapeDtypeStruct((tokens, width), BF16),
        grid_spec=pltpu.PrefetchScalarGridSpec(
            num_scalar_prefetch=1,
            grid=(cuts,),
            in_specs=[
                pl.BlockSpec((tokens, depth), lambda g, b: (0, 0)),
                pl.BlockSpec((depth, step), lambda g, b: (0, b[0] * cuts + g)),
            ],
            out_specs=pl.BlockSpec((tokens, step), lambda g, b: (0, g)),
        ),
        cost_estimate=pl.CostEstimate(
            flops=2 * tokens * depth * width,
            bytes_accessed=2 * (depth * width + tokens * (depth + width)),
            transcendentals=0,
        ),
        compiler_params=pltpu.CompilerParams(vmem_limit_bytes=56 << 20),
        name="project",
    )(block.reshape(1), attended, weight)


def shards(
    queries, image_keys, image_values, layer_input, out_weight, tile_counts, image_range, attn_gate
):
    tokens, width = queries.shape
    hd = image_keys.shape[1]
    y, x, core = (lax.axis_index(n) for n in SEQ)
    z, yh = (lax.axis_index(n) for n in HEAD)
    nx, nc = lax.axis_size("x"), lax.axis_size("core")
    ny = lax.axis_size("y")
    nz, nyh = lax.axis_size("z"), lax.axis_size("yh")

    keys = image_keys.shape[0]
    padded = -(-keys // 128) * 128
    spare = jnp.broadcast_to(image_keys[:1], (padded - keys, hd))
    key_t = jnp.concatenate([image_keys, spare], axis=0).T
    value = jnp.pad(image_values, ((0, padded - keys), (0, 0)))
    own = (key_t, value)
    across = [shifted(v, "y", 1) for v in own]
    beside = [shifted(v, "core", 1) for v in own]

    low, high = image_range[0], image_range[1]
    grade = jnp.where(low < high, low * 16 + high, 1 << 10)
    place = jnp.arange(tokens, dtype=jnp.int32)
    ahead = (grade[None, :] < grade[:, None]) | (
        (grade[None, :] == grade[:, None]) & (place[None, :] < place[:, None])
    )
    rank = jnp.sum(ahead.astype(jnp.int32), axis=1)
    order = (rank[None, :] == place[:, None]).astype(BF16)
    sorted_q = jnp.dot(order, queries, preferred_element_type=F32).astype(BF16)
    sorted_range = jnp.dot(image_range.astype(BF16), order.T, preferred_element_type=F32).astype(BF16)
    edge = jnp.pad(sorted_range, ((0, 14), (0, width - tokens)))
    payload = jnp.concatenate([sorted_q, edge], axis=0)
    payloads = [payload] + [shifted(payload, "x", s) for s in (1, 2, 3)]
    diagonal = [shifted(v, "core", 1) for v in across]
    tiles = (own, beside, across, diagonal)

    def number(yy, cc):
        return (yy % ny * nx + x) * nc + cc % nc

    held = jnp.stack([number(y, core), number(y, core + 1), number(y + 1, core), number(y + 1, core + 1)])
    image = jnp.arange(tile_counts.shape[0])
    ends = jnp.sum(jnp.where(image[None, :] <= image[:, None], tile_counts[None, :], 0), axis=1)
    images = jnp.sum((ends[None, :] <= held[:, None]).astype(jnp.int32), axis=1)

    returned = []
    for turns in GROUPS:
        got = [payloads[s] for s in turns]
        reach = jnp.concatenate([p[tokens : tokens + 2, :tokens] for p in got], axis=1).astype(jnp.int32)
        hits = (reach[0][:, None] <= images[None, :]) & (images[None, :] < reach[1][:, None])
        items, count = work_list(hits, images)
        parts = attend(
            got, reach.T, items, count, images, [t[0] for t in tiles], [t[1] for t in tiles], keys, tokens
        )
        for s, part in zip(turns, parts):
            returned.append(part if s == 0 else shifted(part, "x", nx - s))
    attended = combine(order, returned, hd)

    total = None
    for dz, dy in ((2, 1), (1, 1), (3, 1), (2, 0), (0, 1), (1, 0), (3, 0), (0, 0)):
        block = (z + dz) % nz * nyh + (yh + dy) % nyh
        term = project(attended, out_weight, block, layer_input.shape[1])
        if (dz, dy) != (0, 0):
            term = head_shifted(term, dz, dy)
        term = term.astype(F32)
        total = term if total is None else total + term
    gate = jnp.tanh(attn_gate[0])
    return (layer_input.astype(F32) + gate * total).astype(BF16)


def solution(mesh):
    split = Mesh(mesh.devices.reshape(2, 4, 2, 4, 2), ("y", "x", "core", "z", "yh"))
    return jax.shard_map(
        shards,
        mesh=split,
        in_specs=(
            P(SEQ, HEAD),
            P(SEQ, HEAD),
            P(SEQ, HEAD),
            P(SEQ, HEAD),
            P(HEAD, None),
            P(),
            P(None, SEQ),
            P(),
        ),
        out_specs=P(SEQ, HEAD),
        check_vma=False,
    )
```

profile of v0, /device:TPU:8, one launch (start us, length us, event | category | flops | bytes accessed | tf_op | source)
XLA Modules:
  0.0 141.1 jit_solution(17484441114382240491)
XLA Ops:
  2.1 3.1 %collective-permute-start = (bf16[208,1024]{1,0:T(8,128)(2,1)S(1)}, bf16[208,1024]{1,0:T(8,128)(2,1)S(1)}, u32[]{:S(2)}, u32[]{:S(2)}) collective-permute-start(bf16[208,1024]{1,0:T(8,128)(2,1)S(1)} %fusion.2.refs_6_), channel_id=1, source_target_pairs={{0,32},{16,48},{32,0},{48,16},{1,33},{17,49},{33,1},{49,17},{2,34}... | collective-permute-start | bytes 1277960 | tf_op jit(solution)/shard_map/ppermute | solution.py:23
  5.8 2.6 %collective-permute-start.2 = (bf16[208,1024]{1,0:T(8,128)(2,1)S(1)}, bf16[208,1024]{1,0:T(8,128)(2,1)S(1)}, u32[]{:S(2)}, u32[]{:S(2)}) collective-permute-start(bf16[208,1024]{1,0:T(8,128)(2,1)S(1)} %fusion.2.refs_6_), channel_id=1, source_target_pairs={{0,48},{16,0},{32,16},{48,32},{1,49},{17,1},{33,17},{49,33},{2,50}... | collective-permute-start | bytes 1277960 | tf_op jit(solution)/shard_map/ppermute | solution.py:23
  13.2 3.3 %collective-permute-done.refs_3_ = bf16[208,1024]{1,0:T(8,128)(2,1)S(1)} collective-permute-done((bf16[208,1024]{1,0:T(8,128)(2,1)S(1)}, bf16[208,1024]{1,0:T(8,128)(2,1)S(1)}, u32[]{:S(2)}, u32[]{:S(2)}) %collective-permute-start) | collective-permute-done | bytes 426016 | tf_op jit(solution)/shard_map/ppermute | solution.py:23
  16.9 7.5 %collective-permute-done.1.refs_4_ = bf16[208,1024]{1,0:T(8,128)(2,1)S(1)} collective-permute-done((bf16[208,1024]{1,0:T(8,128)(2,1)S(1)}, bf16[208,1024]{1,0:T(8,128)(2,1)S(1)}, u32[]{:S(2)}, u32[]{:S(2)}) %collective-permute-start.1) | collective-permute-done | bytes 426016 | tf_op jit(solution)/shard_map/ppermute | solution.py:23
  28.0 2.6 %collective-permute-done.7.refs_14_ = bf16[1664,128]{1,0:T(8,128)(2,1)} collective-permute-done((bf16[1664,128]{1,0:T(8,128)(2,1)S(1)}, bf16[1664,128]{1,0:T(8,128)(2,1)}, u32[]{:S(2)}, u32[]{:S(2)}) %collective-permute-start.7) | collective-permute-done | bytes 426016 | tf_op jit(solution)/shard_map/ppermute | solution.py:23
  33.6 22.4 %attend.1 = (bf16[192,1152]{1,0:T(8,128)(2,1)}, bf16[192,1152]{1,0:T(8,128)(2,1)}, bf16[192,1152]{1,0:T(8,128)(2,1)}, bf16[192,1152]{1,0:T(8,128)(2,1)S(1)}) custom-call(s32[99]{0:T(128)S(1)} %compare_select_fusion.1.refs_0_, s32[1]{0:T(128)} %bitcast.10.refs_1_, s32[4]{0:T(128)S(1)} %convert_reduce_fusion.3.refs_2_, ...), custom_call_target="tpu_custom_call" | custom-call | flops 5234491392 | bytes 6553600 | tf_op jit(solution)/shard_map/attend/pallas_call | solution.py:144
  56.1 3.2 %collective-permute-start.11 = (bf16[192,1152]{1,0:T(8,128)(2,1)}, bf16[192,1152]{1,0:T(8,128)(2,1)S(1)}, u32[]{:S(2)}, u32[]{:S(2)}) collective-permute-start(bf16[192,1152]{1,0:T(8,128)(2,1)} %get-tuple-element.11), channel_id=1, source_target_pairs={{0,16},{16,32},{32,48},{48,0},{1,17},{17,33},{33,49},{49,1},{2,18}... | collective-permute-start | bytes 1327112 | tf_op jit(solution)/shard_map/ppermute | solution.py:23
  59.3 2.0 %collective-permute-start.9 = (bf16[192,1152]{1,0:T(8,128)(2,1)}, bf16[192,1152]{1,0:T(8,128)(2,1)S(1)}, u32[]{:S(2)}, u32[]{:S(2)}) collective-permute-start(bf16[192,1152]{1,0:T(8,128)(2,1)} %get-tuple-element.9), channel_id=1, source_target_pairs={{0,32},{16,48},{32,0},{48,16},{1,33},{17,49},{33,1},{49,17},{2,34}... | collective-permute-start | bytes 1327112 | tf_op jit(solution)/shard_map/ppermute | solution.py:23
  61.3 8.5 %collective-permute-done.10.refs_2_ = bf16[192,1152]{1,0:T(8,128)(2,1)S(1)} collective-permute-done((bf16[192,1152]{1,0:T(8,128)(2,1)}, bf16[192,1152]{1,0:T(8,128)(2,1)S(1)}, u32[]{:S(2)}, u32[]{:S(2)}) %collective-permute-start.10) | collective-permute-done | bytes 442400 | tf_op jit(solution)/shard_map/ppermute | solution.py:23
  69.9 10.2 %collective-permute-done.9.refs_1_ = bf16[192,1152]{1,0:T(8,128)(2,1)S(1)} collective-permute-done((bf16[192,1152]{1,0:T(8,128)(2,1)}, bf16[192,1152]{1,0:T(8,128)(2,1)S(1)}, u32[]{:S(2)}, u32[]{:S(2)}) %collective-permute-start.9) | collective-permute-done | bytes 442400 | tf_op jit(solution)/shard_map/ppermute | solution.py:23
  82.3 4.1 %project.8 = bf16[192,1024]{1,0:T(8,128)(2,1)} custom-call(s32[1]{0:T(128)} %bitcast.1.block, bf16[192,1024]{1,0:T(8,128)(2,1)} %copy-done.1, bf16[1024,8192]{1,0:T(8,128)(2,1)} %w_ref.15), custom_call_target="tpu_custom_call" | custom-call | flops 402653184 | bytes 2883584 | tf_op jit(solution)/shard_map/project/pallas_call | solution.py:236
  86.4 5.6 %collective-permute-start.12 = (bf16[192,1024]{1,0:T(8,128)(2,1)}, bf16[192,1024]{1,0:T(8,128)(2,1)S(1)}, u32[]{:S(2)}, u32[]{:S(2)}) collective-permute-start(bf16[192,1024]{1,0:T(8,128)(2,1)} %project.8), channel_id=1, source_target_pairs={{0,5},{1,4},{2,7},{3,6},{4,1},{5,0},{6,3},{7,2},{8,13},{9,12},{10,... | collective-permute-start | bytes 1179656 | tf_op jit(solution)/shard_map/ppermute | solution.py:32
  92.0 4.1 %project.9 = bf16[192,1024]{1,0:T(8,128)(2,1)} custom-call(s32[1]{0:T(128)} %bitcast.14.block, bf16[192,1024]{1,0:T(8,128)(2,1)} %copy-done.1, bf16[1024,8192]{1,0:T(8,128)(2,1)} %w_ref.15), custom_call_target="tpu_custom_call" | custom-call | flops 402653184 | bytes 2883584 | tf_op jit(solution)/shard_map/project/pallas_call | solution.py:236
  96.1 1.7 %collective-permute-start.13 = (bf16[192,1024]{1,0:T(8,128)(2,1)}, bf16[192,1024]{1,0:T(8,128)(2,1)S(1)}, u32[]{:S(2)}, u32[]{:S(2)}) collective-permute-start(bf16[192,1024]{1,0:T(8,128)(2,1)} %project.9), channel_id=1, source_target_pairs={{0,3},{1,2},{2,5},{3,4},{4,7},{5,6},{6,1},{7,0},{8,11},{9,10},{10,... | collective-permute-start | bytes 1179656 | tf_op jit(solution)/shard_map/ppermute | solution.py:32
  97.8 4.1 %project.10 = bf16[192,1024]{1,0:T(8,128)(2,1)} custom-call(s32[1]{0:T(128)} %bitcast.15.block, bf16[192,1024]{1,0:T(8,128)(2,1)} %copy-done.1, bf16[1024,8192]{1,0:T(8,128)(2,1)} %w_ref.15), custom_call_target="tpu_custom_call" | custom-call | flops 402653184 | bytes 2883584 | tf_op jit(solution)/shard_map/project/pallas_call | solution.py:236
  101.9 3.9 %collective-permute-start.14 = (bf16[192,1024]{1,0:T(8,128)(2,1)}, bf16[192,1024]{1,0:T(8,128)(2,1)S(1)}, u32[]{:S(2)}, u32[]{:S(2)}) collective-permute-start(bf16[192,1024]{1,0:T(8,128)(2,1)} %project.10), channel_id=1, source_target_pairs={{0,7},{1,6},{2,1},{3,0},{4,3},{5,2},{6,5},{7,4},{8,15},{9,14},{10,... | collective-permute-start | bytes 1179656 | tf_op jit(solution)/shard_map/ppermute | solution.py:32
  105.8 4.1 %project.11 = bf16[192,1024]{1,0:T(8,128)(2,1)} custom-call(s32[1]{0:T(128)} %bitcast.16.block, bf16[192,1024]{1,0:T(8,128)(2,1)} %copy-done.1, bf16[1024,8192]{1,0:T(8,128)(2,1)} %w_ref.15), custom_call_target="tpu_custom_call" | custom-call | flops 402653184 | bytes 2883584 | tf_op jit(solution)/shard_map/project/pallas_call | solution.py:236
  109.9 4.1 %project.13 = bf16[192,1024]{1,0:T(8,128)(2,1)} custom-call(s32[1]{0:T(128)} %bitcast.18.block, bf16[192,1024]{1,0:T(8,128)(2,1)} %copy-done.1, bf16[1024,8192]{1,0:T(8,128)(2,1)} %w_ref.15), custom_call_target="tpu_custom_call" | custom-call | flops 402653184 | bytes 2883584 | tf_op jit(solution)/shard_map/project/pallas_call | solution.py:236
  114.4 4.2 %project.14 = bf16[192,1024]{1,0:T(8,128)(2,1)} custom-call(s32[1]{0:T(128)} %bitcast.19.block, bf16[192,1024]{1,0:T(8,128)(2,1)} %copy-done.1, bf16[1024,8192]{1,0:T(8,128)(2,1)} %w_ref.15), custom_call_target="tpu_custom_call" | custom-call | flops 402653184 | bytes 2883584 | tf_op jit(solution)/shard_map/project/pallas_call | solution.py:236
  118.5 4.1 %project.12 = bf16[192,1024]{1,0:T(8,128)(2,1)} custom-call(s32[1]{0:T(128)} %bitcast.17.block, bf16[192,1024]{1,0:T(8,128)(2,1)} %copy-done.1, bf16[1024,8192]{1,0:T(8,128)(2,1)} %w_ref.15), custom_call_target="tpu_custom_call" | custom-call | flops 402653184 | bytes 2883584 | tf_op jit(solution)/shard_map/project/pallas_call | solution.py:236
  122.7 2.9 %collective-permute-start.18 = (bf16[192,1024]{1,0:T(8,128)(2,1)}, bf16[192,1024]{1,0:T(8,128)(2,1)S(1)}, u32[]{:S(2)}, u32[]{:S(2)}) collective-permute-start(bf16[192,1024]{1,0:T(8,128)(2,1)} %project.14), channel_id=1, source_target_pairs={{0,6},{1,7},{2,0},{3,1},{4,2},{5,3},{6,4},{7,5},{8,14},{9,15},{10,... | collective-permute-start | bytes 1179656 | tf_op jit(solution)/shard_map/ppermute | solution.py:32
  127.5 4.1 %project.15 = bf16[192,1024]{1,0:T(8,128)(2,1)} custom-call(s32[1]{0:T(128)} %bitcast.20.block, bf16[192,1024]{1,0:T(8,128)(2,1)} %copy-done.1, bf16[1024,8192]{1,0:T(8,128)(2,1)} %w_ref.15), custom_call_target="tpu_custom_call" | custom-call | flops 402653184 | bytes 2883584 | tf_op jit(solution)/shard_map/project/pallas_call | solution.py:236
  132.0 5.3 %collective-permute-done.18 = bf16[192,1024]{1,0:T(8,128)(2,1)S(1)} collective-permute-done((bf16[192,1024]{1,0:T(8,128)(2,1)}, bf16[192,1024]{1,0:T(8,128)(2,1)S(1)}, u32[]{:S(2)}, u32[]{:S(2)}) %collective-permute-start.18) | collective-permute-done | bytes 393248 | tf_op jit(solution)/shard_map/ppermute | solution.py:32
  138.7 2.5 %add_convert_fusion = bf16[192,1024]{1,0:T(8,128)(2,1)} fusion(bf16[192,1024]{1,0:T(8,128)(2,1)} %project.15, bf16[192,1024]{1,0:T(8,128)(2,1)S(1)} %collective-permute-done.18, bf16[192,1024]{1,0:T(8,128)(2,1)S(1)} %collective-permute-done.17, bf16[192,1024]{1,0:T(8,128)(2,1)S(1)} %collective-permute-done.16, ...), kind=kLoop, calls=%fused_computation.5 | loop fusion | flops 3735552 | bytes 3932164 | tf_op jit(solution)/shard_map/convert_element_type | solution.py:324
  (67 shorter events, 20.2 us)
Async XLA Ops:
  0.0 1.8 %copy-start = (bf16[192,1024]{1,0:T(8,128)(2,1)S(1)}, bf16[192,1024]{1,0:T(8,128)(2,1)}, u32[]{:S(2)}) copy-start(bf16[192,1024]{1,0:T(8,128)(2,1)} %param.8) | copy-start | bytes 1179652
  2.1 14.3 %collective-permute-start = (bf16[208,1024]{1,0:T(8,128)(2,1)S(1)}, bf16[208,1024]{1,0:T(8,128)(2,1)S(1)}, u32[]{:S(2)}, u32[]{:S(2)}) collective-permute-start(bf16[208,1024]{1,0:T(8,128)(2,1)S(1)} %fusion.2.refs_6_), channel_id=1, source_target_pairs={{0,32},{16,48},{32,0},{48,16},{1,33},{17,49},{33,1},{49,17},{2,34}... | collective-permute-start | bytes 1277960 | tf_op jit(solution)/shard_map/ppermute | solution.py:23
  5.2 19.2 %collective-permute-start.1 = (bf16[208,1024]{1,0:T(8,128)(2,1)S(1)}, bf16[208,1024]{1,0:T(8,128)(2,1)S(1)}, u32[]{:S(2)}, u32[]{:S(2)}) collective-permute-start(bf16[208,1024]{1,0:T(8,128)(2,1)S(1)} %fusion.2.refs_6_), channel_id=1, source_target_pairs={{0,16},{16,32},{32,48},{48,0},{1,17},{17,33},{33,49},{49,1},{2,18}... | collective-permute-start | bytes 1277960 | tf_op jit(solution)/shard_map/ppermute | solution.py:23
  5.8 18.7 %collective-permute-start.2 = (bf16[208,1024]{1,0:T(8,128)(2,1)S(1)}, bf16[208,1024]{1,0:T(8,128)(2,1)S(1)}, u32[]{:S(2)}, u32[]{:S(2)}) collective-permute-start(bf16[208,1024]{1,0:T(8,128)(2,1)S(1)} %fusion.2.refs_6_), channel_id=1, source_target_pairs={{0,48},{16,0},{32,16},{48,32},{1,49},{17,1},{33,17},{49,33},{2,50}... | collective-permute-start | bytes 1277960 | tf_op jit(solution)/shard_map/ppermute | solution.py:23
  10.6 16.9 %collective-permute-start.4 = (bf16[128,1664]{1,0:T(8,128)(2,1)S(1)}, bf16[128,1664]{1,0:T(8,128)(2,1)}, u32[]{:S(2)}, u32[]{:S(2)}) collective-permute-start(bf16[128,1664]{1,0:T(8,128)(2,1)S(1)} %maximum_bitcast_fusion.refs_8_), channel_id=1, source_target_pairs={{0,64},{64,0},{1,65},{65,1},{2,66},{66,2},{3,67},{67,3},{4,68},{68... | collective-permute-start | bytes 1277960 | tf_op jit(solution)/shard_map/ppermute | solution.py:23
  11.1 20.3 %collective-permute-start.3 = (bf16[128,1664]{1,0:T(8,128)(2,1)S(1)}, bf16[128,1664]{1,0:T(8,128)(2,1)}, u32[]{:S(2)}, u32[]{:S(2)}) collective-permute-start(bf16[128,1664]{1,0:T(8,128)(2,1)S(1)} %maximum_bitcast_fusion.refs_8_), channel_id=1, source_target_pairs={{0,8},{8,0},{1,9},{9,1},{2,10},{10,2},{3,11},{11,3},{4,12},{12,4},... | collective-permute-start | bytes 1277960 | tf_op jit(solution)/shard_map/ppermute | solution.py:23
  16.5 14.2 %collective-permute-start.7 = (bf16[1664,128]{1,0:T(8,128)(2,1)S(1)}, bf16[1664,128]{1,0:T(8,128)(2,1)}, u32[]{:S(2)}, u32[]{:S(2)}) collective-permute-start(bf16[1664,128]{1,0:T(8,128)(2,1)S(1)} %pad.9.refs_12_), channel_id=1, source_target_pairs={{0,64},{64,0},{1,65},{65,1},{2,66},{66,2},{3,67},{67,3},{4,68},{68... | collective-permute-start | bytes 1277960 | tf_op jit(solution)/shard_map/ppermute | solution.py:23
  24.4 7.0 %collective-permute-start.6 = (bf16[1664,128]{1,0:T(8,128)(2,1)S(1)}, bf16[1664,128]{1,0:T(8,128)(2,1)}, u32[]{:S(2)}, u32[]{:S(2)}) collective-permute-start(bf16[1664,128]{1,0:T(8,128)(2,1)S(1)} %pad.9.refs_12_), channel_id=1, source_target_pairs={{0,8},{8,0},{1,9},{9,1},{2,10},{10,2},{3,11},{11,3},{4,12},{12,4},... | collective-permute-start | bytes 1277960 | tf_op jit(solution)/shard_map/ppermute | solution.py:23
  24.5 8.1 %copy-start.2 = (bf16[208,1024]{1,0:T(8,128)(2,1)}, bf16[208,1024]{1,0:T(8,128)(2,1)S(1)}, u32[]{:S(2)}) copy-start(bf16[208,1024]{1,0:T(8,128)(2,1)S(1)} %collective-permute-done.2.refs_5_) | copy-start | bytes 1277956
  27.4 4.0 %collective-permute-start.5 = (bf16[128,1664]{1,0:T(8,128)(2,1)}, bf16[128,1664]{1,0:T(8,128)(2,1)S(1)}, u32[]{:S(2)}, u32[]{:S(2)}) collective-permute-start(bf16[128,1664]{1,0:T(8,128)(2,1)} %collective-permute-done.4.refs_10_), channel_id=1, source_target_pairs={{0,8},{8,0},{1,9},{9,1},{2,10},{10,2},{3,11},{11,3},{4,12},{12,4},... | collective-permute-start | bytes 1277960 | tf_op jit(solution)/shard_map/ppermute | solution.py:23
  30.6 2.0 %collective-permute-start.8 = (bf16[1664,128]{1,0:T(8,128)(2,1)}, bf16[1664,128]{1,0:T(8,128)(2,1)S(1)}, u32[]{:S(2)}, u32[]{:S(2)}) collective-permute-start(bf16[1664,128]{1,0:T(8,128)(2,1)} %collective-permute-done.7.refs_14_), channel_id=1, source_target_pairs={{0,8},{8,0},{1,9},{9,1},{2,10},{10,2},{3,11},{11,3},{4,12},{12,4},... | collective-permute-start | bytes 1277960 | tf_op jit(solution)/shard_map/ppermute | solution.py:23
  32.6 1.0 copy-start.3
  56.1 13.8 %collective-permute-start.10 = (bf16[192,1152]{1,0:T(8,128)(2,1)}, bf16[192,1152]{1,0:T(8,128)(2,1)S(1)}, u32[]{:S(2)}, u32[]{:S(2)}) collective-permute-start(bf16[192,1152]{1,0:T(8,128)(2,1)} %get-tuple-element.10), channel_id=1, source_target_pairs={{0,48},{16,0},{32,16},{48,32},{1,49},{17,1},{33,17},{49,33},{2,50}... | collective-permute-start | bytes 1327112 | tf_op jit(solution)/shard_map/ppermute | solution.py:23
  56.1 13.7 %collective-permute-start.11 = (bf16[192,1152]{1,0:T(8,128)(2,1)}, bf16[192,1152]{1,0:T(8,128)(2,1)S(1)}, u32[]{:S(2)}, u32[]{:S(2)}) collective-permute-start(bf16[192,1152]{1,0:T(8,128)(2,1)} %get-tuple-element.11), channel_id=1, source_target_pairs={{0,16},{16,32},{32,48},{48,0},{1,17},{17,33},{33,49},{49,1},{2,18}... | collective-permute-start | bytes 1327112 | tf_op jit(solution)/shard_map/ppermute | solution.py:23
  59.3 20.7 %collective-permute-start.9 = (bf16[192,1152]{1,0:T(8,128)(2,1)}, bf16[192,1152]{1,0:T(8,128)(2,1)S(1)}, u32[]{:S(2)}, u32[]{:S(2)}) collective-permute-start(bf16[192,1152]{1,0:T(8,128)(2,1)} %get-tuple-element.9), channel_id=1, source_target_pairs={{0,32},{16,48},{32,0},{48,16},{1,33},{17,49},{33,1},{49,17},{2,34}... | collective-permute-start | bytes 1327112 | tf_op jit(solution)/shard_map/ppermute | solution.py:23
  81.6 0.7 copy-start.1
  86.4 36.2 %collective-permute-start.12 = (bf16[192,1024]{1,0:T(8,128)(2,1)}, bf16[192,1024]{1,0:T(8,128)(2,1)S(1)}, u32[]{:S(2)}, u32[]{:S(2)}) collective-permute-start(bf16[192,1024]{1,0:T(8,128)(2,1)} %project.8), channel_id=1, source_target_pairs={{0,5},{1,4},{2,7},{3,6},{4,1},{5,0},{6,3},{7,2},{8,13},{9,12},{10,... | collective-permute-start | bytes 1179656 | tf_op jit(solution)/shard_map/ppermute | solution.py:32
  96.1 29.5 %collective-permute-start.13 = (bf16[192,1024]{1,0:T(8,128)(2,1)}, bf16[192,1024]{1,0:T(8,128)(2,1)S(1)}, u32[]{:S(2)}, u32[]{:S(2)}) collective-permute-start(bf16[192,1024]{1,0:T(8,128)(2,1)} %project.9), channel_id=1, source_target_pairs={{0,3},{1,2},{2,5},{3,4},{4,7},{5,6},{6,1},{7,0},{8,11},{9,10},{10,... | collective-permute-start | bytes 1179656 | tf_op jit(solution)/shard_map/ppermute | solution.py:32
  101.9 29.8 %collective-permute-start.14 = (bf16[192,1024]{1,0:T(8,128)(2,1)}, bf16[192,1024]{1,0:T(8,128)(2,1)S(1)}, u32[]{:S(2)}, u32[]{:S(2)}) collective-permute-start(bf16[192,1024]{1,0:T(8,128)(2,1)} %project.10), channel_id=1, source_target_pairs={{0,7},{1,6},{2,1},{3,0},{4,3},{5,2},{6,5},{7,4},{8,15},{9,14},{10,... | collective-permute-start | bytes 1179656 | tf_op jit(solution)/shard_map/ppermute | solution.py:32
  109.9 21.8 %collective-permute-start.15 = (bf16[192,1024]{1,0:T(8,128)(2,1)}, bf16[192,1024]{1,0:T(8,128)(2,1)S(1)}, u32[]{:S(2)}, u32[]{:S(2)}) collective-permute-start(bf16[192,1024]{1,0:T(8,128)(2,1)} %project.11), channel_id=1, source_target_pairs={{0,4},{1,5},{2,6},{3,7},{4,0},{5,1},{6,2},{7,3},{8,12},{9,13},{10,... | collective-permute-start | bytes 1179656 | tf_op jit(solution)/shard_map/ppermute | solution.py:32
  114.0 18.0 %collective-permute-start.17 = (bf16[192,1024]{1,0:T(8,128)(2,1)}, bf16[192,1024]{1,0:T(8,128)(2,1)S(1)}, u32[]{:S(2)}, u32[]{:S(2)}) collective-permute-start(bf16[192,1024]{1,0:T(8,128)(2,1)} %project.13), channel_id=1, source_target_pairs={{0,2},{1,3},{2,4},{3,5},{4,6},{5,7},{6,0},{7,1},{8,10},{9,11},{10,... | collective-permute-start | bytes 1179656 | tf_op jit(solution)/shard_map/ppermute | solution.py:32
  118.5 20.1 %copy-start.4 = (bf16[192,1024]{1,0:T(8,128)(2,1)S(1)}, bf16[192,1024]{1,0:T(8,128)(2,1)}, u32[]{:S(2)}) copy-start(bf16[192,1024]{1,0:T(8,128)(2,1)} %param.11) | copy-start | bytes 1179652
  122.7 14.6 %collective-permute-start.18 = (bf16[192,1024]{1,0:T(8,128)(2,1)}, bf16[192,1024]{1,0:T(8,128)(2,1)S(1)}, u32[]{:S(2)}, u32[]{:S(2)}) collective-permute-start(bf16[192,1024]{1,0:T(8,128)(2,1)} %project.14), channel_id=1, source_target_pairs={{0,6},{1,7},{2,0},{3,1},{4,2},{5,3},{6,4},{7,5},{8,14},{9,15},{10,... | collective-permute-start | bytes 1179656 | tf_op jit(solution)/shard_map/ppermute | solution.py:32
  125.5 13.1 %collective-permute-start.16 = (bf16[192,1024]{1,0:T(8,128)(2,1)}, bf16[192,1024]{1,0:T(8,128)(2,1)S(1)}, u32[]{:S(2)}, u32[]{:S(2)}) collective-permute-start(bf16[192,1024]{1,0:T(8,128)(2,1)} %project.12), channel_id=1, source_target_pairs={{0,1},{1,0},{2,3},{3,2},{4,5},{5,4},{6,7},{7,6},{8,9},{9,8},{10,11... | collective-permute-start | bytes 1179656 | tf_op jit(solution)/shard_map/ppermute | solution.py:32
where the time goes:
time: 143 us; the launch traced here: 141 us
  Pallas kernels  56.8 us (40%)
  waiting for transfers between devices  40.4 us (28%)
  starting transfers between devices  28.8 us (20%)
  other arithmetic  6.73 us (5%)
  local copies, waits for them, and re-layouts  6.42 us (4%)
    ppermute x12, waiting for transfers between devices, shifted(): lax.ppermute(value, axis, [(s, (s + steps) % count) for s in range(count)])  33.4 us
    pallas_call x8, Pallas kernels, project(): pl.pallas_call(project_kernel, out_shape=jax.ShapeDtypeStruct((tokens, wi...  32.9 us
    pallas_call x1, Pallas kernels, attend(): pl.pallas_call(lambda *refs: attend_kernel(*refs, scale=1.0 / math.sqrt(h...  22.4 us
    ppermute x7, starting transfers between devices, head_shifted(): return lax.ppermute(value, HEAD, pairs)  15.8 us
    ppermute x12, starting transfers between devices, shifted(): lax.ppermute(value, axis, [(s, (s + steps) % count) for s in range(count)])  13 us
    ppermute x7, waiting for transfers between devices, head_shifted(): return lax.ppermute(value, HEAD, pairs)  7.01 us
    unnamed x11, local copies, waits for them, and re-layouts  3 us
  transfers between devices with their start and end apart: 19, of which 10 were waited for; matrix products, arithmetic and copies ran while one was open for 6% of the time, Pallas kernels for 20%

commit v1 on v0

v1 whole, which is shorter than its diff:
```python
import math

import jax
import jax.numpy as jnp
from jax import lax
from jax.experimental import pallas as pl
from jax.experimental.pallas import tpu as pltpu
from jax.sharding import Mesh
from jax.sharding import PartitionSpec as P

SEQ = ("y", "x", "core")
HEAD = ("z", "yh")
CHUNK = 32
HALVES = 2
LOWEST = -1e30
BLOCKED = 1e30
TURNS = (2, 1, 3, 0)
ROUTES = (((2, 1), (1, 1)), ((3, 1), (0, 1), (2, 0)), ((1, 0), (3, 0), (0, 0)))
BF16 = jnp.bfloat16
F32 = jnp.float32


def shifted(value, axis, steps):
    count = lax.axis_size(axis)
    return lax.ppermute(value, axis, [(s, (s + steps) % count) for s in range(count)])


def head_shifted(value, dz, dy):
    nz, ny = lax.axis_size("z"), lax.axis_size("yh")
    pairs = []
    for z in range(nz):
        for y in range(ny):
            pairs.append((z * ny + y, (z + dz) % nz * ny + (y + dy) % ny))
    return lax.ppermute(value, HEAD, pairs)


def attend_kernel(items, count, images, *refs, scale, hd, group, blocks, keys, padded, start):
    q_refs = refs[:blocks]
    key_refs = refs[blocks : blocks + 4]
    value_refs = refs[blocks + 4 : blocks + 8]
    out_refs = refs[blocks + 8 : 2 * blocks + 8]
    q_all, key_all, value_all, first_s, second_s, first_b, second_b, top_ref, acc_ref, sems = refs[
        2 * blocks + 8 :
    ]
    tokens = out_refs[0].shape[0]
    rows = CHUNK * group
    width = group * hd
    factor = scale * math.log2(math.e)
    copies = []
    for j in range(4):
        copies.append(pltpu.make_async_copy(key_refs[j], key_all.at[j], sems.at[2 * j]))
        copies.append(
            pltpu.make_async_copy(
                value_refs[j], value_all.at[j, :, pl.ds(0, hd)], sems.at[2 * j + 1]
            )
        )
    for i in range(blocks):
        copies.append(
            pltpu.make_async_copy(
                q_refs[i].at[pl.ds(start, tokens)], q_all.at[pl.ds(i * tokens, tokens)], sems.at[8 + i]
            )
        )
    for copy in copies:
        copy.start()
    place = lax.broadcasted_iota(jnp.int32, (padded, hd), 0)
    ones = jnp.where(place < keys, 1.0, 0.0).astype(BF16)
    for j in range(4):
        value_all[j, :, hd:] = ones
    top_ref[...] = jnp.full(top_ref.shape, LOWEST, F32)
    acc_ref[...] = jnp.zeros(acc_ref.shape, F32)
    for copy in copies:
        copy.wait()

    def where_is(i):
        item = items[i]
        return item // 8, item % 4, jnp.where(item % 8 < 4, images[item % 4], -1)

    def score(i, scores_ref, best_ref):
        chunk, j, _ = where_is(i)
        at = pl.ds(pl.multiple_of(chunk * CHUNK, CHUNK), CHUNK)
        q = jnp.concatenate([q_all[at, h * hd : (h + 1) * hd] for h in range(group)], axis=0)
        best = None
        for k in range(0, padded, 128):
            part = jnp.dot(q, key_all[j, :, k : k + 128], preferred_element_type=F32)
            scores_ref[:, k : k + 128] = part
            best = part if best is None else jnp.maximum(best, part)
        best_ref[...] = jnp.broadcast_to(jnp.max(best, axis=1, keepdims=True), best_ref.shape)

    def absorb(i, scores_ref, best_ref):
        chunk, j, image = where_is(i)
        at = pl.ds(pl.multiple_of(chunk * rows, rows), rows)
        near = pl.ds(pl.multiple_of(chunk * CHUNK, CHUNK), CHUNK)
        reach = q_all[near, width : width + hd].astype(F32)
        low = jnp.concatenate([reach[:, 0:1]] * group, axis=0)
        high = jnp.concatenate([reach[:, 1:2]] * group, axis=0)
        number = image.astype(F32)
        allowed = (low <= number) & (number < high)
        old = top_ref[at, 0:1]
        new = jnp.where(allowed, jnp.maximum(old, best_ref[:, 0:1]), old)
        anchor = jnp.where(allowed, new, BLOCKED)
        rescale = jnp.exp2((old - new) * factor)
        top_ref[at, :] = jnp.broadcast_to(new, (rows, hd))
        weights = jnp.exp2((scores_ref[...] - anchor) * factor).astype(BF16)
        mixed = jnp.dot(weights, value_all[j], preferred_element_type=F32)
        acc_ref[at, :] = acc_ref[at, :] * rescale + mixed

    def pair(k, carry):
        i = 2 * k
        score(i + 1, second_s, second_b)
        absorb(i, first_s, first_b)
        score(i + 2, first_s, first_b)
        absorb(i + 1, second_s, second_b)
        return carry

    score(0, first_s, first_b)
    lax.fori_loop(0, (count[0] + 1) // 2, pair, 0)

    lane = lax.broadcasted_iota(jnp.int32, (CHUNK, hd), 1)
    for c in range(blocks * tokens // CHUNK):
        out_ref = out_refs[c * CHUNK // tokens]
        near = pl.ds(c * CHUNK % tokens, CHUNK)
        totals = jnp.zeros((CHUNK, hd), F32)
        tops = jnp.zeros((CHUNK, hd), F32)
        for h in range(group):
            at = pl.ds(c * rows + h * CHUNK, CHUNK)
            total = acc_ref[at, hd:]
            safe = jnp.where(total > 0, total, 1.0)
            out_ref[near, h * hd : (h + 1) * hd] = (acc_ref[at, :hd] / safe).astype(BF16)
            totals = jnp.where(lane % group == h, total, totals)
            tops = jnp.where(lane % group == h, top_ref[at, :], tops)
        seen = totals > 0
        logsum = jnp.where(seen, tops * scale + jnp.log(jnp.where(seen, totals, 1.0)), LOWEST)
        hi = logsum.astype(BF16).astype(F32)
        mid = (logsum - hi).astype(BF16).astype(F32)
        lo = logsum - hi - mid
        pieces = jnp.where(lane < group, hi, jnp.where(lane < 2 * group, mid, lo))
        out_ref[near, width:] = pieces.astype(BF16)


def attend(payloads, items, count, images, keys_t, values, keys, tokens, start):
    blocks = len(payloads)
    wide = payloads[0].shape[1]
    hd, padded = keys_t[0].shape
    width = wide - hd
    group = width // hd
    rows = CHUNK * group
    apart = pl.BlockSpec(memory_space=pl.ANY)
    here = pl.BlockSpec(memory_space=pltpu.VMEM)
    return pl.pallas_call(
        lambda *refs: attend_kernel(
            *refs,
            scale=1.0 / math.sqrt(hd),
            hd=hd,
            group=group,
            blocks=blocks,
            keys=keys,
            padded=padded,
            start=start,
        ),
        out_shape=[jax.ShapeDtypeStruct((tokens, wide), BF16)] * blocks,
        grid_spec=pltpu.PrefetchScalarGridSpec(
            num_scalar_prefetch=3,
            grid=(),
            in_specs=[apart] * (blocks + 8),
            out_specs=[here] * blocks,
            scratch_shapes=[
                pltpu.VMEM((blocks * tokens, wide), BF16),
                pltpu.VMEM((4, hd, padded), BF16),
                pltpu.VMEM((4, padded, 2 * hd), BF16),
                pltpu.VMEM((rows, padded), F32),
                pltpu.VMEM((rows, padded), F32),
                pltpu.VMEM((rows, hd), F32),
                pltpu.VMEM((rows, hd), F32),
                pltpu.VMEM((blocks * tokens * group, hd), F32),
                pltpu.VMEM((blocks * tokens * group, 2 * hd), F32),
                pltpu.SemaphoreType.DMA((8 + blocks,)),
            ],
        ),
        compiler_params=pltpu.CompilerParams(vmem_limit_bytes=48 << 20),
        cost_estimate=pl.CostEstimate(
            flops=2 * blocks * tokens * group * padded * 2 * hd,
            bytes_accessed=blocks * tokens * width * 4 + padded * hd * 16,
            transcendentals=blocks * tokens * group * padded * 2,
        ),
        name="attend",
    )(items, count, images, *payloads, *keys_t, *values)


def work_list(hits):
    tokens, tiles = hits.shape
    flags = jnp.any(hits.reshape(tokens // CHUNK, CHUNK, tiles), axis=1).reshape(-1)
    size = flags.shape[0]
    place = jnp.arange(size, dtype=jnp.int32)
    rank = jnp.sum((place[None, :] < place[:, None]) & flags[None, :], axis=1)
    count = jnp.sum(flags.astype(jnp.int32))
    code = place // tiles * 8 + place % tiles + 1
    slot = jnp.arange(size + 3, dtype=jnp.int32)
    chosen = (rank[None, :] == slot[:, None]) & flags[None, :]
    items = jnp.sum(jnp.where(chosen, code[None, :], 0), axis=1)
    items = jnp.where(items > 0, items - 1, 4)
    return items.astype(jnp.int32), count.reshape(1)


def combined(parts, out_ref, hd, group):
    width = group * hd
    sums = []
    for ref in parts:
        pieces = ref[:, width:].astype(F32)
        sums.append(pieces[:, :group] + pieces[:, group : 2 * group] + pieces[:, 2 * group : 3 * group])
    top = jnp.maximum(jnp.maximum(sums[0], sums[1]), jnp.maximum(sums[2], sums[3]))
    shares = [jnp.exp(s - top) for s in sums]
    total = shares[0] + shares[1] + shares[2] + shares[3]
    shares = [s / total for s in shares]
    for h in range(group):
        at = slice(h * hd, (h + 1) * hd)
        mixed = parts[0][:, at].astype(F32) * shares[0][:, h : h + 1]
        for ref, share in zip(parts[1:], shares[1:]):
            mixed = mixed + ref[:, at].astype(F32) * share[:, h : h + 1]
        out_ref[:, at] = mixed.astype(BF16)


def project_kernel(columns, *refs, hd, group, wanted, merge):
    sources = refs[: 4 if merge else 1]
    w_ref = refs[len(sources)]
    outs = refs[len(sources) + 1 : len(sources) + 1 + wanted]
    held, sems = refs[-2:]
    depth, width = held.shape[1:]
    cuts = 2
    piece = depth // cuts
    copies = []
    for i in range(wanted):
        for c in range(cuts):
            at = pl.ds(c * piece, piece)
            copy = pltpu.make_async_copy(
                w_ref.at[at, pl.ds(pl.multiple_of(columns[i] * width, width), width)],
                held.at[i, at],
                sems.at[i * cuts + c],
            )
            copy.start()
            copies.append(copy)
    if merge:
        attended = refs[len(sources) + 1 + wanted]
        combined(sources, attended, hd, group)
    else:
        attended = sources[0]
    for i in range(wanted):
        for c in range(cuts):
            copies[i * cuts + c].wait()
        outs[i][...] = jnp.dot(attended[...], held[i], preferred_element_type=F32).astype(BF16)


def project(sources, weight, columns, width, hd):
    merge = len(sources) > 1
    tokens = sources[0].shape[0]
    depth = weight.shape[0]
    wanted = columns.shape[0]
    here = pl.BlockSpec(memory_space=pltpu.VMEM)
    results = [jax.ShapeDtypeStruct((tokens, width), BF16)] * wanted
    if merge:
        results.append(jax.ShapeDtypeStruct((tokens, depth), BF16))
    return pl.pallas_call(
        lambda *refs: project_kernel(*refs, hd=hd, group=depth // hd, wanted=wanted, merge=merge),
        out_shape=results,
        grid_spec=pltpu.PrefetchScalarGridSpec(
            num_scalar_prefetch=1,
            grid=(),
            in_specs=[here] * len(sources) + [pl.BlockSpec(memory_space=pl.ANY)],
            out_specs=[here] * len(results),
            scratch_shapes=[
                pltpu.VMEM((wanted, depth, width), BF16),
                pltpu.SemaphoreType.DMA((2 * wanted,)),
            ],
        ),
        cost_estimate=pl.CostEstimate(
            flops=2 * tokens * depth * width * wanted,
            bytes_accessed=2 * wanted * (depth * width + tokens * (depth + width)),
            transcendentals=0,
        ),
        compiler_params=pltpu.CompilerParams(vmem_limit_bytes=52 << 20),
        name="project",
    )(columns, *sources, weight)


def settle_kernel(gate_ref, order_ref, layer_ref, *refs):
    terms, out_ref = refs[:-1], refs[-1]
    each = len(terms) // HALVES
    tokens = order_ref.shape[0] // HALVES
    total = None
    for half in range(HALVES):
        order = order_ref[half * tokens : (half + 1) * tokens]
        for ref in terms[half * each : (half + 1) * each]:
            part = lax.dot_general(
                order, ref[...], (((0,), (0,)), ((), ())), preferred_element_type=F32
            )
            total = part if total is None else total + part
    out_ref[...] = (layer_ref[...].astype(F32) + gate_ref[0] * total).astype(BF16)


def settle(gate, order, layer, terms):
    tokens, width = layer.shape
    cuts = 4
    step = width // cuts
    tall = pl.BlockSpec((tokens, step), lambda g: (0, g))
    part = pl.BlockSpec((tokens // HALVES, step), lambda g: (0, g))
    return pl.pallas_call(
        settle_kernel,
        out_shape=jax.ShapeDtypeStruct((tokens, width), BF16),
        grid=(cuts,),
        in_specs=[
            pl.BlockSpec(memory_space=pltpu.SMEM),
            pl.BlockSpec((tokens, tokens), lambda g: (0, 0)),
            tall,
        ]
        + [part] * len(terms),
        out_specs=tall,
        compiler_params=pltpu.CompilerParams(vmem_limit_bytes=32 << 20),
        name="settle",
    )(gate, order, layer, *terms)


def shards(
    queries, image_keys, image_values, layer_input, out_weight, tile_counts, image_range, attn_gate
):
    tokens, width = queries.shape
    keys, hd = image_keys.shape
    y, x, core = (lax.axis_index(n) for n in SEQ)
    z, yh = (lax.axis_index(n) for n in HEAD)
    ny, nx, nc = (lax.axis_size(n) for n in SEQ)
    nz, nyh = (lax.axis_size(n) for n in HEAD)

    padded = -(-keys // 128) * 128
    spare = jnp.broadcast_to(image_keys[:1], (padded - keys, hd))
    key_t = jnp.concatenate([image_keys, spare], axis=0).T
    own = (key_t, jnp.pad(image_values, ((0, padded - keys), (0, 0))))
    across = [shifted(v, "y", 1) for v in own]
    beside = [shifted(v, "core", 1) for v in own]
    diagonal = [shifted(v, "core", 1) for v in across]
    tiles = (own, beside, across, diagonal)

    bounds, _ = lax.optimization_barrier((image_range, key_t))
    low, high = bounds[0], bounds[1]
    grade = jnp.where(low < high, low * 16 + high, 1 << 10)
    place = jnp.arange(tokens, dtype=jnp.int32)
    ahead = (grade[None, :] < grade[:, None]) | (
        (grade[None, :] == grade[:, None]) & (place[None, :] < place[:, None])
    )
    rank = jnp.sum(ahead.astype(jnp.int32), axis=1)
    order = (rank[None, :] == place[:, None]).astype(BF16)
    extra = jnp.pad(bounds.astype(BF16).T, ((0, 0), (0, hd - 2)))
    payload = jnp.dot(
        order, jnp.concatenate([queries, extra], axis=1), preferred_element_type=F32
    ).astype(BF16)
    payloads = [payload if s == 0 else shifted(payload, "x", s) for s in TURNS]

    def number(yy, cc):
        return (yy % ny * nx + x) * nc + cc % nc

    held = jnp.stack([number(y, core), number(y, core + 1), number(y + 1, core), number(y + 1, core + 1)])
    image = jnp.arange(tile_counts.shape[0])
    ends = jnp.sum(jnp.where(image[None, :] <= image[:, None], tile_counts[None, :], 0), axis=1)
    images = jnp.sum((ends[None, :] <= held[:, None]).astype(jnp.int32), axis=1)

    share = tokens // HALVES
    columns = [
        jnp.stack([(z + dz) % nz * nyh + (yh + dy) % nyh for dz, dy in some]).astype(jnp.int32)
        for some in ROUTES
    ]
    terms = []
    for half in range(HALVES):
        start = half * share
        reach = jnp.concatenate(
            [p[start : start + share, width : width + 2] for p in payloads], axis=0
        ).astype(jnp.int32)
        hits = (reach[:, :1] <= images[None, :]) & (images[None, :] < reach[:, 1:])
        items, count = work_list(hits)
        parts = attend(
            payloads, items, count, images, [t[0] for t in tiles], [t[1] for t in tiles], keys, share, start
        )
        parts = [p if s == 0 else shifted(p, "x", nx - s) for s, p in zip(TURNS, parts)]
        sources = parts
        for some, column in zip(ROUTES, columns):
            got = project(sources, out_weight, column, width, hd)
            if len(sources) > 1:
                sources = [got[-1]]
            for (dz, dy), term in zip(some, got):
                terms.append(term if (dz, dy) == (0, 0) else head_shifted(term, dz, dy))
    return settle(jnp.tanh(attn_gate), order, layer_input, terms)


def solution(mesh):
    split = Mesh(mesh.devices.reshape(2, 4, 2, 4, 2), ("y", "x", "core", "z", "yh"))
    return jax.shard_map(
        shards,
        mesh=split,
        in_specs=(
            P(SEQ, HEAD),
            P(SEQ, HEAD),
            P(SEQ, HEAD),
            P(SEQ, HEAD),
            P(HEAD, None),
            P(),
            P(None, SEQ),
            P(),
        ),
        out_specs=P(SEQ, HEAD),
        check_vma=False,
    )
```

time: 143 us -> 150 us (1.049); the launches traced: 141 us -> 151 us
  starting transfers between devices: 28.8 us -> 81.3 us
  Pallas kernels: 56.8 us -> 35.4 us
  waiting for transfers between devices: 40.4 us -> 21 us
  local copies, waits for them, and re-layouts: 6.42 us -> 4.88 us
    ppermute x12 -> x15, starting transfers between devices: 13 us -> 51 us  [shifted(): lax.ppermute(value, axis, [(s, (s + steps) % count) for s in range(count)])]
    ppermute x12 -> x15, waiting for transfers between devices: 33.4 us -> 15.3 us  [shifted(): lax.ppermute(value, axis, [(s, (s + steps) % count) for s in range(count)])]
    ppermute x7 -> x14, starting transfers between devices: 15.8 us -> 30.3 us  [head_shifted(): return lax.ppermute(value, HEAD, pairs)]
    pallas_call x1 -> x2, Pallas kernels: 22.4 us -> 9.57 us  [attend(): pl.pallas_call(lambda *refs: attend_kernel(*refs, scale=1.0 / math.sqrt(h...]
    pallas_call x9 -> x7, Pallas kernels: 34.4 us -> 25.9 us  [the longest x6 22.1 us: project(): pl.pallas_call(lambda *refs: project_kernel(*refs, hd=hd, group=depth //...]
    convert_element_type x1 -> x2, other arithmetic: 2.45 us -> 0.74 us  [shards(): reach = jnp.concatenate([p[start:start + share, width:width + 2] for p in...]
    unnamed x11 -> x4, local copies, waits for them, and re-layouts: 3 us -> 1.39 us
    ppermute x7 -> x14, waiting for transfers between devices: 7.01 us -> 5.74 us  [head_shifted(): return lax.ppermute(value, HEAD, pairs)]
  transfers between devices with their start and end apart: 19 -> 29, of which waited for: 10 -> 6; matrix products, arithmetic and copies ran while one was open for 6% -> 7% of each run, Pallas kernels for 20% -> 18%
where the time goes in v1:
time: 150 us; the launch traced here: 151 us
  starting transfers between devices  81.3 us (54%)
  Pallas kernels  35.4 us (24%)
  waiting for transfers between devices  21 us (14%)
  other arithmetic  6.58 us (4%)
  local copies, waits for them, and re-layouts  4.88 us (3%)
    ppermute x15, starting transfers between devices, shifted(): lax.ppermute(value, axis, [(s, (s + steps) % count) for s in range(count)])  51 us
    ppermute x14, starting transfers between devices, head_shifted(): return lax.ppermute(value, HEAD, pairs)  30.3 us
    pallas_call x6, Pallas kernels, project(): pl.pallas_call(lambda *refs: project_kernel(*refs, hd=hd, group=depth //...  22.1 us
    ppermute x15, waiting for transfers between devices, shifted(): lax.ppermute(value, axis, [(s, (s + steps) % count) for s in range(count)])  15.3 us
    pallas_call x2, Pallas kernels, attend(): pl.pallas_call(lambda *refs: attend_kernel(*refs, scale=1.0 / math.sqrt(h...  9.57 us
    ppermute x14, waiting for transfers between devices, head_shifted(): return lax.ppermute(value, HEAD, pairs)  5.74 us
    pallas_call x1, Pallas kernels, settle(): pl.pallas_call(settle_kernel, out_shape=jax.ShapeDtypeStruct((tokens, wid...  3.77 us
  transfers between devices with their start and end apart: 29, of which 6 were waited for; matrix products, arithmetic and copies ran while one was open for 7% of the time, Pallas kernels for 18%

profile of v1, /device:TPU:8, one launch (start us, length us, event | category | flops | bytes accessed | tf_op | source)
XLA Modules:
  0.0 151.4 jit_solution(17408623180096812735)
XLA Ops:
  5.7 2.9 %collective-permute-start.2 = (bf16[192,1152]{1,0:T(8,128)(2,1)S(1)}, bf16[192,1152]{1,0:T(8,128)(2,1)S(1)}, u32[]{:S(2)}, u32[]{:S(2)}) collective-permute-start(bf16[192,1152]{1,0:T(8,128)(2,1)S(1)} %convolution_convert_fusion.refs_6_), channel_id=1, source_target_pairs={{0,48},{16,0},{32,16},{48,32},{1,49},{17,1},{33,17},{49,33},{2,50}... | collective-permute-start | bytes 1327112 | tf_op jit(solution)/shard_map/ppermute | solution.py:25
  13.1 5.6 %collective-permute-done.2.refs_5_ = bf16[192,1152]{1,0:T(8,128)(2,1)S(1)} collective-permute-done((bf16[192,1152]{1,0:T(8,128)(2,1)S(1)}, bf16[192,1152]{1,0:T(8,128)(2,1)S(1)}, u32[]{:S(2)}, u32[]{:S(2)}) %collective-permute-start.2) | collective-permute-done | bytes 442400 | tf_op jit(solution)/shard_map/ppermute | solution.py:25
  18.7 2.7 %collective-permute-start = (bf16[192,1152]{1,0:T(8,128)(2,1)S(1)}, bf16[192,1152]{1,0:T(8,128)(2,1)S(1)}, u32[]{:S(2)}, u32[]{:S(2)}) collective-permute-start(bf16[192,1152]{1,0:T(8,128)(2,1)S(1)} %convolution_convert_fusion.refs_6_), channel_id=1, source_target_pairs={{0,32},{16,48},{32,0},{48,16},{1,33},{17,49},{33,1},{49,17},{2,34}... | collective-permute-start | bytes 1327112 | tf_op jit(solution)/shard_map/ppermute | solution.py:25
  23.7 8.3 %collective-permute-done.refs_3_ = bf16[192,1152]{1,0:T(8,128)(2,1)S(1)} collective-permute-done((bf16[192,1152]{1,0:T(8,128)(2,1)S(1)}, bf16[192,1152]{1,0:T(8,128)(2,1)S(1)}, u32[]{:S(2)}, u32[]{:S(2)}) %collective-permute-start) | collective-permute-done | bytes 442400 | tf_op jit(solution)/shard_map/ppermute | solution.py:25
  36.2 4.8 %attend.3 = (bf16[96,1152]{1,0:T(8,128)(2,1)S(1)}, bf16[96,1152]{1,0:T(8,128)(2,1)S(1)}, bf16[96,1152]{1,0:T(8,128)(2,1)S(1)}, bf16[96,1152]{1,0:T(8,128)(2,1)S(1)}) custom-call(s32[51]{0:T(128)S(1)} %get-tuple-element.80.refs_0_, s32[1]{0:T(128)} %bitcast.19.refs_1_, s32[4]{0:T(128)S(1)} %convert_reduce_fusion.5.refs_2_, ...), custom_call_target="tpu_custom_call" | custom-call | flops 2617245696 | bytes 4980736 | tf_op jit(solution)/shard_map/attend/pallas_call | solution.py:149
  41.0 11.4 %collective-permute-start.19 = (bf16[96,1152]{1,0:T(8,128)(2,1)S(1)}, bf16[96,1152]{1,0:T(8,128)(2,1)S(1)}, u32[]{:S(2)}, u32[]{:S(2)}) collective-permute-start(bf16[96,1152]{1,0:T(8,128)(2,1)S(1)} %get-tuple-element.46), channel_id=1, source_target_pairs={{0,32},{16,48},{32,0},{48,16},{1,33},{17,49},{33,1},{49,17},{2,34}... | collective-permute-start | bytes 663560 | tf_op jit(solution)/shard_map/ppermute | solution.py:25
  52.4 9.4 %collective-permute-start.20 = (bf16[96,1152]{1,0:T(8,128)(2,1)S(1)}, bf16[96,1152]{1,0:T(8,128)(2,1)S(1)}, u32[]{:S(2)}, u32[]{:S(2)}) collective-permute-start(bf16[96,1152]{1,0:T(8,128)(2,1)S(1)} %get-tuple-element.47), channel_id=1, source_target_pairs={{0,48},{16,0},{32,16},{48,32},{1,49},{17,1},{33,17},{49,33},{2,50}... | collective-permute-start | bytes 663560 | tf_op jit(solution)/shard_map/ppermute | solution.py:25
  62.6 4.7 %attend.2 = (bf16[96,1152]{1,0:T(8,128)(2,1)S(1)}, bf16[96,1152]{1,0:T(8,128)(2,1)S(1)}, bf16[96,1152]{1,0:T(8,128)(2,1)S(1)}, bf16[96,1152]{1,0:T(8,128)(2,1)S(1)}) custom-call(s32[51]{0:T(128)S(1)} %get-tuple-element.81.refs_0_, s32[1]{0:T(128)} %bitcast.12.refs_1_, s32[4]{0:T(128)S(1)} %convert_reduce_fusion.5.refs_2_, ...), custom_call_target="tpu_custom_call" | custom-call | flops 2617245696 | bytes 4980736 | tf_op jit(solution)/shard_map/attend/pallas_call | solution.py:149
  67.4 19.1 %collective-permute-start.9 = (bf16[96,1152]{1,0:T(8,128)(2,1)S(1)}, bf16[96,1152]{1,0:T(8,128)(2,1)S(1)}, u32[]{:S(2)}, u32[]{:S(2)}) collective-permute-start(bf16[96,1152]{1,0:T(8,128)(2,1)S(1)} %get-tuple-element.33), channel_id=1, source_target_pairs={{0,32},{16,48},{32,0},{48,16},{1,33},{17,49},{33,1},{49,17},{2,34}... | collective-permute-start | bytes 663560 | tf_op jit(solution)/shard_map/ppermute | solution.py:25
  88.6 3.2 %project.9 = (bf16[96,1024]{1,0:T(8,128)(2,1)S(1)}, bf16[96,1024]{1,0:T(8,128)(2,1)S(1)}, bf16[96,1024]{1,0:T(8,128)(2,1)S(1)}) custom-call(s32[2]{0:T(128)S(1)} %pad_add_fusion.refs_0_, bf16[96,1152]{1,0:T(8,128)(2,1)S(1)} %collective-permute-done.19.refs_1_, bf16[96,1152]{1,0:T(8,128)(2,1)S(1)} %collective-permute-done.20.refs_2_, ...), custom_call_target="tpu_custom_call" | custom-call | flops 402653184 | bytes 4980736 | tf_op jit(solution)/shard_map/project/pallas_call | solution.py:261
  91.9 5.9 %collective-permute-start.22 = (bf16[96,1024]{1,0:T(8,128)(2,1)S(1)}, bf16[96,1024]{1,0:T(8,128)(2,1)S(1)}, u32[]{:S(2)}, u32[]{:S(2)}) collective-permute-start(bf16[96,1024]{1,0:T(8,128)(2,1)S(1)} %get-tuple-element.50), channel_id=1, source_target_pairs={{0,5},{1,4},{2,7},{3,6},{4,1},{5,0},{6,3},{7,2},{8,13},{9,12},{10,... | collective-permute-start | bytes 589832 | tf_op jit(solution)/shard_map/ppermute | solution.py:34
  99.2 3.3 %project.6 = (bf16[96,1024]{1,0:T(8,128)(2,1)S(1)}, bf16[96,1024]{1,0:T(8,128)(2,1)S(1)}, bf16[96,1024]{1,0:T(8,128)(2,1)S(1)}) custom-call(s32[2]{0:T(128)S(1)} %pad_add_fusion.refs_0_, bf16[96,1152]{1,0:T(8,128)(2,1)S(1)} %collective-permute-done.9.refs_1_, bf16[96,1152]{1,0:T(8,128)(2,1)S(1)} %collective-permute-done.10.refs_2_, ...), custom_call_target="tpu_custom_call" | custom-call | flops 402653184 | bytes 4980736 | tf_op jit(solution)/shard_map/project/pallas_call | solution.py:261
  102.5 3.2 %collective-permute-start.12 = (bf16[96,1024]{1,0:T(8,128)(2,1)S(1)}, bf16[96,1024]{1,0:T(8,128)(2,1)S(1)}, u32[]{:S(2)}, u32[]{:S(2)}) collective-permute-start(bf16[96,1024]{1,0:T(8,128)(2,1)S(1)} %get-tuple-element.37), channel_id=1, source_target_pairs={{0,5},{1,4},{2,7},{3,6},{4,1},{5,0},{6,3},{7,2},{8,13},{9,12},{10,... | collective-permute-start | bytes 589832 | tf_op jit(solution)/shard_map/ppermute | solution.py:34
  105.7 2.3 %collective-permute-start.13 = (bf16[96,1024]{1,0:T(8,128)(2,1)S(1)}, bf16[96,1024]{1,0:T(8,128)(2,1)S(1)}, u32[]{:S(2)}, u32[]{:S(2)}) collective-permute-start(bf16[96,1024]{1,0:T(8,128)(2,1)S(1)} %get-tuple-element.38), channel_id=1, source_target_pairs={{0,3},{1,2},{2,5},{3,4},{4,7},{5,6},{6,1},{7,0},{8,11},{9,10},{10,... | collective-permute-start | bytes 589832 | tf_op jit(solution)/shard_map/ppermute | solution.py:34
  108.1 3.9 %project.8 = (bf16[96,1024]{1,0:T(8,128)(2,1)S(1)}, bf16[96,1024]{1,0:T(8,128)(2,1)S(1)}, bf16[96,1024]{1,0:T(8,128)(2,1)S(1)}) custom-call(s32[3]{0:T(128)S(1)} %pad_add_fusion.3.refs_0_, bf16[96,1024]{1,0:T(8,128)(2,1)S(1)} %get-tuple-element.39.refs_1_, bf16[1024,8192]{1,0:T(8,128)(2,1)} %refs_2_.7), custom_call_target="tpu_custom_call" | custom-call | flops 603979776 | bytes 7471104 | tf_op jit(solution)/shard_map/project/pallas_call | solution.py:261
  112.5 3.9 %project.7 = (bf16[96,1024]{1,0:T(8,128)(2,1)S(1)}, bf16[96,1024]{1,0:T(8,128)(2,1)S(1)}, bf16[96,1024]{1,0:T(8,128)(2,1)S(1)}) custom-call(s32[3]{0:T(128)S(1)} %pad_add_fusion.2.refs_0_, bf16[96,1024]{1,0:T(8,128)(2,1)S(1)} %get-tuple-element.39.refs_1_, bf16[1024,8192]{1,0:T(8,128)(2,1)} %refs_2_.7), custom_call_target="tpu_custom_call" | custom-call | flops 603979776 | bytes 7471104 | tf_op jit(solution)/shard_map/project/pallas_call | solution.py:261
  116.4 2.9 %collective-permute-start.18 = (bf16[96,1024]{1,0:T(8,128)(2,1)S(1)}, bf16[96,1024]{1,0:T(8,128)(2,1)S(1)}, u32[]{:S(2)}, u32[]{:S(2)}) collective-permute-start(bf16[96,1024]{1,0:T(8,128)(2,1)S(1)} %get-tuple-element.44), channel_id=1, source_target_pairs={{0,6},{1,7},{2,0},{3,1},{4,2},{5,3},{6,4},{7,5},{8,14},{9,15},{10,... | collective-permute-start | bytes 589832 | tf_op jit(solution)/shard_map/ppermute | solution.py:34
  119.3 2.1 %collective-permute-start.14 = (bf16[96,1024]{1,0:T(8,128)(2,1)S(1)}, bf16[96,1024]{1,0:T(8,128)(2,1)S(1)}, u32[]{:S(2)}, u32[]{:S(2)}) collective-permute-start(bf16[96,1024]{1,0:T(8,128)(2,1)S(1)} %get-tuple-element.40), channel_id=1, source_target_pairs={{0,7},{1,6},{2,1},{3,0},{4,3},{5,2},{6,5},{7,4},{8,15},{9,14},{10,... | collective-permute-start | bytes 589832 | tf_op jit(solution)/shard_map/ppermute | solution.py:34
  124.3 3.9 %project.10 = (bf16[96,1024]{1,0:T(8,128)(2,1)S(1)}, bf16[96,1024]{1,0:T(8,128)(2,1)S(1)}, bf16[96,1024]{1,0:T(8,128)(2,1)S(1)}) custom-call(s32[3]{0:T(128)S(1)} %pad_add_fusion.2.refs_0_, bf16[96,1024]{1,0:T(8,128)(2,1)S(1)} %get-tuple-element.52.refs_1_, bf16[1024,8192]{1,0:T(8,128)(2,1)} %refs_2_.7), custom_call_target="tpu_custom_call" | custom-call | flops 603979776 | bytes 7471104 | tf_op jit(solution)/shard_map/project/pallas_call | solution.py:261
  128.2 3.9 %project.11 = (bf16[96,1024]{1,0:T(8,128)(2,1)S(1)}, bf16[96,1024]{1,0:T(8,128)(2,1)S(1)}, bf16[96,1024]{1,0:T(8,128)(2,1)S(1)}) custom-call(s32[3]{0:T(128)S(1)} %pad_add_fusion.3.refs_0_, bf16[96,1024]{1,0:T(8,128)(2,1)S(1)} %get-tuple-element.52.refs_1_, bf16[1024,8192]{1,0:T(8,128)(2,1)} %refs_2_.7), custom_call_target="tpu_custom_call" | custom-call | flops 603979776 | bytes 7471104 | tf_op jit(solution)/shard_map/project/pallas_call | solution.py:261
  132.1 5.5 %collective-permute-start.24 = (bf16[96,1024]{1,0:T(8,128)(2,1)S(1)}, bf16[96,1024]{1,0:T(8,128)(2,1)S(1)}, u32[]{:S(2)}, u32[]{:S(2)}) collective-permute-start(bf16[96,1024]{1,0:T(8,128)(2,1)S(1)} %get-tuple-element.53), channel_id=1, source_target_pairs={{0,7},{1,6},{2,1},{3,0},{4,3},{5,2},{6,5},{7,4},{8,15},{9,14},{10,... | collective-permute-start | bytes 589832 | tf_op jit(solution)/shard_map/ppermute | solution.py:34
  139.1 2.8 %collective-permute-start.28 = (bf16[96,1024]{1,0:T(8,128)(2,1)S(1)}, bf16[96,1024]{1,0:T(8,128)(2,1)S(1)}, u32[]{:S(2)}, u32[]{:S(2)}) collective-permute-start(bf16[96,1024]{1,0:T(8,128)(2,1)S(1)} %get-tuple-element.57), channel_id=1, source_target_pairs={{0,6},{1,7},{2,0},{3,1},{4,2},{5,3},{6,4},{7,5},{8,14},{9,15},{10,... | collective-permute-start | bytes 589832 | tf_op jit(solution)/shard_map/ppermute | solution.py:34
  141.9 2.8 %collective-permute-done.25.refs_11_ = bf16[96,1024]{1,0:T(8,128)(2,1)S(1)} collective-permute-done((bf16[96,1024]{1,0:T(8,128)(2,1)S(1)}, bf16[96,1024]{1,0:T(8,128)(2,1)S(1)}, u32[]{:S(2)}, u32[]{:S(2)}) %collective-permute-start.25) | collective-permute-done | bytes 196640 | tf_op jit(solution)/shard_map/ppermute | solution.py:34
  147.7 3.8 %settle.1 = bf16[192,1024]{1,0:T(8,128)(2,1)} custom-call(f32[1]{0:T(128)S(6)} %tanh.3.gate_ref, bf16[192,192]{1,0:T(8,128)(2,1)S(1)} %fusion.7.order_ref, bf16[192,1024]{1,0:T(8,128)(2,1)S(1)} %copy-done, bf16[96,1024]{1,0:T(8,128)(2,1)S(1)} %collective-permute-done.12.refs_0_, bf16[96,1024]{1,0:T(8,128)(2,1)S(1)} %collective-permute-done.13.refs_1_, ...), custom_call_target="tpu_custom_call" | custom-call | tf_op jit(solution)/shard_map/settle/pallas_call | solution.py:305
  (92 shorter events, 28.0 us)
Async XLA Ops:
  2.1 19.5 %collective-permute-start.4 = (bf16[128,1664]{1,0:T(8,128)(2,1)S(1)}, bf16[128,1664]{1,0:T(8,128)(2,1)S(1)}, u32[]{:S(2)}, u32[]{:S(2)}) collective-permute-start(bf16[128,1664]{1,0:T(8,128)(2,1)S(1)} %maximum_bitcast_fusion.refs_7_), channel_id=1, source_target_pairs={{0,64},{64,0},{1,65},{65,1},{2,66},{66,2},{3,67},{67,3},{4,68},{68... | collective-permute-start | bytes 1277960 | tf_op jit(solution)/shard_map/ppermute | solution.py:25
  2.6 33.6 %collective-permute-start.3 = (bf16[128,1664]{1,0:T(8,128)(2,1)S(1)}, bf16[128,1664]{1,0:T(8,128)(2,1)S(1)}, u32[]{:S(2)}, u32[]{:S(2)}) collective-permute-start(bf16[128,1664]{1,0:T(8,128)(2,1)S(1)} %maximum_bitcast_fusion.refs_7_), channel_id=1, source_target_pairs={{0,8},{8,0},{1,9},{9,1},{2,10},{10,2},{3,11},{11,3},{4,12},{12,4},... | collective-permute-start | bytes 1277960 | tf_op jit(solution)/shard_map/ppermute | solution.py:25
  5.7 13.0 %collective-permute-start.2 = (bf16[192,1152]{1,0:T(8,128)(2,1)S(1)}, bf16[192,1152]{1,0:T(8,128)(2,1)S(1)}, u32[]{:S(2)}, u32[]{:S(2)}) collective-permute-start(bf16[192,1152]{1,0:T(8,128)(2,1)S(1)} %convolution_convert_fusion.refs_6_), channel_id=1, source_target_pairs={{0,48},{16,0},{32,16},{48,32},{1,49},{17,1},{33,17},{49,33},{2,50}... | collective-permute-start | bytes 1327112 | tf_op jit(solution)/shard_map/ppermute | solution.py:25
  8.6 14.4 %collective-permute-start.1 = (bf16[192,1152]{1,0:T(8,128)(2,1)S(1)}, bf16[192,1152]{1,0:T(8,128)(2,1)S(1)}, u32[]{:S(2)}, u32[]{:S(2)}) collective-permute-start(bf16[192,1152]{1,0:T(8,128)(2,1)S(1)} %convolution_convert_fusion.refs_6_), channel_id=1, source_target_pairs={{0,16},{16,32},{32,48},{48,0},{1,17},{17,33},{33,49},{49,1},{2,18}... | collective-permute-start | bytes 1327112 | tf_op jit(solution)/shard_map/ppermute | solution.py:25
  9.6 13.4 %collective-permute-start.7 = (bf16[1664,128]{1,0:T(8,128)(2,1)S(1)}, bf16[1664,128]{1,0:T(8,128)(2,1)}, u32[]{:S(2)}, u32[]{:S(2)}) collective-permute-start(bf16[1664,128]{1,0:T(8,128)(2,1)S(1)} %pad.9.refs_11_), channel_id=1, source_target_pairs={{0,64},{64,0},{1,65},{65,1},{2,66},{66,2},{3,67},{67,3},{4,68},{68... | collective-permute-start | bytes 1277960 | tf_op jit(solution)/shard_map/ppermute | solution.py:25
  18.7 13.3 %collective-permute-start = (bf16[192,1152]{1,0:T(8,128)(2,1)S(1)}, bf16[192,1152]{1,0:T(8,128)(2,1)S(1)}, u32[]{:S(2)}, u32[]{:S(2)}) collective-permute-start(bf16[192,1152]{1,0:T(8,128)(2,1)S(1)} %convolution_convert_fusion.refs_6_), channel_id=1, source_target_pairs={{0,32},{16,48},{32,0},{48,16},{1,33},{17,49},{33,1},{49,17},{2,34}... | collective-permute-start | bytes 1327112 | tf_op jit(solution)/shard_map/ppermute | solution.py:25
  21.6 14.6 %collective-permute-start.6 = (bf16[1664,128]{1,0:T(8,128)(2,1)S(1)}, bf16[1664,128]{1,0:T(8,128)(2,1)}, u32[]{:S(2)}, u32[]{:S(2)}) collective-permute-start(bf16[1664,128]{1,0:T(8,128)(2,1)S(1)} %pad.9.refs_11_), channel_id=1, source_target_pairs={{0,8},{8,0},{1,9},{9,1},{2,10},{10,2},{3,11},{11,3},{4,12},{12,4},... | collective-permute-start | bytes 1277960 | tf_op jit(solution)/shard_map/ppermute | solution.py:25
  23.0 13.2 %collective-permute-start.5 = (bf16[128,1664]{1,0:T(8,128)(2,1)S(1)}, bf16[128,1664]{1,0:T(8,128)(2,1)}, u32[]{:S(2)}, u32[]{:S(2)}) collective-permute-start(bf16[128,1664]{1,0:T(8,128)(2,1)S(1)} %collective-permute-done.4.refs_9_), channel_id=1, source_target_pairs={{0,8},{8,0},{1,9},{9,1},{2,10},{10,2},{3,11},{11,3},{4,12},{12,4},... | collective-permute-start | bytes 1277960 | tf_op jit(solution)/shard_map/ppermute | solution.py:25
  23.0 13.2 %collective-permute-start.8 = (bf16[1664,128]{1,0:T(8,128)(2,1)}, bf16[1664,128]{1,0:T(8,128)(2,1)}, u32[]{:S(2)}, u32[]{:S(2)}) collective-permute-start(bf16[1664,128]{1,0:T(8,128)(2,1)} %collective-permute-done.7.refs_13_), channel_id=1, source_target_pairs={{0,8},{8,0},{1,9},{9,1},{2,10},{10,2},{3,11},{11,3},{4,12},{12,4},... | collective-permute-start | bytes 1277960 | tf_op jit(solution)/shard_map/ppermute | solution.py:25
  41.0 45.9 %collective-permute-start.19 = (bf16[96,1152]{1,0:T(8,128)(2,1)S(1)}, bf16[96,1152]{1,0:T(8,128)(2,1)S(1)}, u32[]{:S(2)}, u32[]{:S(2)}) collective-permute-start(bf16[96,1152]{1,0:T(8,128)(2,1)S(1)} %get-tuple-element.46), channel_id=1, source_target_pairs={{0,32},{16,48},{32,0},{48,16},{1,33},{17,49},{33,1},{49,17},{2,34}... | collective-permute-start | bytes 663560 | tf_op jit(solution)/shard_map/ppermute | solution.py:25
  52.4 36.2 %collective-permute-start.20 = (bf16[96,1152]{1,0:T(8,128)(2,1)S(1)}, bf16[96,1152]{1,0:T(8,128)(2,1)S(1)}, u32[]{:S(2)}, u32[]{:S(2)}) collective-permute-start(bf16[96,1152]{1,0:T(8,128)(2,1)S(1)} %get-tuple-element.47), channel_id=1, source_target_pairs={{0,48},{16,0},{32,16},{48,32},{1,49},{17,1},{33,17},{49,33},{2,50}... | collective-permute-start | bytes 663560 | tf_op jit(solution)/shard_map/ppermute | solution.py:25
  61.8 26.8 %collective-permute-start.21 = (bf16[96,1152]{1,0:T(8,128)(2,1)S(1)}, bf16[96,1152]{1,0:T(8,128)(2,1)S(1)}, u32[]{:S(2)}, u32[]{:S(2)}) collective-permute-start(bf16[96,1152]{1,0:T(8,128)(2,1)S(1)} %get-tuple-element.48), channel_id=1, source_target_pairs={{0,16},{16,32},{32,48},{48,0},{1,17},{17,33},{33,49},{49,1},{2,18}... | collective-permute-start | bytes 663560 | tf_op jit(solution)/shard_map/ppermute | solution.py:25
  67.4 31.9 %collective-permute-start.9 = (bf16[96,1152]{1,0:T(8,128)(2,1)S(1)}, bf16[96,1152]{1,0:T(8,128)(2,1)S(1)}, u32[]{:S(2)}, u32[]{:S(2)}) collective-permute-start(bf16[96,1152]{1,0:T(8,128)(2,1)S(1)} %get-tuple-element.33), channel_id=1, source_target_pairs={{0,32},{16,48},{32,0},{48,16},{1,33},{17,49},{33,1},{49,17},{2,34}... | collective-permute-start | bytes 663560 | tf_op jit(solution)/shard_map/ppermute | solution.py:25
  86.4 12.8 %collective-permute-start.10 = (bf16[96,1152]{1,0:T(8,128)(2,1)S(1)}, bf16[96,1152]{1,0:T(8,128)(2,1)S(1)}, u32[]{:S(2)}, u32[]{:S(2)}) collective-permute-start(bf16[96,1152]{1,0:T(8,128)(2,1)S(1)} %get-tuple-element.34), channel_id=1, source_target_pairs={{0,48},{16,0},{32,16},{48,32},{1,49},{17,1},{33,17},{49,33},{2,50}... | collective-permute-start | bytes 663560 | tf_op jit(solution)/shard_map/ppermute | solution.py:25
  86.9 12.4 %collective-permute-start.11 = (bf16[96,1152]{1,0:T(8,128)(2,1)S(1)}, bf16[96,1152]{1,0:T(8,128)(2,1)S(1)}, u32[]{:S(2)}, u32[]{:S(2)}) collective-permute-start(bf16[96,1152]{1,0:T(8,128)(2,1)S(1)} %get-tuple-element.35), channel_id=1, source_target_pairs={{0,16},{16,32},{32,48},{48,0},{1,17},{17,33},{33,49},{49,1},{2,18}... | collective-permute-start | bytes 663560 | tf_op jit(solution)/shard_map/ppermute | solution.py:25
  91.9 24.6 %collective-permute-start.22 = (bf16[96,1024]{1,0:T(8,128)(2,1)S(1)}, bf16[96,1024]{1,0:T(8,128)(2,1)S(1)}, u32[]{:S(2)}, u32[]{:S(2)}) collective-permute-start(bf16[96,1024]{1,0:T(8,128)(2,1)S(1)} %get-tuple-element.50), channel_id=1, source_target_pairs={{0,5},{1,4},{2,7},{3,6},{4,1},{5,0},{6,3},{7,2},{8,13},{9,12},{10,... | collective-permute-start | bytes 589832 | tf_op jit(solution)/shard_map/ppermute | solution.py:34
  97.8 21.5 %collective-permute-start.23 = (bf16[96,1024]{1,0:T(8,128)(2,1)S(1)}, bf16[96,1024]{1,0:T(8,128)(2,1)S(1)}, u32[]{:S(2)}, u32[]{:S(2)}) collective-permute-start(bf16[96,1024]{1,0:T(8,128)(2,1)S(1)} %get-tuple-element.51), channel_id=1, source_target_pairs={{0,3},{1,2},{2,5},{3,4},{4,7},{5,6},{6,1},{7,0},{8,11},{9,10},{10,... | collective-permute-start | bytes 589832 | tf_op jit(solution)/shard_map/ppermute | solution.py:34
  102.5 18.9 %collective-permute-start.12 = (bf16[96,1024]{1,0:T(8,128)(2,1)S(1)}, bf16[96,1024]{1,0:T(8,128)(2,1)S(1)}, u32[]{:S(2)}, u32[]{:S(2)}) collective-permute-start(bf16[96,1024]{1,0:T(8,128)(2,1)S(1)} %get-tuple-element.37), channel_id=1, source_target_pairs={{0,5},{1,4},{2,7},{3,6},{4,1},{5,0},{6,3},{7,2},{8,13},{9,12},{10,... | collective-permute-start | bytes 589832 | tf_op jit(solution)/shard_map/ppermute | solution.py:34
  105.7 16.7 %collective-permute-start.13 = (bf16[96,1024]{1,0:T(8,128)(2,1)S(1)}, bf16[96,1024]{1,0:T(8,128)(2,1)S(1)}, u32[]{:S(2)}, u32[]{:S(2)}) collective-permute-start(bf16[96,1024]{1,0:T(8,128)(2,1)S(1)} %get-tuple-element.38), channel_id=1, source_target_pairs={{0,3},{1,2},{2,5},{3,4},{4,7},{5,6},{6,1},{7,0},{8,11},{9,10},{10,... | collective-permute-start | bytes 589832 | tf_op jit(solution)/shard_map/ppermute | solution.py:34
  112.1 20.1 %collective-permute-start.17 = (bf16[96,1024]{1,0:T(8,128)(2,1)S(1)}, bf16[96,1024]{1,0:T(8,128)(2,1)S(1)}, u32[]{:S(2)}, u32[]{:S(2)}) collective-permute-start(bf16[96,1024]{1,0:T(8,128)(2,1)S(1)} %get-tuple-element.43), channel_id=1, source_target_pairs={{0,2},{1,3},{2,4},{3,5},{4,6},{5,7},{6,0},{7,1},{8,10},{9,11},{10,... | collective-permute-start | bytes 589832 | tf_op jit(solution)/shard_map/ppermute | solution.py:34
  116.4 21.2 %collective-permute-start.18 = (bf16[96,1024]{1,0:T(8,128)(2,1)S(1)}, bf16[96,1024]{1,0:T(8,128)(2,1)S(1)}, u32[]{:S(2)}, u32[]{:S(2)}) collective-permute-start(bf16[96,1024]{1,0:T(8,128)(2,1)S(1)} %get-tuple-element.44), channel_id=1, source_target_pairs={{0,6},{1,7},{2,0},{3,1},{4,2},{5,3},{6,4},{7,5},{8,14},{9,15},{10,... | collective-permute-start | bytes 589832 | tf_op jit(solution)/shard_map/ppermute | solution.py:34
  119.3 19.2 %collective-permute-start.14 = (bf16[96,1024]{1,0:T(8,128)(2,1)S(1)}, bf16[96,1024]{1,0:T(8,128)(2,1)S(1)}, u32[]{:S(2)}, u32[]{:S(2)}) collective-permute-start(bf16[96,1024]{1,0:T(8,128)(2,1)S(1)} %get-tuple-element.40), channel_id=1, source_target_pairs={{0,7},{1,6},{2,1},{3,0},{4,3},{5,2},{6,5},{7,4},{8,15},{9,14},{10,... | collective-permute-start | bytes 589832 | tf_op jit(solution)/shard_map/ppermute | solution.py:34
  121.5 17.1 %collective-permute-start.15 = (bf16[96,1024]{1,0:T(8,128)(2,1)S(1)}, bf16[96,1024]{1,0:T(8,128)(2,1)S(1)}, u32[]{:S(2)}, u32[]{:S(2)}) collective-permute-start(bf16[96,1024]{1,0:T(8,128)(2,1)S(1)} %get-tuple-element.41), channel_id=1, source_target_pairs={{0,1},{1,0},{2,3},{3,2},{4,5},{5,4},{6,7},{7,6},{8,9},{9,8},{10,11... | collective-permute-start | bytes 589832 | tf_op jit(solution)/shard_map/ppermute | solution.py:34
  122.4 16.7 %collective-permute-start.16 = (bf16[96,1024]{1,0:T(8,128)(2,1)S(1)}, bf16[96,1024]{1,0:T(8,128)(2,1)S(1)}, u32[]{:S(2)}, u32[]{:S(2)}) collective-permute-start(bf16[96,1024]{1,0:T(8,128)(2,1)S(1)} %get-tuple-element.42), channel_id=1, source_target_pairs={{0,4},{1,5},{2,6},{3,7},{4,0},{5,1},{6,2},{7,3},{8,12},{9,13},{10,... | collective-permute-start | bytes 589832 | tf_op jit(solution)/shard_map/ppermute | solution.py:34
  (6 other events, 65.2 us)

commit v2 on v1

--- a/solution.py
+++ b/solution.py
@@ -11,10 +11,9 @@
 SEQ = ("y", "x", "core")
 HEAD = ("z", "yh")
 CHUNK = 32
-HALVES = 2
+GROUPS = ((2, 1, 3, 0),)
 LOWEST = -1e30
 BLOCKED = 1e30
-TURNS = (2, 1, 3, 0)
 ROUTES = (((2, 1), (1, 1)), ((3, 1), (0, 1), (2, 0)), ((1, 0), (3, 0), (0, 0)))
 BF16 = jnp.bfloat16
 F32 = jnp.float32
@@ -34,7 +33,7 @@
     return lax.ppermute(value, HEAD, pairs)
 
 
-def attend_kernel(items, count, images, *refs, scale, hd, group, blocks, keys, padded, start):
+def attend_kernel(items, count, images, *refs, scale, hd, group, blocks, keys, padded):
     q_refs = refs[:blocks]
     key_refs = refs[blocks : blocks + 4]
     value_refs = refs[blocks + 4 : blocks + 8]
@@ -57,7 +56,7 @@
     for i in range(blocks):
         copies.append(
             pltpu.make_async_copy(
-                q_refs[i].at[pl.ds(start, tokens)], q_all.at[pl.ds(i * tokens, tokens)], sems.at[8 + i]
+                q_refs[i], q_all.at[pl.ds(i * tokens, tokens)], sems.at[8 + i]
             )
         )
     for copy in copies:
@@ -137,7 +136,7 @@
         out_ref[near, width:] = pieces.astype(BF16)
 
 
-def attend(payloads, items, count, images, keys_t, values, keys, tokens, start):
+def attend(payloads, items, count, images, keys_t, values, keys, tokens):
     blocks = len(payloads)
     wide = payloads[0].shape[1]
     hd, padded = keys_t[0].shape
@@ -155,7 +154,6 @@
             blocks=blocks,
             keys=keys,
             padded=padded,
-            start=start,
         ),
         out_shape=[jax.ShapeDtypeStruct((tokens, wide), BF16)] * blocks,
         grid_spec=pltpu.PrefetchScalarGridSpec(
@@ -176,7 +174,7 @@
                 pltpu.SemaphoreType.DMA((8 + blocks,)),
             ],
         ),
-        compiler_params=pltpu.CompilerParams(vmem_limit_bytes=48 << 20),
+        compiler_params=pltpu.CompilerParams(vmem_limit_bytes=32 << 20),
         cost_estimate=pl.CostEstimate(
             flops=2 * blocks * tokens * group * padded * 2 * hd,
             bytes_accessed=blocks * tokens * width * 4 + padded * hd * 16,
@@ -186,9 +184,9 @@
     )(items, count, images, *payloads, *keys_t, *values)
 
 
-def work_list(hits):
-    tokens, tiles = hits.shape
-    flags = jnp.any(hits.reshape(tokens // CHUNK, CHUNK, tiles), axis=1).reshape(-1)
+def work_list(wanted):
+    tiles = wanted.shape[-1]
+    flags = wanted.reshape(-1) > 0
     size = flags.shape[0]
     place = jnp.arange(size, dtype=jnp.int32)
     rank = jnp.sum((place[None, :] < place[:, None]) & flags[None, :], axis=1)
@@ -272,27 +270,21 @@
             ],
         ),
         cost_estimate=pl.CostEstimate(
-            flops=2 * tokens * depth * width * wanted,
-            bytes_accessed=2 * wanted * (depth * width + tokens * (depth + width)),
-            transcendentals=0,
-        ),
-        compiler_params=pltpu.CompilerParams(vmem_limit_bytes=52 << 20),
+            flops=2 * tokens * depth, bytes_accessed=2 * tokens * depth, transcendentals=0
+        ),
+        compiler_params=pltpu.CompilerParams(vmem_limit_bytes=50 << 20),
         name="project",
     )(columns, *sources, weight)
 
 
 def settle_kernel(gate_ref, order_ref, layer_ref, *refs):
     terms, out_ref = refs[:-1], refs[-1]
-    each = len(terms) // HALVES
-    tokens = order_ref.shape[0] // HALVES
     total = None
-    for half in range(HALVES):
-        order = order_ref[half * tokens : (half + 1) * tokens]
-        for ref in terms[half * each : (half + 1) * each]:
-            part = lax.dot_general(
-                order, ref[...], (((0,), (0,)), ((), ())), preferred_element_type=F32
-            )
-            total = part if total is None else total + part
+    for ref in terms:
+        part = lax.dot_general(
+            order_ref[...], ref[...], (((0,), (0,)), ((), ())), preferred_element_type=F32
+        )
+        total = part if total is None else total + part
     out_ref[...] = (layer_ref[...].astype(F32) + gate_ref[0] * total).astype(BF16)
 
 
@@ -301,7 +293,6 @@
     cuts = 4
     step = width // cuts
     tall = pl.BlockSpec((tokens, step), lambda g: (0, g))
-    part = pl.BlockSpec((tokens // HALVES, step), lambda g: (0, g))
     return pl.pallas_call(
         settle_kernel,
         out_shape=jax.ShapeDtypeStruct((tokens, width), BF16),
@@ -311,9 +302,9 @@
             pl.BlockSpec((tokens, tokens), lambda g: (0, 0)),
             tall,
         ]
-        + [part] * len(terms),
+        + [tall] * len(terms),
         out_specs=tall,
-        compiler_params=pltpu.CompilerParams(vmem_limit_bytes=32 << 20),
+        compiler_params=pltpu.CompilerParams(vmem_limit_bytes=24 << 20),
         name="settle",
     )(gate, order, layer, *terms)
 
@@ -331,13 +322,11 @@
     padded = -(-keys // 128) * 128
     spare = jnp.broadcast_to(image_keys[:1], (padded - keys, hd))
     key_t = jnp.concatenate([image_keys, spare], axis=0).T
-    own = (key_t, jnp.pad(image_values, ((0, padded - keys), (0, 0))))
+    value = jnp.pad(image_values, ((0, padded - keys), (0, 0)))
+    own = (key_t, value)
     across = [shifted(v, "y", 1) for v in own]
-    beside = [shifted(v, "core", 1) for v in own]
-    diagonal = [shifted(v, "core", 1) for v in across]
-    tiles = (own, beside, across, diagonal)
-
-    bounds, _ = lax.optimization_barrier((image_range, key_t))
+
+    bounds, _, _ = lax.optimization_barrier((image_range, key_t, value))
     low, high = bounds[0], bounds[1]
     grade = jnp.where(low < high, low * 16 + high, 1 << 10)
     place = jnp.arange(tokens, dtype=jnp.int32)
@@ -350,40 +339,61 @@
     payload = jnp.dot(
         order, jnp.concatenate([queries, extra], axis=1), preferred_element_type=F32
     ).astype(BF16)
-    payloads = [payload if s == 0 else shifted(payload, "x", s) for s in TURNS]
+    payloads = {s: shifted(payload, "x", s) for s in (2, 1, 3)}
+    payloads[0] = payload
+    late = lax.optimization_barrier((key_t, value, payloads[1]))[:2]
+    beside = [shifted(v, "core", 1) for v in late]
+    diagonal = [shifted(v, "core", 1) for v in across]
+    tiles = (own, beside, across, diagonal)
+
+    image = jnp.arange(tile_counts.shape[0])
+    ends = jnp.sum(jnp.where(image[None, :] <= image[:, None], tile_counts[None, :], 0), axis=1)
+    tile = jnp.arange(ny * nx * nc, dtype=jnp.int32)
+    owner = jnp.sum((ends[None, :] <= tile[:, None]).astype(jnp.int32), axis=1)
+    hits = (low[:, None] <= owner[None, :]) & (owner[None, :] < high[:, None])
+    which = jnp.arange(tokens // CHUNK, dtype=jnp.int32)
+    member = rank[:, None] // CHUNK == which[None, :]
+    live = jnp.any(member[:, :, None] & hits[:, None, :], axis=0).astype(jnp.int32)
+    everyone = lax.all_gather(live, "x")
 
     def number(yy, cc):
         return (yy % ny * nx + x) * nc + cc % nc
 
     held = jnp.stack([number(y, core), number(y, core + 1), number(y + 1, core), number(y + 1, core + 1)])
-    image = jnp.arange(tile_counts.shape[0])
-    ends = jnp.sum(jnp.where(image[None, :] <= image[:, None], tile_counts[None, :], 0), axis=1)
-    images = jnp.sum((ends[None, :] <= held[:, None]).astype(jnp.int32), axis=1)
-
-    share = tokens // HALVES
-    columns = [
-        jnp.stack([(z + dz) % nz * nyh + (yh + dy) % nyh for dz, dy in some]).astype(jnp.int32)
-        for some in ROUTES
-    ]
+    mine = (held[:, None] == tile[None, :]).astype(jnp.int32)
+    images = jnp.sum(mine * owner[None, :], axis=1)
+
+    parts = {}
+    for turns in GROUPS:
+        source = jnp.stack([(x - s) % nx for s in turns])
+        from_whom = (source[:, None] == jnp.arange(nx)[None, :]).astype(jnp.int32)
+        chosen = from_whom[:, :, None, None, None] * everyone[None, :, :, None, :]
+        wanted = jnp.sum(chosen * mine[None, None, None, :, :], axis=(1, 4))
+        items, count = work_list(wanted)
+        got = attend(
+            [payloads[s] for s in turns],
+            items,
+            count,
+            images,
+            [t[0] for t in tiles],
+            [t[1] for t in tiles],
+            keys,
+            tokens,
+        )
+        for s, part in zip(turns, got):
+            parts[s] = part if s == 0 else shifted(part, "x", nx - s)
+
+    sources = [parts[s] for s in (2, 1, 3, 0)]
     terms = []
-    for half in range(HALVES):
-        start = half * share
-        reach = jnp.concatenate(
-            [p[start : start + share, width : width + 2] for p in payloads], axis=0
-        ).astype(jnp.int32)
-        hits = (reach[:, :1] <= images[None, :]) & (images[None, :] < reach[:, 1:])
-        items, count = work_list(hits)
-        parts = attend(
-            payloads, items, count, images, [t[0] for t in tiles], [t[1] for t in tiles], keys, share, start
-        )
-        parts = [p if s == 0 else shifted(p, "x", nx - s) for s, p in zip(TURNS, parts)]
-        sources = parts
-        for some, column in zip(ROUTES, columns):
-            got = project(sources, out_weight, column, width, hd)
-            if len(sources) > 1:
-                sources = [got[-1]]
-            for (dz, dy), term in zip(some, got):
-                terms.append(term if (dz, dy) == (0, 0) else head_shifted(term, dz, dy))
+    for some in ROUTES:
+        column = jnp.stack([(z + dz) % nz * nyh + (yh + dy) % nyh for dz, dy in some]).astype(jnp.int32)
+        got = project(sources, out_weight, column, width, hd)
+        if len(sources) > 1:
+            sources = [got[-1]]
+        for (dz, dy), term in zip(some, got):
+            if len(terms) > 4:
+                term = lax.optimization_barrier((term, terms[len(terms) - 5]))[0]
+            terms.append(term if (dz, dy) == (0, 0) else head_shifted(term, dz, dy))
     return settle(jnp.tanh(attn_gate), order, layer_input, terms)
 
 

time: 150 us -> 153 us (1.020)
  starting transfers between devices: 81.3 us -> 49 us
  waiting for transfers between devices: 21 us -> 48.4 us
  blocking collectives: 0 us -> 21.1 us
  Pallas kernels: 35.4 us -> 24.5 us
    all_gather x0 -> x1, blocking collectives: none -> 21.1 us  [shards(): everyone = lax.all_gather(live, 'x')]
    ppermute x14 -> x7, waiting for transfers between devices: 5.74 us -> 24.6 us  [head_shifted(): return lax.ppermute(value, HEAD, pairs)]
    ppermute x15 -> x12, starting transfers between devices: 51 us -> 33.2 us  [shifted(): lax.ppermute(value, axis, [(s, (s + steps) % count) for s in range(count)])]
    ppermute x14 -> x7, starting transfers between devices: 30.3 us -> 15.8 us  [head_shifted(): return lax.ppermute(value, HEAD, pairs)]
    pallas_call x6 -> x3, Pallas kernels: 22.1 us -> 11.5 us  [project(): pl.pallas_call(lambda *refs: project_kernel(*refs, hd=hd, group=depth //...]
    ppermute x15 -> x12, waiting for transfers between devices: 15.3 us -> 23.9 us  [shifted(): lax.ppermute(value, axis, [(s, (s + steps) % count) for s in range(count)])]
    unnamed x4 -> x8, local copies, waits for them, and re-layouts: 1.39 us -> 3.15 us
    pallas_call x2 -> x1, Pallas kernels: 9.57 us -> 10.1 us  [attend(): pl.pallas_call(lambda *refs: attend_kernel(*refs, scale=1.0 / math.sqrt(h...]
  transfers between devices with their start and end apart: 29 -> 19, of which waited for: 6 -> 9; matrix products, arithmetic and copies ran while one was open for 7% -> 2% of each run, Pallas kernels for 18% -> 5%
where the time goes in v2:
time: 153 us; the launch traced here: 155 us
  starting transfers between devices  49 us (32%)
  waiting for transfers between devices  48.4 us (32%)
  Pallas kernels  24.5 us (16%)
  blocking collectives  21.1 us (14%)
  other arithmetic  5.07 us (3%)
  local copies, waits for them, and re-layouts  5.06 us (3%)
    ppermute x12, starting transfers between devices, shifted(): lax.ppermute(value, axis, [(s, (s + steps) % count) for s in range(count)])  33.2 us
    ppermute x7, waiting for transfers between devices, head_shifted(): return lax.ppermute(value, HEAD, pairs)  24.6 us
    ppermute x12, waiting for transfers between devices, shifted(): lax.ppermute(value, axis, [(s, (s + steps) % count) for s in range(count)])  23.9 us
    all_gather x1, blocking collectives, shards(): everyone = lax.all_gather(live, 'x')  21.1 us
    ppermute x7, starting transfers between devices, head_shifted(): return lax.ppermute(value, HEAD, pairs)  15.8 us
    pallas_call x3, Pallas kernels, project(): pl.pallas_call(lambda *refs: project_kernel(*refs, hd=hd, group=depth //...  11.5 us
    pallas_call x1, Pallas kernels, attend(): pl.pallas_call(lambda *refs: attend_kernel(*refs, scale=1.0 / math.sqrt(h...  10.1 us
    unnamed x8, local copies, waits for them, and re-layouts  3.15 us
  transfers between devices with their start and end apart: 19, of which 9 were waited for; matrix products, arithmetic and copies ran while one was open for 2% of the time, Pallas kernels for 5%

profile of v2, /device:TPU:8, one launch (start us, length us, event | category | flops | bytes accessed | tf_op | source)
XLA Modules:
  0.0 155.4 jit_solution(6180993014965348560)
XLA Ops:
  5.0 1.3 convolution_convert_fusion.refs_6_
  6.3 1.6 %collective-permute-start.1 = (bf16[192,1152]{1,0:T(8,128)(2,1)S(1)}, bf16[192,1152]{1,0:T(8,128)(2,1)S(1)}, u32[]{:S(2)}, u32[]{:S(2)}) collective-permute-start(bf16[192,1152]{1,0:T(8,128)(2,1)S(1)} %convolution_convert_fusion.refs_6_), channel_id=1, source_target_pairs={{0,16},{16,32},{32,48},{48,0},{1,17},{17,33},{33,49},{49,1},{2,18}... | collective-permute-start | bytes 1327112 | tf_op jit(solution)/shard_map/ppermute | solution.py:24
  7.8 2.7 %collective-permute-start = (bf16[192,1152]{1,0:T(8,128)(2,1)S(1)}, bf16[192,1152]{1,0:T(8,128)(2,1)S(1)}, u32[]{:S(2)}, u32[]{:S(2)}) collective-permute-start(bf16[192,1152]{1,0:T(8,128)(2,1)S(1)} %convolution_convert_fusion.refs_6_), channel_id=1, source_target_pairs={{0,32},{16,48},{32,0},{48,16},{1,33},{17,49},{33,1},{49,17},{2,34}... | collective-permute-start | bytes 1327112 | tf_op jit(solution)/shard_map/ppermute | solution.py:24
  10.5 1.4 collective-permute-start.2
  12.4 1.6 %collective-permute-start.7 = (bf16[1664,128]{1,0:T(8,128)(2,1)S(1)}, bf16[1664,128]{1,0:T(8,128)(2,1)}, u32[]{:S(2)}, u32[]{:S(2)}) collective-permute-start(bf16[1664,128]{1,0:T(8,128)(2,1)S(1)} %pad.8.refs_11_), channel_id=1, source_target_pairs={{0,64},{64,0},{1,65},{65,1},{2,66},{66,2},{3,67},{67,3},{4,68},{68... | collective-permute-start | bytes 1277960 | tf_op jit(solution)/shard_map/ppermute | solution.py:24
  15.3 21.1 %all-gather.1 = s32[4,6,16]{2,1,0:T(8,128)S(1)} all-gather(s32[1,6,16]{2,1,0:T(8,128)S(1)} %convert_bitcast_fusion), channel_id=2, replica_groups=mesh['y'=2,'x'=4,'core'=2,'z'=4,'yh'=2] {'x'}, dimensions={0}, use_global_device_ids=true | all-gather | bytes 1920 | tf_op jit(solution)/shard_map/all_gather | solution.py:357
  43.2 10.1 %attend.1 = (bf16[192,1152]{1,0:T(8,128)(2,1)}, bf16[192,1152]{1,0:T(8,128)(2,1)}, bf16[192,1152]{1,0:T(8,128)(2,1)}, bf16[192,1152]{1,0:T(8,128)(2,1)S(1)}) custom-call(s32[99]{0:T(128)S(1)} %compare_select_fusion.1.refs_0_, s32[1]{0:T(128)} %bitcast.16.refs_1_, s32[4]{0:T(128)S(1)} %select_reduce_fusion.2.refs_2_, ...), custom_call_target="tpu_custom_call" | custom-call | flops 5234491392 | bytes 6553600 | tf_op jit(solution)/shard_map/attend/pallas_call | solution.py:148
  53.3 22.8 %collective-permute-start.10 = (bf16[192,1152]{1,0:T(8,128)(2,1)}, bf16[192,1152]{1,0:T(8,128)(2,1)S(1)}, u32[]{:S(2)}, u32[]{:S(2)}) collective-permute-start(bf16[192,1152]{1,0:T(8,128)(2,1)} %get-tuple-element.28), channel_id=1, source_target_pairs={{0,48},{16,0},{32,16},{48,32},{1,49},{17,1},{33,17},{49,33},{2,50}... | collective-permute-start | bytes 1327112 | tf_op jit(solution)/shard_map/ppermute | solution.py:24
  76.2 1.5 collective-permute-start.9
  77.8 18.0 %collective-permute-done.10.refs_2_ = bf16[192,1152]{1,0:T(8,128)(2,1)S(1)} collective-permute-done((bf16[192,1152]{1,0:T(8,128)(2,1)}, bf16[192,1152]{1,0:T(8,128)(2,1)S(1)}, u32[]{:S(2)}, u32[]{:S(2)}) %collective-permute-start.10) | collective-permute-done | bytes 442400 | tf_op jit(solution)/shard_map/ppermute | solution.py:24
  95.8 3.9 %collective-permute-done.11.refs_3_ = bf16[192,1152]{1,0:T(8,128)(2,1)S(1)} collective-permute-done((bf16[192,1152]{1,0:T(8,128)(2,1)}, bf16[192,1152]{1,0:T(8,128)(2,1)S(1)}, u32[]{:S(2)}, u32[]{:S(2)}) %collective-permute-start.11) | collective-permute-done | bytes 442400 | tf_op jit(solution)/shard_map/ppermute | solution.py:24
  99.7 3.4 %project.3 = (bf16[192,1024]{1,0:T(8,128)(2,1)S(1)}, bf16[192,1024]{1,0:T(8,128)(2,1)S(1)}, bf16[192,1024]{1,0:T(8,128)(2,1)S(1)}) custom-call(s32[2]{0:T(128)S(1)} %pad_add_fusion.refs_0_, bf16[192,1152]{1,0:T(8,128)(2,1)S(1)} %collective-permute-done.9.refs_1_, bf16[192,1152]{1,0:T(8,128)(2,1)S(1)} %collective-permute-done.10.refs_2_, ...), custom_call_target="tpu_custom_call" | custom-call | flops 393216 | bytes 393216 | tf_op jit(solution)/shard_map/project/pallas_call | solution.py:259
  103.2 3.7 %collective-permute-start.13 = (bf16[192,1024]{1,0:T(8,128)(2,1)S(1)}, bf16[192,1024]{1,0:T(8,128)(2,1)S(1)}, u32[]{:S(2)}, u32[]{:S(2)}) collective-permute-start(bf16[192,1024]{1,0:T(8,128)(2,1)S(1)} %get-tuple-element.32), channel_id=1, source_target_pairs={{0,3},{1,2},{2,5},{3,4},{4,7},{5,6},{6,1},{7,0},{8,11},{9,10},{10,... | collective-permute-start | bytes 1179656 | tf_op jit(solution)/shard_map/ppermute | solution.py:33
  106.9 4.3 %collective-permute-start.12 = (bf16[192,1024]{1,0:T(8,128)(2,1)S(1)}, bf16[192,1024]{1,0:T(8,128)(2,1)S(1)}, u32[]{:S(2)}, u32[]{:S(2)}) collective-permute-start(bf16[192,1024]{1,0:T(8,128)(2,1)S(1)} %get-tuple-element.31), channel_id=1, source_target_pairs={{0,5},{1,4},{2,7},{3,6},{4,1},{5,0},{6,3},{7,2},{8,13},{9,12},{10,... | collective-permute-start | bytes 1179656 | tf_op jit(solution)/shard_map/ppermute | solution.py:33
  111.3 4.0 %project.4 = (bf16[192,1024]{1,0:T(8,128)(2,1)S(1)}, bf16[192,1024]{1,0:T(8,128)(2,1)S(1)}, bf16[192,1024]{1,0:T(8,128)(2,1)S(1)}) custom-call(s32[3]{0:T(128)S(1)} %pad_add_fusion.3.refs_0_, bf16[192,1024]{1,0:T(8,128)(2,1)S(1)} %get-tuple-element.33.refs_1_, bf16[1024,8192]{1,0:T(8,128)(2,1)} %refs_2_.3), custom_call_target="tpu_custom_call" | custom-call | flops 393216 | bytes 393216 | tf_op jit(solution)/shard_map/project/pallas_call | solution.py:259
  115.3 2.7 %collective-permute-start.14 = (bf16[192,1024]{1,0:T(8,128)(2,1)S(1)}, bf16[192,1024]{1,0:T(8,128)(2,1)S(1)}, u32[]{:S(2)}, u32[]{:S(2)}) collective-permute-start(bf16[192,1024]{1,0:T(8,128)(2,1)S(1)} %get-tuple-element.34), channel_id=1, source_target_pairs={{0,7},{1,6},{2,1},{3,0},{4,3},{5,2},{6,5},{7,4},{8,15},{9,14},{10,... | collective-permute-start | bytes 1179656 | tf_op jit(solution)/shard_map/ppermute | solution.py:33
  118.0 4.0 %project.5 = (bf16[192,1024]{1,0:T(8,128)(2,1)S(1)}, bf16[192,1024]{1,0:T(8,128)(2,1)S(1)}, bf16[192,1024]{1,0:T(8,128)(2,1)S(1)}) custom-call(s32[3]{0:T(128)S(1)} %pad_add_fusion.4.refs_0_, bf16[192,1024]{1,0:T(8,128)(2,1)S(1)} %get-tuple-element.33.refs_1_, bf16[1024,8192]{1,0:T(8,128)(2,1)} %refs_2_.3), custom_call_target="tpu_custom_call" | custom-call | flops 393216 | bytes 393216 | tf_op jit(solution)/shard_map/project/pallas_call | solution.py:259
  122.1 1.4 collective-permute-start.15
  123.5 3.6 %collective-permute-start.18 = (bf16[192,1024]{1,0:T(8,128)(2,1)S(1)}, bf16[192,1024]{1,0:T(8,128)(2,1)S(1)}, u32[]{:S(2)}, u32[]{:S(2)}) collective-permute-start(bf16[192,1024]{1,0:T(8,128)(2,1)S(1)} %get-tuple-element.40), channel_id=1, source_target_pairs={{0,6},{1,7},{2,0},{3,1},{4,2},{5,3},{6,4},{7,5},{8,14},{9,15},{10,... | collective-permute-start | bytes 1179656 | tf_op jit(solution)/shard_map/ppermute | solution.py:33
  127.2 2.3 %collective-permute-done.12.refs_0_ = bf16[192,1024]{1,0:T(8,128)(2,1)S(1)} collective-permute-done((bf16[192,1024]{1,0:T(8,128)(2,1)S(1)}, bf16[192,1024]{1,0:T(8,128)(2,1)S(1)}, u32[]{:S(2)}, u32[]{:S(2)}) %collective-permute-start.12) | collective-permute-done | bytes 393248 | tf_op jit(solution)/shard_map/ppermute | solution.py:33
  130.2 6.1 %collective-permute-done.14.refs_2_ = bf16[192,1024]{1,0:T(8,128)(2,1)S(1)} collective-permute-done((bf16[192,1024]{1,0:T(8,128)(2,1)S(1)}, bf16[192,1024]{1,0:T(8,128)(2,1)S(1)}, u32[]{:S(2)}, u32[]{:S(2)}) %collective-permute-start.14) | collective-permute-done | bytes 393248 | tf_op jit(solution)/shard_map/ppermute | solution.py:33
  136.3 7.8 %collective-permute-done.15.refs_3_ = bf16[192,1024]{1,0:T(8,128)(2,1)S(1)} collective-permute-done((bf16[192,1024]{1,0:T(8,128)(2,1)S(1)}, bf16[192,1024]{1,0:T(8,128)(2,1)S(1)}, u32[]{:S(2)}, u32[]{:S(2)}) %collective-permute-start.15) | collective-permute-done | bytes 393248 | tf_op jit(solution)/shard_map/ppermute | solution.py:33
  144.1 8.3 %collective-permute-done.18.refs_6_ = bf16[192,1024]{1,0:T(8,128)(2,1)S(1)} collective-permute-done((bf16[192,1024]{1,0:T(8,128)(2,1)S(1)}, bf16[192,1024]{1,0:T(8,128)(2,1)S(1)}, u32[]{:S(2)}, u32[]{:S(2)}) %collective-permute-start.18) | collective-permute-done | bytes 393248 | tf_op jit(solution)/shard_map/ppermute | solution.py:33
  152.5 2.9 %settle.1 = bf16[192,1024]{1,0:T(8,128)(2,1)} custom-call(f32[1]{0:T(128)S(6)} %tanh.3.gate_ref, bf16[192,192]{1,0:T(8,128)(2,1)S(1)} %fusion.7.order_ref, bf16[192,1024]{1,0:T(8,128)(2,1)S(1)} %copy-done, bf16[192,1024]{1,0:T(8,128)(2,1)S(1)} %collective-permute-done.12.refs_0_, bf16[192,1024]{1,0:T(8,128)(2,1)S(1)} %collective-permute-done.13.refs_1_, ...), custom_call_target="tpu_custom_call" | custom-call | tf_op jit(solution)/shard_map/settle/pallas_call | solution.py:296
  (61 shorter events, 13.7 us)
Async XLA Ops:
  6.3 33.3 %collective-permute-start.1 = (bf16[192,1152]{1,0:T(8,128)(2,1)S(1)}, bf16[192,1152]{1,0:T(8,128)(2,1)S(1)}, u32[]{:S(2)}, u32[]{:S(2)}) collective-permute-start(bf16[192,1152]{1,0:T(8,128)(2,1)S(1)} %convolution_convert_fusion.refs_6_), channel_id=1, source_target_pairs={{0,16},{16,32},{32,48},{48,0},{1,17},{17,33},{33,49},{49,1},{2,18}... | collective-permute-start | bytes 1327112 | tf_op jit(solution)/shard_map/ppermute | solution.py:24
  7.8 31.9 %collective-permute-start = (bf16[192,1152]{1,0:T(8,128)(2,1)S(1)}, bf16[192,1152]{1,0:T(8,128)(2,1)S(1)}, u32[]{:S(2)}, u32[]{:S(2)}) collective-permute-start(bf16[192,1152]{1,0:T(8,128)(2,1)S(1)} %convolution_convert_fusion.refs_6_), channel_id=1, source_target_pairs={{0,32},{16,48},{32,0},{48,16},{1,33},{17,49},{33,1},{49,17},{2,34}... | collective-permute-start | bytes 1327112 | tf_op jit(solution)/shard_map/ppermute | solution.py:24
  10.5 29.7 %collective-permute-start.2 = (bf16[192,1152]{1,0:T(8,128)(2,1)S(1)}, bf16[192,1152]{1,0:T(8,128)(2,1)S(1)}, u32[]{:S(2)}, u32[]{:S(2)}) collective-permute-start(bf16[192,1152]{1,0:T(8,128)(2,1)S(1)} %convolution_convert_fusion.refs_6_), channel_id=1, source_target_pairs={{0,48},{16,0},{32,16},{48,32},{1,49},{17,1},{33,17},{49,33},{2,50}... | collective-permute-start | bytes 1327112 | tf_op jit(solution)/shard_map/ppermute | solution.py:24
  12.0 26.2 %collective-permute-start.4 = (bf16[128,1664]{1,0:T(8,128)(2,1)S(1)}, bf16[128,1664]{1,0:T(8,128)(2,1)S(1)}, u32[]{:S(2)}, u32[]{:S(2)}) collective-permute-start(bf16[128,1664]{1,0:T(8,128)(2,1)S(1)} %maximum_bitcast_fusion.refs_7_), channel_id=1, source_target_pairs={{0,64},{64,0},{1,65},{65,1},{2,66},{66,2},{3,67},{67,3},{4,68},{68... | collective-permute-start | bytes 1277960 | tf_op jit(solution)/shard_map/ppermute | solution.py:24
  12.4 26.6 %collective-permute-start.7 = (bf16[1664,128]{1,0:T(8,128)(2,1)S(1)}, bf16[1664,128]{1,0:T(8,128)(2,1)}, u32[]{:S(2)}, u32[]{:S(2)}) collective-permute-start(bf16[1664,128]{1,0:T(8,128)(2,1)S(1)} %pad.8.refs_11_), channel_id=1, source_target_pairs={{0,64},{64,0},{1,65},{65,1},{2,66},{66,2},{3,67},{67,3},{4,68},{68... | collective-permute-start | bytes 1277960 | tf_op jit(solution)/shard_map/ppermute | solution.py:24
  38.2 2.0 %collective-permute-start.5 = (bf16[128,1664]{1,0:T(8,128)(2,1)S(1)}, bf16[128,1664]{1,0:T(8,128)(2,1)S(1)}, u32[]{:S(2)}, u32[]{:S(2)}) collective-permute-start(bf16[128,1664]{1,0:T(8,128)(2,1)S(1)} %collective-permute-done.4.refs_9_), channel_id=1, source_target_pairs={{0,8},{8,0},{1,9},{9,1},{2,10},{10,2},{3,11},{11,3},{4,12},{12,4},... | collective-permute-start | bytes 1277960 | tf_op jit(solution)/shard_map/ppermute | solution.py:24
  38.3 0.8 copy-start.1
  39.1 2.1 %collective-permute-start.8 = (bf16[1664,128]{1,0:T(8,128)(2,1)}, bf16[1664,128]{1,0:T(8,128)(2,1)S(1)}, u32[]{:S(2)}, u32[]{:S(2)}) collective-permute-start(bf16[1664,128]{1,0:T(8,128)(2,1)} %collective-permute-done.7.refs_13_), channel_id=1, source_target_pairs={{0,8},{8,0},{1,9},{9,1},{2,10},{10,2},{3,11},{11,3},{4,12},{12,4},... | collective-permute-start | bytes 1277960 | tf_op jit(solution)/shard_map/ppermute | solution.py:24
  39.6 2.0 %collective-permute-start.3 = (bf16[128,1664]{1,0:T(8,128)(2,1)S(1)}, bf16[128,1664]{1,0:T(8,128)(2,1)S(1)}, u32[]{:S(2)}, u32[]{:S(2)}) collective-permute-start(bf16[128,1664]{1,0:T(8,128)(2,1)S(1)} %maximum_bitcast_fusion.refs_7_), channel_id=1, source_target_pairs={{0,8},{8,0},{1,9},{9,1},{2,10},{10,2},{3,11},{11,3},{4,12},{12,4},... | collective-permute-start | bytes 1277960 | tf_op jit(solution)/shard_map/ppermute | solution.py:24
  39.7 2.5 %collective-permute-start.6 = (bf16[1664,128]{1,0:T(8,128)(2,1)S(1)}, bf16[1664,128]{1,0:T(8,128)(2,1)S(1)}, u32[]{:S(2)}, u32[]{:S(2)}) collective-permute-start(bf16[1664,128]{1,0:T(8,128)(2,1)S(1)} %pad.8.refs_11_), channel_id=1, source_target_pairs={{0,8},{8,0},{1,9},{9,1},{2,10},{10,2},{3,11},{11,3},{4,12},{12,4},... | collective-permute-start | bytes 1277960 | tf_op jit(solution)/shard_map/ppermute | solution.py:24
  42.2 1.0 copy-start.2
  53.3 42.5 %collective-permute-start.10 = (bf16[192,1152]{1,0:T(8,128)(2,1)}, bf16[192,1152]{1,0:T(8,128)(2,1)S(1)}, u32[]{:S(2)}, u32[]{:S(2)}) collective-permute-start(bf16[192,1152]{1,0:T(8,128)(2,1)} %get-tuple-element.28), channel_id=1, source_target_pairs={{0,48},{16,0},{32,16},{48,32},{1,49},{17,1},{33,17},{49,33},{2,50}... | collective-permute-start | bytes 1327112 | tf_op jit(solution)/shard_map/ppermute | solution.py:24
  76.2 23.5 %collective-permute-start.11 = (bf16[192,1152]{1,0:T(8,128)(2,1)}, bf16[192,1152]{1,0:T(8,128)(2,1)S(1)}, u32[]{:S(2)}, u32[]{:S(2)}) collective-permute-start(bf16[192,1152]{1,0:T(8,128)(2,1)} %get-tuple-element.29), channel_id=1, source_target_pairs={{0,16},{16,32},{32,48},{48,0},{1,17},{17,33},{33,49},{49,1},{2,18}... | collective-permute-start | bytes 1327112 | tf_op jit(solution)/shard_map/ppermute | solution.py:24
  76.2 23.5 %collective-permute-start.9 = (bf16[192,1152]{1,0:T(8,128)(2,1)}, bf16[192,1152]{1,0:T(8,128)(2,1)S(1)}, u32[]{:S(2)}, u32[]{:S(2)}) collective-permute-start(bf16[192,1152]{1,0:T(8,128)(2,1)} %get-tuple-element.27), channel_id=1, source_target_pairs={{0,32},{16,48},{32,0},{48,16},{1,33},{17,49},{33,1},{49,17},{2,34}... | collective-permute-start | bytes 1327112 | tf_op jit(solution)/shard_map/ppermute | solution.py:24
  103.2 20.3 %collective-permute-start.13 = (bf16[192,1024]{1,0:T(8,128)(2,1)S(1)}, bf16[192,1024]{1,0:T(8,128)(2,1)S(1)}, u32[]{:S(2)}, u32[]{:S(2)}) collective-permute-start(bf16[192,1024]{1,0:T(8,128)(2,1)S(1)} %get-tuple-element.32), channel_id=1, source_target_pairs={{0,3},{1,2},{2,5},{3,4},{4,7},{5,6},{6,1},{7,0},{8,11},{9,10},{10,... | collective-permute-start | bytes 1179656 | tf_op jit(solution)/shard_map/ppermute | solution.py:33
  106.9 22.6 %collective-permute-start.12 = (bf16[192,1024]{1,0:T(8,128)(2,1)S(1)}, bf16[192,1024]{1,0:T(8,128)(2,1)S(1)}, u32[]{:S(2)}, u32[]{:S(2)}) collective-permute-start(bf16[192,1024]{1,0:T(8,128)(2,1)S(1)} %get-tuple-element.31), channel_id=1, source_target_pairs={{0,5},{1,4},{2,7},{3,6},{4,1},{5,0},{6,3},{7,2},{8,13},{9,12},{10,... | collective-permute-start | bytes 1179656 | tf_op jit(solution)/shard_map/ppermute | solution.py:33
  111.3 41.2 %copy-start = (bf16[192,1024]{1,0:T(8,128)(2,1)S(1)}, bf16[192,1024]{1,0:T(8,128)(2,1)}, u32[]{:S(2)}) copy-start(bf16[192,1024]{1,0:T(8,128)(2,1)} %layer_ref.1) | copy-start | bytes 1179652
  115.3 21.0 %collective-permute-start.14 = (bf16[192,1024]{1,0:T(8,128)(2,1)S(1)}, bf16[192,1024]{1,0:T(8,128)(2,1)S(1)}, u32[]{:S(2)}, u32[]{:S(2)}) collective-permute-start(bf16[192,1024]{1,0:T(8,128)(2,1)S(1)} %get-tuple-element.34), channel_id=1, source_target_pairs={{0,7},{1,6},{2,1},{3,0},{4,3},{5,2},{6,5},{7,4},{8,15},{9,14},{10,... | collective-permute-start | bytes 1179656 | tf_op jit(solution)/shard_map/ppermute | solution.py:33
  122.1 22.1 %collective-permute-start.15 = (bf16[192,1024]{1,0:T(8,128)(2,1)S(1)}, bf16[192,1024]{1,0:T(8,128)(2,1)S(1)}, u32[]{:S(2)}, u32[]{:S(2)}) collective-permute-start(bf16[192,1024]{1,0:T(8,128)(2,1)S(1)} %get-tuple-element.35), channel_id=1, source_target_pairs={{0,1},{1,0},{2,3},{3,2},{4,5},{5,4},{6,7},{7,6},{8,9},{9,8},{10,11... | collective-permute-start | bytes 1179656 | tf_op jit(solution)/shard_map/ppermute | solution.py:33
  123.5 20.7 %collective-permute-start.16 = (bf16[192,1024]{1,0:T(8,128)(2,1)S(1)}, bf16[192,1024]{1,0:T(8,128)(2,1)S(1)}, u32[]{:S(2)}, u32[]{:S(2)}) collective-permute-start(bf16[192,1024]{1,0:T(8,128)(2,1)S(1)} %get-tuple-element.36), channel_id=1, source_target_pairs={{0,4},{1,5},{2,6},{3,7},{4,0},{5,1},{6,2},{7,3},{8,12},{9,13},{10,... | collective-permute-start | bytes 1179656 | tf_op jit(solution)/shard_map/ppermute | solution.py:33
  123.5 28.9 %collective-permute-start.18 = (bf16[192,1024]{1,0:T(8,128)(2,1)S(1)}, bf16[192,1024]{1,0:T(8,128)(2,1)S(1)}, u32[]{:S(2)}, u32[]{:S(2)}) collective-permute-start(bf16[192,1024]{1,0:T(8,128)(2,1)S(1)} %get-tuple-element.40), channel_id=1, source_target_pairs={{0,6},{1,7},{2,0},{3,1},{4,2},{5,3},{6,4},{7,5},{8,14},{9,15},{10,... | collective-permute-start | bytes 1179656 | tf_op jit(solution)/shard_map/ppermute | solution.py:33
  129.5 23.0 %collective-permute-start.17 = (bf16[192,1024]{1,0:T(8,128)(2,1)S(1)}, bf16[192,1024]{1,0:T(8,128)(2,1)S(1)}, u32[]{:S(2)}, u32[]{:S(2)}) collective-permute-start(bf16[192,1024]{1,0:T(8,128)(2,1)S(1)} %get-tuple-element.38), channel_id=1, source_target_pairs={{0,2},{1,3},{2,4},{3,5},{4,6},{5,7},{6,0},{7,1},{8,10},{9,11},{10,... | collective-permute-start | bytes 1179656 | tf_op jit(solution)/shard_map/ppermute | solution.py:33

commit v3 on v2

--- a/solution.py
+++ b/solution.py
@@ -14,7 +14,6 @@
 GROUPS = ((2, 1, 3, 0),)
 LOWEST = -1e30
 BLOCKED = 1e30
-ROUTES = (((2, 1), (1, 1)), ((3, 1), (0, 1), (2, 0)), ((1, 0), (3, 0), (0, 0)))
 BF16 = jnp.bfloat16
 F32 = jnp.float32
 
@@ -199,7 +198,7 @@
     return items.astype(jnp.int32), count.reshape(1)
 
 
-def combined(parts, out_ref, hd, group):
+def combined(order_ref, parts, out_ref, hd, group):
     width = group * hd
     sums = []
     for ref in parts:
@@ -214,50 +213,48 @@
         mixed = parts[0][:, at].astype(F32) * shares[0][:, h : h + 1]
         for ref, share in zip(parts[1:], shares[1:]):
             mixed = mixed + ref[:, at].astype(F32) * share[:, h : h + 1]
-        out_ref[:, at] = mixed.astype(BF16)
-
-
-def project_kernel(columns, *refs, hd, group, wanted, merge):
-    sources = refs[: 4 if merge else 1]
+        placed = lax.dot_general(
+            order_ref[...], mixed.astype(BF16), (((0,), (0,)), ((), ())), preferred_element_type=F32
+        )
+        out_ref[:, at] = placed.astype(BF16)
+
+
+def project_kernel(columns, *refs, hd, group, pieces, merge):
+    sources = refs[: 5 if merge else 1]
     w_ref = refs[len(sources)]
-    outs = refs[len(sources) + 1 : len(sources) + 1 + wanted]
+    outs = refs[len(sources) + 1 : len(sources) + 1 + len(pieces)]
     held, sems = refs[-2:]
-    depth, width = held.shape[1:]
-    cuts = 2
-    piece = depth // cuts
+    width = held.shape[2]
     copies = []
-    for i in range(wanted):
-        for c in range(cuts):
-            at = pl.ds(c * piece, piece)
-            copy = pltpu.make_async_copy(
-                w_ref.at[at, pl.ds(pl.multiple_of(columns[i] * width, width), width)],
-                held.at[i, at],
-                sems.at[i * cuts + c],
-            )
-            copy.start()
-            copies.append(copy)
+    for i in range(sum(pieces)):
+        start = pl.multiple_of(columns[i] * width, width)
+        copies.append(pltpu.make_async_copy(w_ref.at[:, pl.ds(start, width)], held.at[i], sems.at[i]))
+        copies[-1].start()
     if merge:
-        attended = refs[len(sources) + 1 + wanted]
-        combined(sources, attended, hd, group)
+        attended = refs[len(sources) + 1 + len(pieces)]
+        combined(sources[0], sources[1:], attended, hd, group)
     else:
         attended = sources[0]
-    for i in range(wanted):
-        for c in range(cuts):
-            copies[i * cuts + c].wait()
-        outs[i][...] = jnp.dot(attended[...], held[i], preferred_element_type=F32).astype(BF16)
-
-
-def project(sources, weight, columns, width, hd):
+    i = 0
+    for out_ref, count in zip(outs, pieces):
+        for c in range(count):
+            copies[i].wait()
+            term = jnp.dot(attended[...], held[i], preferred_element_type=F32)
+            out_ref[:, c * width : (c + 1) * width] = term.astype(BF16)
+            i += 1
+
+
+def project(sources, weight, columns, pieces, width, hd):
     merge = len(sources) > 1
-    tokens = sources[0].shape[0]
+    tokens = sources[-1].shape[0]
     depth = weight.shape[0]
-    wanted = columns.shape[0]
+    total = sum(pieces)
     here = pl.BlockSpec(memory_space=pltpu.VMEM)
-    results = [jax.ShapeDtypeStruct((tokens, width), BF16)] * wanted
+    results = [jax.ShapeDtypeStruct((tokens, width * count), BF16) for count in pieces]
     if merge:
         results.append(jax.ShapeDtypeStruct((tokens, depth), BF16))
     return pl.pallas_call(
-        lambda *refs: project_kernel(*refs, hd=hd, group=depth // hd, wanted=wanted, merge=merge),
+        lambda *refs: project_kernel(*refs, hd=hd, group=depth // hd, pieces=pieces, merge=merge),
         out_shape=results,
         grid_spec=pltpu.PrefetchScalarGridSpec(
             num_scalar_prefetch=1,
@@ -265,8 +262,8 @@
             in_specs=[here] * len(sources) + [pl.BlockSpec(memory_space=pl.ANY)],
             out_specs=[here] * len(results),
             scratch_shapes=[
-                pltpu.VMEM((wanted, depth, width), BF16),
-                pltpu.SemaphoreType.DMA((2 * wanted,)),
+                pltpu.VMEM((total, depth, width), BF16),
+                pltpu.SemaphoreType.DMA((total,)),
             ],
         ),
         cost_estimate=pl.CostEstimate(
@@ -274,39 +271,57 @@
         ),
         compiler_params=pltpu.CompilerParams(vmem_limit_bytes=50 << 20),
         name="project",
-    )(columns, *sources, weight)
-
-
-def settle_kernel(gate_ref, order_ref, layer_ref, *refs):
-    terms, out_ref = refs[:-1], refs[-1]
-    total = None
-    for ref in terms:
-        part = lax.dot_general(
-            order_ref[...], ref[...], (((0,), (0,)), ((), ())), preferred_element_type=F32
-        )
-        total = part if total is None else total + part
-    out_ref[...] = (layer_ref[...].astype(F32) + gate_ref[0] * total).astype(BF16)
-
-
-def settle(gate, order, layer, terms):
+    )(jnp.stack(columns).astype(jnp.int32), *sources, weight)
+
+
+def add_kernel(*refs, count):
+    parts, send_ref, keep_ref = refs[:count], refs[-2], refs[-1]
+    total = parts[0][...].astype(F32)
+    for ref in parts[1:]:
+        total = total + ref[...].astype(F32)
+    cut = send_ref.shape[1]
+    send_ref[...] = total[:, :cut].astype(BF16)
+    keep_ref[...] = total[:, cut:]
+
+
+def add_up(parts, keep):
+    tokens, width = parts[0].shape
+    return pl.pallas_call(
+        lambda *refs: add_kernel(*refs, count=len(parts)),
+        out_shape=[
+            jax.ShapeDtypeStruct((tokens, width - keep), BF16),
+            jax.ShapeDtypeStruct((tokens, keep), F32),
+        ],
+        compiler_params=pltpu.CompilerParams(vmem_limit_bytes=24 << 20),
+        name="add_up",
+    )(*parts)
+
+
+def settle_kernel(gate_ref, layer_ref, *refs):
+    parts, out_ref = refs[:-1], refs[-1]
+    half = out_ref.shape[1] // 2
+    for at, some in ((slice(0, half), parts[:2]), (slice(half, None), parts[2:])):
+        total = some[0][...]
+        for ref in some[1:]:
+            total = total + ref[...].astype(F32)
+        out_ref[:, at] = (layer_ref[:, at].astype(F32) + gate_ref[0] * total).astype(BF16)
+
+
+def settle(gate, layer, parts):
     tokens, width = layer.shape
-    cuts = 4
-    step = width // cuts
-    tall = pl.BlockSpec((tokens, step), lambda g: (0, g))
+    cuts = 2
+    rows = tokens // cuts
+    wide = pl.BlockSpec((rows, width), lambda g: (g, 0))
+    part = pl.BlockSpec((rows, width // 2), lambda g: (g, 0))
     return pl.pallas_call(
         settle_kernel,
         out_shape=jax.ShapeDtypeStruct((tokens, width), BF16),
         grid=(cuts,),
-        in_specs=[
-            pl.BlockSpec(memory_space=pltpu.SMEM),
-            pl.BlockSpec((tokens, tokens), lambda g: (0, 0)),
-            tall,
-        ]
-        + [tall] * len(terms),
-        out_specs=tall,
+        in_specs=[pl.BlockSpec(memory_space=pltpu.SMEM), wide] + [part] * len(parts),
+        out_specs=wide,
         compiler_params=pltpu.CompilerParams(vmem_limit_bytes=24 << 20),
         name="settle",
-    )(gate, order, layer, *terms)
+    )(gate, layer, *parts)
 
 
 def shards(
@@ -335,26 +350,25 @@
     )
     rank = jnp.sum(ahead.astype(jnp.int32), axis=1)
     order = (rank[None, :] == place[:, None]).astype(BF16)
-    extra = jnp.pad(bounds.astype(BF16).T, ((0, 0), (0, hd - 2)))
-    payload = jnp.dot(
-        order, jnp.concatenate([queries, extra], axis=1), preferred_element_type=F32
-    ).astype(BF16)
-    payloads = {s: shifted(payload, "x", s) for s in (2, 1, 3)}
-    payloads[0] = payload
-    late = lax.optimization_barrier((key_t, value, payloads[1]))[:2]
-    beside = [shifted(v, "core", 1) for v in late]
-    diagonal = [shifted(v, "core", 1) for v in across]
-    tiles = (own, beside, across, diagonal)
-
     image = jnp.arange(tile_counts.shape[0])
     ends = jnp.sum(jnp.where(image[None, :] <= image[:, None], tile_counts[None, :], 0), axis=1)
     tile = jnp.arange(ny * nx * nc, dtype=jnp.int32)
     owner = jnp.sum((ends[None, :] <= tile[:, None]).astype(jnp.int32), axis=1)
     hits = (low[:, None] <= owner[None, :]) & (owner[None, :] < high[:, None])
-    which = jnp.arange(tokens // CHUNK, dtype=jnp.int32)
-    member = rank[:, None] // CHUNK == which[None, :]
-    live = jnp.any(member[:, :, None] & hits[:, None, :], axis=0).astype(jnp.int32)
-    everyone = lax.all_gather(live, "x")
+    same = (place[:, None] // CHUNK == rank[None, :] // CHUNK).astype(BF16)
+    live = jnp.dot(same, hits.astype(BF16), preferred_element_type=F32) > 0
+    flagged = jnp.pad(live.astype(F32), ((0, 0), (width + 16, hd - 16 - tile.shape[0])))
+    extra = jnp.pad(bounds.astype(BF16).T, ((0, 0), (0, hd - 2)))
+    payload = jnp.dot(
+        order, jnp.concatenate([queries, extra], axis=1), preferred_element_type=F32
+    )
+    payload = (payload + flagged).astype(BF16)
+    payloads = {s: shifted(payload, "x", s) for s in (2, 1, 3)}
+    payloads[0] = payload
+    late = lax.optimization_barrier((key_t, value, across[0]))[:2]
+    beside = [shifted(v, "core", 1) for v in late]
+    diagonal = [shifted(v, "core", 1) for v in across]
+    tiles = (own, beside, across, diagonal)
 
     def number(yy, cc):
         return (yy % ny * nx + x) * nc + cc % nc
@@ -365,10 +379,8 @@
 
     parts = {}
     for turns in GROUPS:
-        source = jnp.stack([(x - s) % nx for s in turns])
-        from_whom = (source[:, None] == jnp.arange(nx)[None, :]).astype(jnp.int32)
-        chosen = from_whom[:, :, None, None, None] * everyone[None, :, :, None, :]
-        wanted = jnp.sum(chosen * mine[None, None, None, :, :], axis=(1, 4))
+        flags = jnp.concatenate([payloads[s][::CHUNK, width + 16 : width + 32] for s in turns], axis=0)
+        wanted = jnp.sum(flags.astype(jnp.int32)[:, None, :] * mine[None, :, :], axis=2)
         items, count = work_list(wanted)
         got = attend(
             [payloads[s] for s in turns],
@@ -383,18 +395,26 @@
         for s, part in zip(turns, got):
             parts[s] = part if s == 0 else shifted(part, "x", nx - s)
 
-    sources = [parts[s] for s in (2, 1, 3, 0)]
-    terms = []
-    for some in ROUTES:
-        column = jnp.stack([(z + dz) % nz * nyh + (yh + dy) % nyh for dz, dy in some]).astype(jnp.int32)
-        got = project(sources, out_weight, column, width, hd)
-        if len(sources) > 1:
-            sources = [got[-1]]
-        for (dz, dy), term in zip(some, got):
-            if len(terms) > 4:
-                term = lax.optimization_barrier((term, terms[len(terms) - 5]))[0]
-            terms.append(term if (dz, dy) == (0, 0) else head_shifted(term, dz, dy))
-    return settle(jnp.tanh(attn_gate), order, layer_input, terms)
+    half = width // 2
+
+    def first(dz, dy):
+        return ((z + dz) % nz * nyh + (yh + dy) % nyh) * 2
+
+    sources = [order] + [parts[s] for s in (2, 1, 3, 0)]
+    over_y, attended = project(
+        sources, out_weight, [first(dz, 1) + 1 for dz in (1, 2, 3, 0)], (4,), half, hd
+    )
+    got_y = shifted(over_y, "yh", 1)
+    far = [first(dz, dy) for dz in (2, 1, 3) for dy in (1, 0)]
+    over_z = project([attended], out_weight, far, (2, 2, 2), half, hd)
+    got_z = [shifted(term, "z", dz) for dz, term in zip((2, 1, 3), over_z)]
+    near = [first(0, 1), first(0, 0)] + [first(dz, 0) + 1 for dz in (1, 2, 3, 0)]
+    own_z, own_y = project([attended], out_weight, near, (2, 4), half, hd)
+    late_z, kept_b = add_up([own_y, got_y], half)
+    ends_b = [shifted(late_z[:, i * half : (i + 1) * half], "z", i + 1) for i in (1, 0, 2)]
+    late_y, kept_a = add_up([own_z] + got_z, half)
+    end_a = shifted(late_y, "yh", 1)
+    return settle(jnp.tanh(attn_gate), layer_input, [kept_a, end_a, kept_b] + ends_b)
 
 
 def solution(mesh):

time: 153 us -> 140 us (0.915); the launches traced: 155 us -> 138 us
  Pallas kernels: 24.5 us -> 46.3 us
  blocking collectives: 21.1 us -> 0 us
  starting transfers between devices: 49 us -> 27.9 us
  waiting for transfers between devices: 48.4 us -> 51.8 us
    ppermute x12 -> x20, waiting for transfers between devices: 23.9 us -> 51.8 us  [shifted(): lax.ppermute(value, axis, [(s, (s + steps) % count) for s in range(count)])]
    ppermute x7 -> x0, waiting for transfers between devices: 24.6 us -> none  [head_shifted(): return lax.ppermute(value, HEAD, pairs)]
    pallas_call x1, Pallas kernels: 10.1 us -> 31.3 us  [attend(): pl.pallas_call(lambda *refs: attend_kernel(*refs, scale=1.0 / math.sqrt(h...]
    all_gather x1 -> x0, blocking collectives: 21.1 us -> none  [shards(): everyone = lax.all_gather(live, 'x')]
    ppermute x7 -> x0, starting transfers between devices: 15.8 us -> none  [head_shifted(): return lax.ppermute(value, HEAD, pairs)]
    ppermute x12 -> x20, starting transfers between devices: 33.2 us -> 27.9 us  [shifted(): lax.ppermute(value, axis, [(s, (s + steps) % count) for s in range(count)])]
    pallas_call x3, Pallas kernels: 11.5 us -> 13.6 us  [project(): pl.pallas_call(lambda *refs: project_kernel(*refs, hd=hd, group=depth //...]
    pallas_call x1, Pallas kernels: 2.9 us -> 0.91 us  [settle(): pl.pallas_call(settle_kernel, out_shape=jax.ShapeDtypeStruct((tokens, wid...]
  transfers between devices with their start and end apart: 19 -> 20, of which waited for: 9 -> 11; matrix products, arithmetic and copies ran while one was open for 2% -> 2% of each run, Pallas kernels for 5% -> 7%
where the time goes in v3:
time: 140 us; the launch traced here: 138 us
  waiting for transfers between devices  51.8 us (37%)
  Pallas kernels  46.3 us (33%)
  starting transfers between devices  27.9 us (20%)
  local copies, waits for them, and re-layouts  5.86 us (4%)
  other arithmetic  4.04 us (3%)
  matrix products  1.53 us (1%)
    ppermute x20, waiting for transfers between devices, shifted(): lax.ppermute(value, axis, [(s, (s + steps) % count) for s in range(count)])  51.8 us
    pallas_call x1, Pallas kernels, attend(): pl.pallas_call(lambda *refs: attend_kernel(*refs, scale=1.0 / math.sqrt(h...  31.3 us
    ppermute x20, starting transfers between devices, shifted(): lax.ppermute(value, axis, [(s, (s + steps) % count) for s in range(count)])  27.9 us
    pallas_call x3, Pallas kernels, project(): pl.pallas_call(lambda *refs: project_kernel(*refs, hd=hd, group=depth //...  13.6 us
    unnamed x8, local copies, waits for them, and re-layouts  3.15 us
  transfers between devices with their start and end apart: 20, of which 11 were waited for; matrix products, arithmetic and copies ran while one was open for 2% of the time, Pallas kernels for 7%

profile of v3, /device:TPU:8, one launch (start us, length us, event | category | flops | bytes accessed | tf_op | source)
XLA Modules:
  0.0 138.2 jit_solution(1987154088202714874)
XLA Ops:
  6.1 1.3 fusion.refs_6_
  7.4 3.1 %collective-permute-start = (bf16[192,1152]{1,0:T(8,128)(2,1)S(1)}, bf16[192,1152]{1,0:T(8,128)(2,1)S(1)}, u32[]{:S(2)}, u32[]{:S(2)}) collective-permute-start(bf16[192,1152]{1,0:T(8,128)(2,1)S(1)} %fusion.refs_6_), channel_id=1, source_target_pairs={{0,32},{16,48},{32,0},{48,16},{1,33},{17,49},{33,1},{49,17},{2,34}... | collective-permute-start | bytes 1327112 | tf_op jit(solution)/shard_map/ppermute | solution.py:23
  11.1 2.6 %collective-permute-start.2 = (bf16[192,1152]{1,0:T(8,128)(2,1)S(1)}, bf16[192,1152]{1,0:T(8,128)(2,1)S(1)}, u32[]{:S(2)}, u32[]{:S(2)}) collective-permute-start(bf16[192,1152]{1,0:T(8,128)(2,1)S(1)} %fusion.refs_6_), channel_id=1, source_target_pairs={{0,48},{16,0},{32,16},{48,32},{1,49},{17,1},{33,17},{49,33},{2,50}... | collective-permute-start | bytes 1327112 | tf_op jit(solution)/shard_map/ppermute | solution.py:23
  14.2 1.6 %collective-permute-start.7 = (bf16[1664,128]{1,0:T(8,128)(2,1)S(1)}, bf16[1664,128]{1,0:T(8,128)(2,1)}, u32[]{:S(2)}, u32[]{:S(2)}) collective-permute-start(bf16[1664,128]{1,0:T(8,128)(2,1)S(1)} %pad.15.refs_11_), channel_id=1, source_target_pairs={{0,64},{64,0},{1,65},{65,1},{2,66},{66,2},{3,67},{67,3},{4,68},{68... | collective-permute-start | bytes 1277960 | tf_op jit(solution)/shard_map/ppermute | solution.py:23
  16.2 10.3 %collective-permute-done.3.refs_9_ = bf16[128,1664]{1,0:T(8,128)(2,1)S(1)} collective-permute-done((bf16[128,1664]{1,0:T(8,128)(2,1)S(1)}, bf16[128,1664]{1,0:T(8,128)(2,1)S(1)}, u32[]{:S(2)}, u32[]{:S(2)}) %collective-permute-start.3) | collective-permute-done | bytes 426016 | tf_op jit(solution)/shard_map/ppermute | solution.py:23
  27.1 6.6 %collective-permute-done.7.refs_13_ = bf16[1664,128]{1,0:T(8,128)(2,1)} collective-permute-done((bf16[1664,128]{1,0:T(8,128)(2,1)S(1)}, bf16[1664,128]{1,0:T(8,128)(2,1)}, u32[]{:S(2)}, u32[]{:S(2)}) %collective-permute-start.7) | collective-permute-done | bytes 426016 | tf_op jit(solution)/shard_map/ppermute | solution.py:23
  37.7 31.3 %attend.1 = (bf16[192,1152]{1,0:T(8,128)(2,1)}, bf16[192,1152]{1,0:T(8,128)(2,1)}, bf16[192,1152]{1,0:T(8,128)(2,1)}, bf16[192,1152]{1,0:T(8,128)(2,1)S(1)}) custom-call(s32[99]{0:T(128)S(1)} %compare_select_fusion.1.refs_0_, s32[1]{0:T(128)} %bitcast.20.refs_1_, s32[4]{0:T(128)S(1)} %select_reduce_fusion.2.refs_2_, ...), custom_call_target="tpu_custom_call" | custom-call | flops 5234491392 | bytes 6553600 | tf_op jit(solution)/shard_map/attend/pallas_call | solution.py:147
  69.1 2.0 %collective-permute-start.11 = (bf16[192,1152]{1,0:T(8,128)(2,1)}, bf16[192,1152]{1,0:T(8,128)(2,1)S(1)}, u32[]{:S(2)}, u32[]{:S(2)}) collective-permute-start(bf16[192,1152]{1,0:T(8,128)(2,1)} %get-tuple-element.28), channel_id=1, source_target_pairs={{0,16},{16,32},{32,48},{48,0},{1,17},{17,33},{33,49},{49,1},{2,18}... | collective-permute-start | bytes 1327112 | tf_op jit(solution)/shard_map/ppermute | solution.py:23
  71.2 11.2 %collective-permute-done.10.refs_3_ = bf16[192,1152]{1,0:T(8,128)(2,1)S(1)} collective-permute-done((bf16[192,1152]{1,0:T(8,128)(2,1)}, bf16[192,1152]{1,0:T(8,128)(2,1)S(1)}, u32[]{:S(2)}, u32[]{:S(2)}) %collective-permute-start.10) | collective-permute-done | bytes 442400 | tf_op jit(solution)/shard_map/ppermute | solution.py:23
  82.4 8.7 %collective-permute-done.11.refs_4_ = bf16[192,1152]{1,0:T(8,128)(2,1)S(1)} collective-permute-done((bf16[192,1152]{1,0:T(8,128)(2,1)}, bf16[192,1152]{1,0:T(8,128)(2,1)S(1)}, u32[]{:S(2)}, u32[]{:S(2)}) %collective-permute-start.11) | collective-permute-done | bytes 442400 | tf_op jit(solution)/shard_map/ppermute | solution.py:23
  91.1 4.7 %project.3 = (bf16[192,2048]{1,0:T(8,128)(2,1)S(1)}, bf16[192,1024]{1,0:T(8,128)(2,1)S(1)}) custom-call(s32[4]{0:T(128)S(1)} %pad_add_fusion.refs_0_, bf16[192,192]{1,0:T(8,128)(2,1)S(1)} %fusion.8.refs_1_, bf16[192,1152]{1,0:T(8,128)(2,1)S(1)} %collective-permute-done.9.refs_2_, bf16[192,1152]{1,0:T(8,128)(2,1)S(1)} %collective-permute-done.10.refs_3_, ...), custom_call_target="tpu_custom_call" | custom-call | flops 393216 | bytes 393216 | tf_op jit(solution)/shard_map/project/pallas_call | solution.py:256
  95.8 2.6 %collective-permute-start.16 = (bf16[192,2048]{1,0:T(8,128)(2,1)S(1)}, bf16[192,2048]{1,0:T(8,128)(2,1)S(1)}, u32[]{:S(2)}, u32[]{:S(2)}) collective-permute-start(bf16[192,2048]{1,0:T(8,128)(2,1)S(1)} %get-tuple-element.38), channel_id=1, source_target_pairs={{0,1},{1,0},{2,3},{3,2},{4,5},{5,4},{6,7},{7,6},{8,9},{9,8},{10,11... | collective-permute-start | bytes 2359304 | tf_op jit(solution)/shard_map/ppermute | solution.py:23
  98.4 4.9 %project.5 = (bf16[192,1024]{1,0:T(8,128)(2,1)}, bf16[192,1024]{1,0:T(8,128)(2,1)}, bf16[192,1024]{1,0:T(8,128)(2,1)}) custom-call(s32[6]{0:T(128)S(1)} %stack.95.refs_0_, bf16[192,1024]{1,0:T(8,128)(2,1)S(1)} %get-tuple-element.30.refs_1_, bf16[1024,8192]{1,0:T(8,128)(2,1)} %refs_2_.3), custom_call_target="tpu_custom_call" | custom-call | flops 393216 | bytes 393216 | tf_op jit(solution)/shard_map/project/pallas_call | solution.py:256
  103.3 3.9 %collective-permute-start.12 = (bf16[192,1024]{1,0:T(8,128)(2,1)}, bf16[192,1024]{1,0:T(8,128)(2,1)S(1)}, u32[]{:S(2)}, u32[]{:S(2)}) collective-permute-start(bf16[192,1024]{1,0:T(8,128)(2,1)} %get-tuple-element.32), channel_id=1, source_target_pairs={{0,4},{2,6},{4,0},{6,2},{1,5},{3,7},{5,1},{7,3},{8,12},{10,14},{12... | collective-permute-start | bytes 1179656 | tf_op jit(solution)/shard_map/ppermute | solution.py:23
  108.2 2.2 %collective-permute-start.14 = (bf16[192,1024]{1,0:T(8,128)(2,1)}, bf16[192,1024]{1,0:T(8,128)(2,1)S(1)}, u32[]{:S(2)}, u32[]{:S(2)}) collective-permute-start(bf16[192,1024]{1,0:T(8,128)(2,1)} %get-tuple-element.34), channel_id=1, source_target_pairs={{0,6},{2,0},{4,2},{6,4},{1,7},{3,1},{5,3},{7,5},{8,14},{10,8},{12,... | collective-permute-start | bytes 1179656 | tf_op jit(solution)/shard_map/ppermute | solution.py:23
  110.5 4.1 %project.4 = (bf16[192,1024]{1,0:T(8,128)(2,1)S(1)}, bf16[192,2048]{1,0:T(8,128)(2,1)S(1)}) custom-call(s32[6]{0:T(128)S(1)} %stack.78.refs_0_, bf16[192,1024]{1,0:T(8,128)(2,1)S(1)} %get-tuple-element.30.refs_1_, bf16[1024,8192]{1,0:T(8,128)(2,1)} %refs_2_.3), custom_call_target="tpu_custom_call" | custom-call | flops 393216 | bytes 393216 | tf_op jit(solution)/shard_map/project/pallas_call | solution.py:256
  114.7 2.8 %collective-permute-done.12.refs_1_ = bf16[192,1024]{1,0:T(8,128)(2,1)S(1)} collective-permute-done((bf16[192,1024]{1,0:T(8,128)(2,1)}, bf16[192,1024]{1,0:T(8,128)(2,1)S(1)}, u32[]{:S(2)}, u32[]{:S(2)}) %collective-permute-start.12) | collective-permute-done | bytes 393248 | tf_op jit(solution)/shard_map/ppermute | solution.py:23
  117.5 5.4 %collective-permute-done.13.refs_2_ = bf16[192,1024]{1,0:T(8,128)(2,1)S(1)} collective-permute-done((bf16[192,1024]{1,0:T(8,128)(2,1)}, bf16[192,1024]{1,0:T(8,128)(2,1)S(1)}, u32[]{:S(2)}, u32[]{:S(2)}) %collective-permute-start.13) | collective-permute-done | bytes 393248 | tf_op jit(solution)/shard_map/ppermute | solution.py:23
  123.9 1.3 collective-permute-start.15
  125.4 2.1 %collective-permute-start.17 = (bf16[192,512]{1,0:T(8,128)(2,1)S(1)}, bf16[192,512]{1,0:T(8,128)(2,1)S(1)}, u32[]{:S(2)}, u32[]{:S(2)}) collective-permute-start(bf16[192,512]{1,0:T(8,128)(2,1)S(1)} %get-tuple-element.45), channel_id=1, source_target_pairs={{0,4},{2,6},{4,0},{6,2},{1,5},{3,7},{5,1},{7,3},{8,12},{10,14},{12... | collective-permute-start | bytes 589832 | tf_op jit(solution)/shard_map/ppermute | solution.py:23
  127.6 1.5 %collective-permute-start.18 = (bf16[192,512]{1,0:T(8,128)(2,1)S(1)}, bf16[192,512]{1,0:T(8,128)(2,1)S(1)}, u32[]{:S(2)}, u32[]{:S(2)}) collective-permute-start(bf16[192,512]{1,0:T(8,128)(2,1)S(1)} %get-tuple-element.44), channel_id=1, source_target_pairs={{0,2},{2,4},{4,6},{6,0},{1,3},{3,5},{5,7},{7,1},{8,10},{10,12},{12... | collective-permute-start | bytes 589832 | tf_op jit(solution)/shard_map/ppermute | solution.py:23
  129.0 1.8 %collective-permute-start.19 = (bf16[192,512]{1,0:T(8,128)(2,1)S(1)}, bf16[192,512]{1,0:T(8,128)(2,1)S(1)}, u32[]{:S(2)}, u32[]{:S(2)}) collective-permute-start(bf16[192,512]{1,0:T(8,128)(2,1)S(1)} %get-tuple-element.43), channel_id=1, source_target_pairs={{0,6},{2,0},{4,2},{6,4},{1,7},{3,1},{5,3},{7,5},{8,14},{10,8},{12,... | collective-permute-start | bytes 589832 | tf_op jit(solution)/shard_map/ppermute | solution.py:23
  131.5 3.1 %collective-permute-done.17.refs_3_ = bf16[192,512]{1,0:T(8,128)(2,1)S(1)} collective-permute-done((bf16[192,512]{1,0:T(8,128)(2,1)S(1)}, bf16[192,512]{1,0:T(8,128)(2,1)S(1)}, u32[]{:S(2)}, u32[]{:S(2)}) %collective-permute-start.17) | collective-permute-done | bytes 196640 | tf_op jit(solution)/shard_map/ppermute | solution.py:23
  134.6 2.1 %collective-permute-done.18.refs_4_ = bf16[192,512]{1,0:T(8,128)(2,1)S(1)} collective-permute-done((bf16[192,512]{1,0:T(8,128)(2,1)S(1)}, bf16[192,512]{1,0:T(8,128)(2,1)S(1)}, u32[]{:S(2)}, u32[]{:S(2)}) %collective-permute-start.18) | collective-permute-done | bytes 196640 | tf_op jit(solution)/shard_map/ppermute | solution.py:23
  (66 shorter events, 16.3 us)
Async XLA Ops:
  7.4 19.1 %collective-permute-start = (bf16[192,1152]{1,0:T(8,128)(2,1)S(1)}, bf16[192,1152]{1,0:T(8,128)(2,1)S(1)}, u32[]{:S(2)}, u32[]{:S(2)}) collective-permute-start(bf16[192,1152]{1,0:T(8,128)(2,1)S(1)} %fusion.refs_6_), channel_id=1, source_target_pairs={{0,32},{16,48},{32,0},{48,16},{1,33},{17,49},{33,1},{49,17},{2,34}... | collective-permute-start | bytes 1327112 | tf_op jit(solution)/shard_map/ppermute | solution.py:23
  10.5 24.0 %collective-permute-start.1 = (bf16[192,1152]{1,0:T(8,128)(2,1)S(1)}, bf16[192,1152]{1,0:T(8,128)(2,1)S(1)}, u32[]{:S(2)}, u32[]{:S(2)}) collective-permute-start(bf16[192,1152]{1,0:T(8,128)(2,1)S(1)} %fusion.refs_6_), channel_id=1, source_target_pairs={{0,16},{16,32},{32,48},{48,0},{1,17},{17,33},{33,49},{49,1},{2,18}... | collective-permute-start | bytes 1327112 | tf_op jit(solution)/shard_map/ppermute | solution.py:23
  11.1 24.0 %collective-permute-start.2 = (bf16[192,1152]{1,0:T(8,128)(2,1)S(1)}, bf16[192,1152]{1,0:T(8,128)(2,1)S(1)}, u32[]{:S(2)}, u32[]{:S(2)}) collective-permute-start(bf16[192,1152]{1,0:T(8,128)(2,1)S(1)} %fusion.refs_6_), channel_id=1, source_target_pairs={{0,48},{16,0},{32,16},{48,32},{1,49},{17,1},{33,17},{49,33},{2,50}... | collective-permute-start | bytes 1327112 | tf_op jit(solution)/shard_map/ppermute | solution.py:23
  13.7 12.8 %collective-permute-start.3 = (bf16[128,1664]{1,0:T(8,128)(2,1)S(1)}, bf16[128,1664]{1,0:T(8,128)(2,1)S(1)}, u32[]{:S(2)}, u32[]{:S(2)}) collective-permute-start(bf16[128,1664]{1,0:T(8,128)(2,1)S(1)} %maximum_bitcast_fusion.refs_7_), channel_id=1, source_target_pairs={{0,64},{64,0},{1,65},{65,1},{2,66},{66,2},{3,67},{67,3},{4,68},{68... | collective-permute-start | bytes 1277960 | tf_op jit(solution)/shard_map/ppermute | solution.py:23
  14.2 19.5 %collective-permute-start.7 = (bf16[1664,128]{1,0:T(8,128)(2,1)S(1)}, bf16[1664,128]{1,0:T(8,128)(2,1)}, u32[]{:S(2)}, u32[]{:S(2)}) collective-permute-start(bf16[1664,128]{1,0:T(8,128)(2,1)S(1)} %pad.15.refs_11_), channel_id=1, source_target_pairs={{0,64},{64,0},{1,65},{65,1},{2,66},{66,2},{3,67},{67,3},{4,68},{68... | collective-permute-start | bytes 1277960 | tf_op jit(solution)/shard_map/ppermute | solution.py:23
  26.5 10.0 %collective-permute-start.4 = (bf16[128,1664]{1,0:T(8,128)(2,1)S(1)}, bf16[128,1664]{1,0:T(8,128)(2,1)}, u32[]{:S(2)}, u32[]{:S(2)}) collective-permute-start(bf16[128,1664]{1,0:T(8,128)(2,1)S(1)} %maximum_bitcast_fusion.refs_7_), channel_id=1, source_target_pairs={{0,8},{8,0},{1,9},{9,1},{2,10},{10,2},{3,11},{11,3},{4,12},{12,4},... | collective-permute-start | bytes 1277960 | tf_op jit(solution)/shard_map/ppermute | solution.py:23
  26.5 10.0 %collective-permute-start.6 = (bf16[1664,128]{1,0:T(8,128)(2,1)S(1)}, bf16[1664,128]{1,0:T(8,128)(2,1)}, u32[]{:S(2)}, u32[]{:S(2)}) collective-permute-start(bf16[1664,128]{1,0:T(8,128)(2,1)S(1)} %pad.15.refs_11_), channel_id=1, source_target_pairs={{0,8},{8,0},{1,9},{9,1},{2,10},{10,2},{3,11},{11,3},{4,12},{12,4},... | collective-permute-start | bytes 1277960 | tf_op jit(solution)/shard_map/ppermute | solution.py:23
  33.7 2.8 %collective-permute-start.5 = (bf16[128,1664]{1,0:T(8,128)(2,1)S(1)}, bf16[128,1664]{1,0:T(8,128)(2,1)}, u32[]{:S(2)}, u32[]{:S(2)}) collective-permute-start(bf16[128,1664]{1,0:T(8,128)(2,1)S(1)} %collective-permute-done.3.refs_9_), channel_id=1, source_target_pairs={{0,8},{8,0},{1,9},{9,1},{2,10},{10,2},{3,11},{11,3},{4,12},{12,4},... | collective-permute-start | bytes 1277960 | tf_op jit(solution)/shard_map/ppermute | solution.py:23
  33.7 0.8 copy-start.1
  34.4 2.2 %collective-permute-start.8 = (bf16[1664,128]{1,0:T(8,128)(2,1)}, bf16[1664,128]{1,0:T(8,128)(2,1)}, u32[]{:S(2)}, u32[]{:S(2)}) collective-permute-start(bf16[1664,128]{1,0:T(8,128)(2,1)} %collective-permute-done.7.refs_13_), channel_id=1, source_target_pairs={{0,8},{8,0},{1,9},{9,1},{2,10},{10,2},{3,11},{11,3},{4,12},{12,4},... | collective-permute-start | bytes 1277960 | tf_op jit(solution)/shard_map/ppermute | solution.py:23
  36.7 1.0 copy-start.2
  69.0 13.4 %collective-permute-start.10 = (bf16[192,1152]{1,0:T(8,128)(2,1)}, bf16[192,1152]{1,0:T(8,128)(2,1)S(1)}, u32[]{:S(2)}, u32[]{:S(2)}) collective-permute-start(bf16[192,1152]{1,0:T(8,128)(2,1)} %get-tuple-element.27), channel_id=1, source_target_pairs={{0,48},{16,0},{32,16},{48,32},{1,49},{17,1},{33,17},{49,33},{2,50}... | collective-permute-start | bytes 1327112 | tf_op jit(solution)/shard_map/ppermute | solution.py:23
  69.1 22.0 %collective-permute-start.11 = (bf16[192,1152]{1,0:T(8,128)(2,1)}, bf16[192,1152]{1,0:T(8,128)(2,1)S(1)}, u32[]{:S(2)}, u32[]{:S(2)}) collective-permute-start(bf16[192,1152]{1,0:T(8,128)(2,1)} %get-tuple-element.28), channel_id=1, source_target_pairs={{0,16},{16,32},{32,48},{48,0},{1,17},{17,33},{33,49},{49,1},{2,18}... | collective-permute-start | bytes 1327112 | tf_op jit(solution)/shard_map/ppermute | solution.py:23
  71.1 20.0 %collective-permute-start.9 = (bf16[192,1152]{1,0:T(8,128)(2,1)}, bf16[192,1152]{1,0:T(8,128)(2,1)S(1)}, u32[]{:S(2)}, u32[]{:S(2)}) collective-permute-start(bf16[192,1152]{1,0:T(8,128)(2,1)} %get-tuple-element.26), channel_id=1, source_target_pairs={{0,32},{16,48},{32,0},{48,16},{1,33},{17,49},{33,1},{49,17},{2,34}... | collective-permute-start | bytes 1327112 | tf_op jit(solution)/shard_map/ppermute | solution.py:23
  95.8 29.4 %collective-permute-start.16 = (bf16[192,2048]{1,0:T(8,128)(2,1)S(1)}, bf16[192,2048]{1,0:T(8,128)(2,1)S(1)}, u32[]{:S(2)}, u32[]{:S(2)}) collective-permute-start(bf16[192,2048]{1,0:T(8,128)(2,1)S(1)} %get-tuple-element.38), channel_id=1, source_target_pairs={{0,1},{1,0},{2,3},{3,2},{4,5},{5,4},{6,7},{7,6},{8,9},{9,8},{10,11... | collective-permute-start | bytes 2359304 | tf_op jit(solution)/shard_map/ppermute | solution.py:23
  98.4 38.9 %copy-start = (bf16[192,1024]{1,0:T(8,128)(2,1)S(1)}, bf16[192,1024]{1,0:T(8,128)(2,1)}, u32[]{:S(2)}) copy-start(bf16[192,1024]{1,0:T(8,128)(2,1)} %layer_ref.1) | copy-start | bytes 1179652
  103.3 14.2 %collective-permute-start.12 = (bf16[192,1024]{1,0:T(8,128)(2,1)}, bf16[192,1024]{1,0:T(8,128)(2,1)S(1)}, u32[]{:S(2)}, u32[]{:S(2)}) collective-permute-start(bf16[192,1024]{1,0:T(8,128)(2,1)} %get-tuple-element.32), channel_id=1, source_target_pairs={{0,4},{2,6},{4,0},{6,2},{1,5},{3,7},{5,1},{7,3},{8,12},{10,14},{12... | collective-permute-start | bytes 1179656 | tf_op jit(solution)/shard_map/ppermute | solution.py:23
  107.2 15.7 %collective-permute-start.13 = (bf16[192,1024]{1,0:T(8,128)(2,1)}, bf16[192,1024]{1,0:T(8,128)(2,1)S(1)}, u32[]{:S(2)}, u32[]{:S(2)}) collective-permute-start(bf16[192,1024]{1,0:T(8,128)(2,1)} %get-tuple-element.33), channel_id=1, source_target_pairs={{0,2},{2,4},{4,6},{6,0},{1,3},{3,5},{5,7},{7,1},{8,10},{10,12},{12... | collective-permute-start | bytes 1179656 | tf_op jit(solution)/shard_map/ppermute | solution.py:23
  108.2 15.4 %collective-permute-start.14 = (bf16[192,1024]{1,0:T(8,128)(2,1)}, bf16[192,1024]{1,0:T(8,128)(2,1)S(1)}, u32[]{:S(2)}, u32[]{:S(2)}) collective-permute-start(bf16[192,1024]{1,0:T(8,128)(2,1)} %get-tuple-element.34), channel_id=1, source_target_pairs={{0,6},{2,0},{4,2},{6,4},{1,7},{3,1},{5,3},{7,5},{8,14},{10,8},{12,... | collective-permute-start | bytes 1179656 | tf_op jit(solution)/shard_map/ppermute | solution.py:23
  123.9 7.6 %collective-permute-start.15 = (bf16[192,512]{1,0:T(8,128)(2,1)S(1)}, bf16[192,512]{1,0:T(8,128)(2,1)S(1)}, u32[]{:S(2)}, u32[]{:S(2)}) collective-permute-start(bf16[192,512]{1,0:T(8,128)(2,1)S(1)} %get-tuple-element.36), channel_id=1, source_target_pairs={{0,1},{1,0},{2,3},{3,2},{4,5},{5,4},{6,7},{7,6},{8,9},{9,8},{10,11... | collective-permute-start | bytes 589832 | tf_op jit(solution)/shard_map/ppermute | solution.py:23
  125.4 9.1 %collective-permute-start.17 = (bf16[192,512]{1,0:T(8,128)(2,1)S(1)}, bf16[192,512]{1,0:T(8,128)(2,1)S(1)}, u32[]{:S(2)}, u32[]{:S(2)}) collective-permute-start(bf16[192,512]{1,0:T(8,128)(2,1)S(1)} %get-tuple-element.45), channel_id=1, source_target_pairs={{0,4},{2,6},{4,0},{6,2},{1,5},{3,7},{5,1},{7,3},{8,12},{10,14},{12... | collective-permute-start | bytes 589832 | tf_op jit(solution)/shard_map/ppermute | solution.py:23
  127.6 9.1 %collective-permute-start.18 = (bf16[192,512]{1,0:T(8,128)(2,1)S(1)}, bf16[192,512]{1,0:T(8,128)(2,1)S(1)}, u32[]{:S(2)}, u32[]{:S(2)}) collective-permute-start(bf16[192,512]{1,0:T(8,128)(2,1)S(1)} %get-tuple-element.44), channel_id=1, source_target_pairs={{0,2},{2,4},{4,6},{6,0},{1,3},{3,5},{5,7},{7,1},{8,10},{10,12},{12... | collective-permute-start | bytes 589832 | tf_op jit(solution)/shard_map/ppermute | solution.py:23
  129.0 8.3 %collective-permute-start.19 = (bf16[192,512]{1,0:T(8,128)(2,1)S(1)}, bf16[192,512]{1,0:T(8,128)(2,1)S(1)}, u32[]{:S(2)}, u32[]{:S(2)}) collective-permute-start(bf16[192,512]{1,0:T(8,128)(2,1)S(1)} %get-tuple-element.43), channel_id=1, source_target_pairs={{0,6},{2,0},{4,2},{6,4},{1,7},{3,1},{5,3},{7,5},{8,14},{10,8},{12,... | collective-permute-start | bytes 589832 | tf_op jit(solution)/shard_map/ppermute | solution.py:23

commit v4 on v3

--- a/solution.py
+++ b/solution.py
@@ -34,11 +34,10 @@
 
 def attend_kernel(items, count, images, *refs, scale, hd, group, blocks, keys, padded):
     q_refs = refs[:blocks]
-    key_refs = refs[blocks : blocks + 4]
-    value_refs = refs[blocks + 4 : blocks + 8]
-    out_refs = refs[blocks + 8 : 2 * blocks + 8]
-    q_all, key_all, value_all, first_s, second_s, first_b, second_b, top_ref, acc_ref, sems = refs[
-        2 * blocks + 8 :
+    tile_refs = refs[blocks : blocks + 4]
+    out_refs = refs[blocks + 4 : 2 * blocks + 4]
+    q_all, key_all, value_in, value_all, first_s, second_s, first_b, second_b, top_ref, acc_ref, sems = refs[
+        2 * blocks + 4 :
     ]
     tokens = out_refs[0].shape[0]
     rows = CHUNK * group
@@ -46,11 +45,11 @@
     factor = scale * math.log2(math.e)
     copies = []
     for j in range(4):
-        copies.append(pltpu.make_async_copy(key_refs[j], key_all.at[j], sems.at[2 * j]))
         copies.append(
-            pltpu.make_async_copy(
-                value_refs[j], value_all.at[j, :, pl.ds(0, hd)], sems.at[2 * j + 1]
-            )
+            pltpu.make_async_copy(tile_refs[j].at[pl.ds(0, hd)], key_all.at[j], sems.at[2 * j])
+        )
+        copies.append(
+            pltpu.make_async_copy(tile_refs[j].at[pl.ds(hd, hd)], value_in.at[j], sems.at[2 * j + 1])
         )
     for i in range(blocks):
         copies.append(
@@ -68,6 +67,9 @@
     acc_ref[...] = jnp.zeros(acc_ref.shape, F32)
     for copy in copies:
         copy.wait()
+    for j in range(4):
+        for k in range(0, padded, hd):
+            value_all[j, k : k + hd, :hd] = value_in[j, :, k : k + hd]
 
     def where_is(i):
         item = items[i]
@@ -135,10 +137,10 @@
         out_ref[near, width:] = pieces.astype(BF16)
 
 
-def attend(payloads, items, count, images, keys_t, values, keys, tokens):
+def attend(payloads, items, count, images, tiles, keys, tokens, hd):
     blocks = len(payloads)
     wide = payloads[0].shape[1]
-    hd, padded = keys_t[0].shape
+    padded = tiles[0].shape[1]
     width = wide - hd
     group = width // hd
     rows = CHUNK * group
@@ -158,10 +160,11 @@
         grid_spec=pltpu.PrefetchScalarGridSpec(
             num_scalar_prefetch=3,
             grid=(),
-            in_specs=[apart] * (blocks + 8),
+            in_specs=[apart] * (blocks + 4),
             out_specs=[here] * blocks,
             scratch_shapes=[
                 pltpu.VMEM((blocks * tokens, wide), BF16),
+                pltpu.VMEM((4, hd, padded), BF16),
                 pltpu.VMEM((4, hd, padded), BF16),
                 pltpu.VMEM((4, padded, 2 * hd), BF16),
                 pltpu.VMEM((rows, padded), F32),
@@ -180,7 +183,49 @@
             transcendentals=blocks * tokens * group * padded * 2,
         ),
         name="attend",
-    )(items, count, images, *payloads, *keys_t, *values)
+    )(items, count, images, *payloads, *tiles)
+
+
+def prepare_kernel(key_ref, value_ref, q_ref, order_ref, extra_ref, tile_ref, payload_ref):
+    keys, hd = key_ref.shape
+    padded = tile_ref.shape[1]
+    width = q_ref.shape[1]
+    whole = keys // hd * hd
+    mid = keys // 16 * 16
+    for k in range(0, whole, hd):
+        block = key_ref[k : k + hd].astype(F32)
+        tile_ref[:hd, k : k + hd] = block.T.astype(BF16)
+        tile_ref[hd:, k : k + hd] = value_ref[k : k + hd]
+    first = lax.broadcasted_iota(jnp.int32, (padded - mid, hd), 0) == 0
+    last_key = jnp.where(first, key_ref[mid:keys].astype(F32), key_ref[0:1].astype(F32))
+    last_value = jnp.where(first, value_ref[mid:keys].astype(F32), 0.0)
+    block = jnp.concatenate([key_ref[whole:mid].astype(F32), last_key], axis=0)
+    tile_ref[:hd, whole:] = block.T.astype(BF16)
+    block = jnp.concatenate([value_ref[whole:mid].astype(F32), last_value], axis=0)
+    tile_ref[hd:, whole:] = block.astype(BF16)
+    order = order_ref[...]
+    step = 2 * hd
+    for k in range(0, width, step):
+        part = jnp.dot(order, q_ref[:, k : k + step], preferred_element_type=F32)
+        payload_ref[:, k : k + step] = part.astype(BF16)
+    payload_ref[:, width:] = extra_ref[...].astype(BF16)
+
+
+def prepare(keys, values, queries, order, extra, padded):
+    hd = keys.shape[1]
+    tokens, width = queries.shape
+    here = pl.BlockSpec(memory_space=pltpu.VMEM)
+    return pl.pallas_call(
+        prepare_kernel,
+        out_shape=[
+            jax.ShapeDtypeStruct((2 * hd, padded), BF16),
+            jax.ShapeDtypeStruct((tokens, width + hd), BF16),
+        ],
+        in_specs=[here] * 5,
+        out_specs=[here] * 2,
+        compiler_params=pltpu.CompilerParams(vmem_limit_bytes=24 << 20),
+        name="prepare",
+    )(keys, values, queries, order, extra)
 
 
 def work_list(wanted):
@@ -335,14 +380,7 @@
     nz, nyh = (lax.axis_size(n) for n in HEAD)
 
     padded = -(-keys // 128) * 128
-    spare = jnp.broadcast_to(image_keys[:1], (padded - keys, hd))
-    key_t = jnp.concatenate([image_keys, spare], axis=0).T
-    value = jnp.pad(image_values, ((0, padded - keys), (0, 0)))
-    own = (key_t, value)
-    across = [shifted(v, "y", 1) for v in own]
-
-    bounds, _, _ = lax.optimization_barrier((image_range, key_t, value))
-    low, high = bounds[0], bounds[1]
+    low, high = image_range[0], image_range[1]
     grade = jnp.where(low < high, low * 16 + high, 1 << 10)
     place = jnp.arange(tokens, dtype=jnp.int32)
     ahead = (grade[None, :] < grade[:, None]) | (
@@ -357,17 +395,20 @@
     hits = (low[:, None] <= owner[None, :]) & (owner[None, :] < high[:, None])
     same = (place[:, None] // CHUNK == rank[None, :] // CHUNK).astype(BF16)
     live = jnp.dot(same, hits.astype(BF16), preferred_element_type=F32) > 0
-    flagged = jnp.pad(live.astype(F32), ((0, 0), (width + 16, hd - 16 - tile.shape[0])))
-    extra = jnp.pad(bounds.astype(BF16).T, ((0, 0), (0, hd - 2)))
-    payload = jnp.dot(
-        order, jnp.concatenate([queries, extra], axis=1), preferred_element_type=F32
+    span = jnp.dot(order, image_range.astype(BF16).T, preferred_element_type=F32)
+    extra = jnp.concatenate(
+        [
+            jnp.pad(span, ((0, 0), (0, 14))),
+            jnp.pad(live.astype(F32), ((0, 0), (0, hd - 16 - tile.shape[0]))),
+        ],
+        axis=1,
     )
-    payload = (payload + flagged).astype(BF16)
+    own, payload = prepare(image_keys, image_values, queries, order, extra, padded)
+    across = shifted(own, "y", 1)
     payloads = {s: shifted(payload, "x", s) for s in (2, 1, 3)}
     payloads[0] = payload
-    late = lax.optimization_barrier((key_t, value, across[0]))[:2]
-    beside = [shifted(v, "core", 1) for v in late]
-    diagonal = [shifted(v, "core", 1) for v in across]
+    beside = shifted(own, "core", 1)
+    diagonal = shifted(across, "core", 1)
     tiles = (own, beside, across, diagonal)
 
     def number(yy, cc):
@@ -387,10 +428,10 @@
             items,
             count,
             images,
-            [t[0] for t in tiles],
-            [t[1] for t in tiles],
+            tiles,
             keys,
             tokens,
+            hd,
         )
         for s, part in zip(turns, got):
             parts[s] = part if s == 0 else shifted(part, "x", nx - s)
@@ -401,18 +442,18 @@
         return ((z + dz) % nz * nyh + (yh + dy) % nyh) * 2
 
     sources = [order] + [parts[s] for s in (2, 1, 3, 0)]
-    over_y, attended = project(
-        sources, out_weight, [first(dz, 1) + 1 for dz in (1, 2, 3, 0)], (4,), half, hd
-    )
+    far = [first(dz, dy) for dz in (2, 1) for dy in (1, 0)]
+    *over_z, attended = project(sources, out_weight, far, (2, 2), half, hd)
+    got_z = [shifted(term, "z", dz) for dz, term in zip((2, 1), over_z)]
+    mixed = [first(3, 1), first(3, 0)] + [first(dz, 1) + 1 for dz in (1, 2, 3, 0)]
+    last_z, over_y = project([attended], out_weight, mixed, (2, 4), half, hd)
     got_y = shifted(over_y, "yh", 1)
-    far = [first(dz, dy) for dz in (2, 1, 3) for dy in (1, 0)]
-    over_z = project([attended], out_weight, far, (2, 2, 2), half, hd)
-    got_z = [shifted(term, "z", dz) for dz, term in zip((2, 1, 3), over_z)]
+    got_z.append(shifted(last_z, "z", 3))
     near = [first(0, 1), first(0, 0)] + [first(dz, 0) + 1 for dz in (1, 2, 3, 0)]
     own_z, own_y = project([attended], out_weight, near, (2, 4), half, hd)
     late_z, kept_b = add_up([own_y, got_y], half)
     ends_b = [shifted(late_z[:, i * half : (i + 1) * half], "z", i + 1) for i in (1, 0, 2)]
-    late_y, kept_a = add_up([own_z] + got_z, half)
+    late_y, kept_a = add_up([own_z] + got_z[::-1], half)
     end_a = shifted(late_y, "yh", 1)
     return settle(jnp.tanh(attn_gate), layer_input, [kept_a, end_a, kept_b] + ends_b)
 

time: 140 us -> 136 us (0.971); the launches traced: 138 us -> 137 us
  Pallas kernels: 46.3 us -> 36.7 us
  waiting for transfers between devices: 51.8 us -> 59.7 us
  starting transfers between devices: 27.9 us -> 31.5 us
  local copies, waits for them, and re-layouts: 5.86 us -> 3.9 us
    pallas_call x1, Pallas kernels: 31.3 us -> 21.1 us  [attend(): pl.pallas_call(lambda *refs: attend_kernel(*refs, scale=1.0 / math.sqrt(h...]
    ppermute x20 -> x17, waiting for transfers between devices: 51.8 us -> 59.7 us  [shifted(): lax.ppermute(value, axis, [(s, (s + steps) % count) for s in range(count)])]
    ppermute x20 -> x17, starting transfers between devices: 27.9 us -> 31.5 us  [shifted(): lax.ppermute(value, axis, [(s, (s + steps) % count) for s in range(count)])]
  transfers between devices with their start and end apart: 20 -> 17, of which waited for: 11 -> 11; matrix products, arithmetic and copies ran while one was open for 2% -> 2% of each run, Pallas kernels for 7% -> 3%
where the time goes in v4:
time: 136 us; the launch traced here: 137 us
  waiting for transfers between devices  59.7 us (44%)
  Pallas kernels  36.7 us (27%)
  starting transfers between devices  31.5 us (23%)
  local copies, waits for them, and re-layouts  3.9 us (3%)
  other arithmetic  3.37 us (2%)
    ppermute x17, waiting for transfers between devices, shifted(): lax.ppermute(value, axis, [(s, (s + steps) % count) for s in range(count)])  59.7 us
    ppermute x17, starting transfers between devices, shifted(): lax.ppermute(value, axis, [(s, (s + steps) % count) for s in range(count)])  31.5 us
    pallas_call x1, Pallas kernels, attend(): pl.pallas_call(lambda *refs: attend_kernel(*refs, scale=1.0 / math.sqrt(h...  21.1 us
    pallas_call x3, Pallas kernels, project(): pl.pallas_call(lambda *refs: project_kernel(*refs, hd=hd, group=depth //...  14 us
    unnamed x8, local copies, waits for them, and re-layouts  3 us
  transfers between devices with their start and end apart: 17, of which 11 were waited for; matrix products, arithmetic and copies ran while one was open for 2% of the time, Pallas kernels for 3%

profile of v4, /device:TPU:8, one launch (start us, length us, event | category | flops | bytes accessed | tf_op | source)
XLA Modules:
  0.0 137.0 jit_solution(648275176068751942)
XLA Ops:
  4.1 1.0 copy-done.1
  6.8 3.1 %collective-permute-start = (bf16[192,1152]{1,0:T(8,128)(2,1)S(1)}, bf16[192,1152]{1,0:T(8,128)(2,1)S(1)}, u32[]{:S(2)}, u32[]{:S(2)}) collective-permute-start(bf16[192,1152]{1,0:T(8,128)(2,1)S(1)} %get-tuple-element.22.refs_6_), channel_id=1, source_target_pairs={{0,32},{16,48},{32,0},{48,16},{1,33},{17,49},{33,1},{49,17},{2,34}... | collective-permute-start | bytes 1327112 | tf_op jit(solution)/shard_map/ppermute | solution.py:23
  10.5 2.6 %collective-permute-start.2 = (bf16[192,1152]{1,0:T(8,128)(2,1)S(1)}, bf16[192,1152]{1,0:T(8,128)(2,1)S(1)}, u32[]{:S(2)}, u32[]{:S(2)}) collective-permute-start(bf16[192,1152]{1,0:T(8,128)(2,1)S(1)} %get-tuple-element.22.refs_6_), channel_id=1, source_target_pairs={{0,48},{16,0},{32,16},{48,32},{1,49},{17,1},{33,17},{49,33},{2,50}... | collective-permute-start | bytes 1327112 | tf_op jit(solution)/shard_map/ppermute | solution.py:23
  13.6 7.9 %collective-permute-done.refs_3_ = bf16[192,1152]{1,0:T(8,128)(2,1)S(1)} collective-permute-done((bf16[192,1152]{1,0:T(8,128)(2,1)S(1)}, bf16[192,1152]{1,0:T(8,128)(2,1)S(1)}, u32[]{:S(2)}, u32[]{:S(2)}) %collective-permute-start) | collective-permute-done | bytes 442400 | tf_op jit(solution)/shard_map/ppermute | solution.py:23
  21.6 7.9 %collective-permute-done.1.refs_4_ = bf16[192,1152]{1,0:T(8,128)(2,1)S(1)} collective-permute-done((bf16[192,1152]{1,0:T(8,128)(2,1)S(1)}, bf16[192,1152]{1,0:T(8,128)(2,1)S(1)}, u32[]{:S(2)}, u32[]{:S(2)}) %collective-permute-start.1) | collective-permute-done | bytes 442400 | tf_op jit(solution)/shard_map/ppermute | solution.py:23
  31.1 1.4 %collective-permute-done.5.refs_10_ = bf16[256,1664]{1,0:T(8,128)(2,1)} collective-permute-done((bf16[256,1664]{1,0:T(8,128)(2,1)}, bf16[256,1664]{1,0:T(8,128)(2,1)}, u32[]{:S(2)}, u32[]{:S(2)}) %collective-permute-start.5) | collective-permute-done | bytes 852000 | tf_op jit(solution)/shard_map/ppermute | solution.py:23
  32.5 21.1 %attend.1 = (bf16[192,1152]{1,0:T(8,128)(2,1)}, bf16[192,1152]{1,0:T(8,128)(2,1)}, bf16[192,1152]{1,0:T(8,128)(2,1)}, bf16[192,1152]{1,0:T(8,128)(2,1)S(1)}) custom-call(s32[99]{0:T(128)S(1)} %compare_select_fusion.1.refs_0_, s32[1]{0:T(128)} %bitcast.17.refs_1_, s32[4]{0:T(128)S(1)} %select_reduce_fusion.2.refs_2_, ...), custom_call_target="tpu_custom_call" | custom-call | flops 5234491392 | bytes 6553600 | tf_op jit(solution)/shard_map/attend/pallas_call | solution.py:149
  53.6 5.9 %collective-permute-start.6 = (bf16[192,1152]{1,0:T(8,128)(2,1)}, bf16[192,1152]{1,0:T(8,128)(2,1)S(1)}, u32[]{:S(2)}, u32[]{:S(2)}) collective-permute-start(bf16[192,1152]{1,0:T(8,128)(2,1)} %get-tuple-element.24), channel_id=1, source_target_pairs={{0,32},{16,48},{32,0},{48,16},{1,33},{17,49},{33,1},{49,17},{2,34}... | collective-permute-start | bytes 1327112 | tf_op jit(solution)/shard_map/ppermute | solution.py:23
  59.5 4.6 %collective-permute-start.7 = (bf16[192,1152]{1,0:T(8,128)(2,1)}, bf16[192,1152]{1,0:T(8,128)(2,1)S(1)}, u32[]{:S(2)}, u32[]{:S(2)}) collective-permute-start(bf16[192,1152]{1,0:T(8,128)(2,1)} %get-tuple-element.25), channel_id=1, source_target_pairs={{0,48},{16,0},{32,16},{48,32},{1,49},{17,1},{33,17},{49,33},{2,50}... | collective-permute-start | bytes 1327112 | tf_op jit(solution)/shard_map/ppermute | solution.py:23
  65.0 3.5 %collective-permute-done.6.refs_2_ = bf16[192,1152]{1,0:T(8,128)(2,1)S(1)} collective-permute-done((bf16[192,1152]{1,0:T(8,128)(2,1)}, bf16[192,1152]{1,0:T(8,128)(2,1)S(1)}, u32[]{:S(2)}, u32[]{:S(2)}) %collective-permute-start.6) | collective-permute-done | bytes 442400 | tf_op jit(solution)/shard_map/ppermute | solution.py:23
  68.6 15.6 %collective-permute-done.7.refs_3_ = bf16[192,1152]{1,0:T(8,128)(2,1)S(1)} collective-permute-done((bf16[192,1152]{1,0:T(8,128)(2,1)}, bf16[192,1152]{1,0:T(8,128)(2,1)S(1)}, u32[]{:S(2)}, u32[]{:S(2)}) %collective-permute-start.7) | collective-permute-done | bytes 442400 | tf_op jit(solution)/shard_map/ppermute | solution.py:23
  84.1 5.4 %project.3 = (bf16[192,1024]{1,0:T(8,128)(2,1)}, bf16[192,1024]{1,0:T(8,128)(2,1)}, bf16[192,1024]{1,0:T(8,128)(2,1)S(1)}) custom-call(s32[4]{0:T(128)S(1)} %pad_add_fusion.refs_0_, bf16[192,192]{1,0:T(8,128)(2,1)S(1)} %fusion.1.order_ref.refs_1_, bf16[192,1152]{1,0:T(8,128)(2,1)S(1)} %collective-permute-done.6.refs_2_, ...), custom_call_target="tpu_custom_call" | custom-call | flops 393216 | bytes 393216 | tf_op jit(solution)/shard_map/project/pallas_call | solution.py:301
  89.5 4.5 %project.5 = (bf16[192,1024]{1,0:T(8,128)(2,1)}, bf16[192,2048]{1,0:T(8,128)(2,1)S(1)}) custom-call(s32[6]{0:T(128)S(1)} %stack.95.refs_0_, bf16[192,1024]{1,0:T(8,128)(2,1)S(1)} %get-tuple-element.28.refs_1_, bf16[1024,8192]{1,0:T(8,128)(2,1)} %refs_2_.3), custom_call_target="tpu_custom_call" | custom-call | flops 393216 | bytes 393216 | tf_op jit(solution)/shard_map/project/pallas_call | solution.py:301
  94.0 2.7 %collective-permute-start.13 = (bf16[192,2048]{1,0:T(8,128)(2,1)S(1)}, bf16[192,2048]{1,0:T(8,128)(2,1)S(1)}, u32[]{:S(2)}, u32[]{:S(2)}) collective-permute-start(bf16[192,2048]{1,0:T(8,128)(2,1)S(1)} %get-tuple-element.36), channel_id=1, source_target_pairs={{0,1},{1,0},{2,3},{3,2},{4,5},{5,4},{6,7},{7,6},{8,9},{9,8},{10,11... | collective-permute-start | bytes 2359304 | tf_op jit(solution)/shard_map/ppermute | solution.py:23
  96.8 4.0 %collective-permute-start.9 = (bf16[192,1024]{1,0:T(8,128)(2,1)}, bf16[192,1024]{1,0:T(8,128)(2,1)S(1)}, u32[]{:S(2)}, u32[]{:S(2)}) collective-permute-start(bf16[192,1024]{1,0:T(8,128)(2,1)} %get-tuple-element.30), channel_id=1, source_target_pairs={{0,6},{2,0},{4,2},{6,4},{1,7},{3,1},{5,3},{7,5},{8,14},{10,8},{12,... | collective-permute-start | bytes 1179656 | tf_op jit(solution)/shard_map/ppermute | solution.py:23
  100.7 1.9 %collective-permute-start.11 = (bf16[192,1024]{1,0:T(8,128)(2,1)}, bf16[192,1024]{1,0:T(8,128)(2,1)S(1)}, u32[]{:S(2)}, u32[]{:S(2)}) collective-permute-start(bf16[192,1024]{1,0:T(8,128)(2,1)} %get-tuple-element.32), channel_id=1, source_target_pairs={{0,4},{2,6},{4,0},{6,2},{1,5},{3,7},{5,1},{7,3},{8,12},{10,14},{12... | collective-permute-start | bytes 1179656 | tf_op jit(solution)/shard_map/ppermute | solution.py:23
  102.7 4.1 %project.4 = (bf16[192,1024]{1,0:T(8,128)(2,1)S(1)}, bf16[192,2048]{1,0:T(8,128)(2,1)S(1)}) custom-call(s32[6]{0:T(128)S(1)} %stack.78.refs_0_, bf16[192,1024]{1,0:T(8,128)(2,1)S(1)} %get-tuple-element.28.refs_1_, bf16[1024,8192]{1,0:T(8,128)(2,1)} %refs_2_.3), custom_call_target="tpu_custom_call" | custom-call | flops 393216 | bytes 393216 | tf_op jit(solution)/shard_map/project/pallas_call | solution.py:301
  106.9 12.1 %collective-permute-done.9.refs_1_ = bf16[192,1024]{1,0:T(8,128)(2,1)S(1)} collective-permute-done((bf16[192,1024]{1,0:T(8,128)(2,1)}, bf16[192,1024]{1,0:T(8,128)(2,1)S(1)}, u32[]{:S(2)}, u32[]{:S(2)}) %collective-permute-start.9) | collective-permute-done | bytes 393248 | tf_op jit(solution)/shard_map/ppermute | solution.py:23
  118.9 3.4 %collective-permute-done.10.refs_2_ = bf16[192,1024]{1,0:T(8,128)(2,1)S(1)} collective-permute-done((bf16[192,1024]{1,0:T(8,128)(2,1)}, bf16[192,1024]{1,0:T(8,128)(2,1)S(1)}, u32[]{:S(2)}, u32[]{:S(2)}) %collective-permute-start.10) | collective-permute-done | bytes 393248 | tf_op jit(solution)/shard_map/ppermute | solution.py:23
  122.5 1.1 collective-permute-start.12
  124.9 2.7 %collective-permute-start.16 = (bf16[192,512]{1,0:T(8,128)(2,1)S(1)}, bf16[192,512]{1,0:T(8,128)(2,1)S(1)}, u32[]{:S(2)}, u32[]{:S(2)}) collective-permute-start(bf16[192,512]{1,0:T(8,128)(2,1)S(1)} %get-tuple-element.41), channel_id=1, source_target_pairs={{0,6},{2,0},{4,2},{6,4},{1,7},{3,1},{5,3},{7,5},{8,14},{10,8},{12,... | collective-permute-start | bytes 589832 | tf_op jit(solution)/shard_map/ppermute | solution.py:23
  128.3 2.6 %collective-permute-done.12.refs_1_ = bf16[192,512]{1,0:T(8,128)(2,1)S(1)} collective-permute-done((bf16[192,512]{1,0:T(8,128)(2,1)S(1)}, bf16[192,512]{1,0:T(8,128)(2,1)S(1)}, u32[]{:S(2)}, u32[]{:S(2)}) %collective-permute-start.12) | collective-permute-done | bytes 196640 | tf_op jit(solution)/shard_map/ppermute | solution.py:23
  130.8 2.5 %collective-permute-done.14.refs_3_ = bf16[192,512]{1,0:T(8,128)(2,1)S(1)} collective-permute-done((bf16[192,512]{1,0:T(8,128)(2,1)S(1)}, bf16[192,512]{1,0:T(8,128)(2,1)S(1)}, u32[]{:S(2)}, u32[]{:S(2)}) %collective-permute-start.14) | collective-permute-done | bytes 196640 | tf_op jit(solution)/shard_map/ppermute | solution.py:23
  133.3 2.8 %collective-permute-done.15.refs_4_ = bf16[192,512]{1,0:T(8,128)(2,1)S(1)} collective-permute-done((bf16[192,512]{1,0:T(8,128)(2,1)S(1)}, bf16[192,512]{1,0:T(8,128)(2,1)S(1)}, u32[]{:S(2)}, u32[]{:S(2)}) %collective-permute-start.15) | collective-permute-done | bytes 196640 | tf_op jit(solution)/shard_map/ppermute | solution.py:23
  (58 shorter events, 11.9 us)
Async XLA Ops:
  3.1 1.0 copy-start
  4.1 1.0 copy-start.1
  5.1 1.0 copy-start.3
  6.4 23.4 %collective-permute-start.4 = (bf16[256,1664]{1,0:T(8,128)(2,1)S(1)}, bf16[256,1664]{1,0:T(8,128)(2,1)}, u32[]{:S(2)}, u32[]{:S(2)}) collective-permute-start(bf16[256,1664]{1,0:T(8,128)(2,1)S(1)} %get-tuple-element.23.refs_7_), channel_id=1, source_target_pairs={{0,64},{64,0},{1,65},{65,1},{2,66},{66,2},{3,67},{67,3},{4,68},{68... | collective-permute-start | bytes 2555912 | tf_op jit(solution)/shard_map/ppermute | solution.py:23
  6.8 14.6 %collective-permute-start = (bf16[192,1152]{1,0:T(8,128)(2,1)S(1)}, bf16[192,1152]{1,0:T(8,128)(2,1)S(1)}, u32[]{:S(2)}, u32[]{:S(2)}) collective-permute-start(bf16[192,1152]{1,0:T(8,128)(2,1)S(1)} %get-tuple-element.22.refs_6_), channel_id=1, source_target_pairs={{0,32},{16,48},{32,0},{48,16},{1,33},{17,49},{33,1},{49,17},{2,34}... | collective-permute-start | bytes 1327112 | tf_op jit(solution)/shard_map/ppermute | solution.py:23
  9.9 19.5 %collective-permute-start.1 = (bf16[192,1152]{1,0:T(8,128)(2,1)S(1)}, bf16[192,1152]{1,0:T(8,128)(2,1)S(1)}, u32[]{:S(2)}, u32[]{:S(2)}) collective-permute-start(bf16[192,1152]{1,0:T(8,128)(2,1)S(1)} %get-tuple-element.22.refs_6_), channel_id=1, source_target_pairs={{0,16},{16,32},{32,48},{48,0},{1,17},{17,33},{33,49},{49,1},{2,18}... | collective-permute-start | bytes 1327112 | tf_op jit(solution)/shard_map/ppermute | solution.py:23
  10.5 19.1 %collective-permute-start.2 = (bf16[192,1152]{1,0:T(8,128)(2,1)S(1)}, bf16[192,1152]{1,0:T(8,128)(2,1)S(1)}, u32[]{:S(2)}, u32[]{:S(2)}) collective-permute-start(bf16[192,1152]{1,0:T(8,128)(2,1)S(1)} %get-tuple-element.22.refs_6_), channel_id=1, source_target_pairs={{0,48},{16,0},{32,16},{48,32},{1,49},{17,1},{33,17},{49,33},{2,50}... | collective-permute-start | bytes 1327112 | tf_op jit(solution)/shard_map/ppermute | solution.py:23
  13.2 17.9 %collective-permute-start.3 = (bf16[256,1664]{1,0:T(8,128)(2,1)S(1)}, bf16[256,1664]{1,0:T(8,128)(2,1)}, u32[]{:S(2)}, u32[]{:S(2)}) collective-permute-start(bf16[256,1664]{1,0:T(8,128)(2,1)S(1)} %get-tuple-element.23.refs_7_), channel_id=1, source_target_pairs={{0,8},{8,0},{1,9},{9,1},{2,10},{10,2},{3,11},{11,3},{4,12},{12,4},... | collective-permute-start | bytes 2555912 | tf_op jit(solution)/shard_map/ppermute | solution.py:23
  29.8 2.7 %collective-permute-start.5 = (bf16[256,1664]{1,0:T(8,128)(2,1)}, bf16[256,1664]{1,0:T(8,128)(2,1)}, u32[]{:S(2)}, u32[]{:S(2)}) collective-permute-start(bf16[256,1664]{1,0:T(8,128)(2,1)} %collective-permute-done.4.refs_9_), channel_id=1, source_target_pairs={{0,8},{8,0},{1,9},{9,1},{2,10},{10,2},{3,11},{11,3},{4,12},{12,4},... | collective-permute-start | bytes 2555912 | tf_op jit(solution)/shard_map/ppermute | solution.py:23
  53.6 15.0 %collective-permute-start.6 = (bf16[192,1152]{1,0:T(8,128)(2,1)}, bf16[192,1152]{1,0:T(8,128)(2,1)S(1)}, u32[]{:S(2)}, u32[]{:S(2)}) collective-permute-start(bf16[192,1152]{1,0:T(8,128)(2,1)} %get-tuple-element.24), channel_id=1, source_target_pairs={{0,32},{16,48},{32,0},{48,16},{1,33},{17,49},{33,1},{49,17},{2,34}... | collective-permute-start | bytes 1327112 | tf_op jit(solution)/shard_map/ppermute | solution.py:23
  59.5 24.6 %collective-permute-start.7 = (bf16[192,1152]{1,0:T(8,128)(2,1)}, bf16[192,1152]{1,0:T(8,128)(2,1)S(1)}, u32[]{:S(2)}, u32[]{:S(2)}) collective-permute-start(bf16[192,1152]{1,0:T(8,128)(2,1)} %get-tuple-element.25), channel_id=1, source_target_pairs={{0,48},{16,0},{32,16},{48,32},{1,49},{17,1},{33,17},{49,33},{2,50}... | collective-permute-start | bytes 1327112 | tf_op jit(solution)/shard_map/ppermute | solution.py:23
  64.1 20.0 %collective-permute-start.8 = (bf16[192,1152]{1,0:T(8,128)(2,1)}, bf16[192,1152]{1,0:T(8,128)(2,1)S(1)}, u32[]{:S(2)}, u32[]{:S(2)}) collective-permute-start(bf16[192,1152]{1,0:T(8,128)(2,1)} %get-tuple-element.26), channel_id=1, source_target_pairs={{0,16},{16,32},{32,48},{48,0},{1,17},{17,33},{33,49},{49,1},{2,18}... | collective-permute-start | bytes 1327112 | tf_op jit(solution)/shard_map/ppermute | solution.py:23
  89.5 46.6 %copy-start.2 = (bf16[192,1024]{1,0:T(8,128)(2,1)S(1)}, bf16[192,1024]{1,0:T(8,128)(2,1)}, u32[]{:S(2)}) copy-start(bf16[192,1024]{1,0:T(8,128)(2,1)} %layer_ref.1) | copy-start | bytes 1179652
  94.0 29.6 %collective-permute-start.13 = (bf16[192,2048]{1,0:T(8,128)(2,1)S(1)}, bf16[192,2048]{1,0:T(8,128)(2,1)S(1)}, u32[]{:S(2)}, u32[]{:S(2)}) collective-permute-start(bf16[192,2048]{1,0:T(8,128)(2,1)S(1)} %get-tuple-element.36), channel_id=1, source_target_pairs={{0,1},{1,0},{2,3},{3,2},{4,5},{5,4},{6,7},{7,6},{8,9},{9,8},{10,11... | collective-permute-start | bytes 2359304 | tf_op jit(solution)/shard_map/ppermute | solution.py:23
  96.8 22.2 %collective-permute-start.9 = (bf16[192,1024]{1,0:T(8,128)(2,1)}, bf16[192,1024]{1,0:T(8,128)(2,1)S(1)}, u32[]{:S(2)}, u32[]{:S(2)}) collective-permute-start(bf16[192,1024]{1,0:T(8,128)(2,1)} %get-tuple-element.30), channel_id=1, source_target_pairs={{0,6},{2,0},{4,2},{6,4},{1,7},{3,1},{5,3},{7,5},{8,14},{10,8},{12,... | collective-permute-start | bytes 1179656 | tf_op jit(solution)/shard_map/ppermute | solution.py:23
  100.7 21.6 %collective-permute-start.10 = (bf16[192,1024]{1,0:T(8,128)(2,1)}, bf16[192,1024]{1,0:T(8,128)(2,1)S(1)}, u32[]{:S(2)}, u32[]{:S(2)}) collective-permute-start(bf16[192,1024]{1,0:T(8,128)(2,1)} %get-tuple-element.31), channel_id=1, source_target_pairs={{0,2},{2,4},{4,6},{6,0},{1,3},{3,5},{5,7},{7,1},{8,10},{10,12},{12... | collective-permute-start | bytes 1179656 | tf_op jit(solution)/shard_map/ppermute | solution.py:23
  100.7 21.6 %collective-permute-start.11 = (bf16[192,1024]{1,0:T(8,128)(2,1)}, bf16[192,1024]{1,0:T(8,128)(2,1)S(1)}, u32[]{:S(2)}, u32[]{:S(2)}) collective-permute-start(bf16[192,1024]{1,0:T(8,128)(2,1)} %get-tuple-element.32), channel_id=1, source_target_pairs={{0,4},{2,6},{4,0},{6,2},{1,5},{3,7},{5,1},{7,3},{8,12},{10,14},{12... | collective-permute-start | bytes 1179656 | tf_op jit(solution)/shard_map/ppermute | solution.py:23
  122.5 8.3 %collective-permute-start.12 = (bf16[192,512]{1,0:T(8,128)(2,1)S(1)}, bf16[192,512]{1,0:T(8,128)(2,1)S(1)}, u32[]{:S(2)}, u32[]{:S(2)}) collective-permute-start(bf16[192,512]{1,0:T(8,128)(2,1)S(1)} %get-tuple-element.34), channel_id=1, source_target_pairs={{0,1},{1,0},{2,3},{3,2},{4,5},{5,4},{6,7},{7,6},{8,9},{9,8},{10,11... | collective-permute-start | bytes 589832 | tf_op jit(solution)/shard_map/ppermute | solution.py:23
  123.9 9.4 %collective-permute-start.14 = (bf16[192,512]{1,0:T(8,128)(2,1)S(1)}, bf16[192,512]{1,0:T(8,128)(2,1)S(1)}, u32[]{:S(2)}, u32[]{:S(2)}) collective-permute-start(bf16[192,512]{1,0:T(8,128)(2,1)S(1)} %get-tuple-element.43), channel_id=1, source_target_pairs={{0,4},{2,6},{4,0},{6,2},{1,5},{3,7},{5,1},{7,3},{8,12},{10,14},{12... | collective-permute-start | bytes 589832 | tf_op jit(solution)/shard_map/ppermute | solution.py:23
  124.3 11.8 %collective-permute-start.15 = (bf16[192,512]{1,0:T(8,128)(2,1)S(1)}, bf16[192,512]{1,0:T(8,128)(2,1)S(1)}, u32[]{:S(2)}, u32[]{:S(2)}) collective-permute-start(bf16[192,512]{1,0:T(8,128)(2,1)S(1)} %get-tuple-element.42), channel_id=1, source_target_pairs={{0,2},{2,4},{4,6},{6,0},{1,3},{3,5},{5,7},{7,1},{8,10},{10,12},{12... | collective-permute-start | bytes 589832 | tf_op jit(solution)/shard_map/ppermute | solution.py:23
  124.9 11.2 %collective-permute-start.16 = (bf16[192,512]{1,0:T(8,128)(2,1)S(1)}, bf16[192,512]{1,0:T(8,128)(2,1)S(1)}, u32[]{:S(2)}, u32[]{:S(2)}) collective-permute-start(bf16[192,512]{1,0:T(8,128)(2,1)S(1)} %get-tuple-element.41), channel_id=1, source_target_pairs={{0,6},{2,0},{4,2},{6,4},{1,7},{3,1},{5,3},{7,5},{8,14},{10,8},{12,... | collective-permute-start | bytes 589832 | tf_op jit(solution)/shard_map/ppermute | solution.py:23

commit v5 on v4

--- a/solution.py
+++ b/solution.py
@@ -11,7 +11,7 @@
 SEQ = ("y", "x", "core")
 HEAD = ("z", "yh")
 CHUNK = 32
-GROUPS = ((2, 1, 3, 0),)
+GROUPS = ((2, 1, 3), (0,))
 LOWEST = -1e30
 BLOCKED = 1e30
 BF16 = jnp.bfloat16
@@ -186,12 +186,19 @@
     )(items, count, images, *payloads, *tiles)
 
 
-def prepare_kernel(key_ref, value_ref, q_ref, order_ref, extra_ref, tile_ref, payload_ref):
+def pack_kernel(key_hbm, value_hbm, tile_ref, key_ref, value_ref, sems):
+    copies = [
+        pltpu.make_async_copy(key_hbm, key_ref, sems.at[0]),
+        pltpu.make_async_copy(value_hbm, value_ref, sems.at[1]),
+    ]
+    for copy in copies:
+        copy.start()
+    for copy in copies:
+        copy.wait()
     keys, hd = key_ref.shape
-    padded = tile_ref.shape[1]
-    width = q_ref.shape[1]
     whole = keys // hd * hd
     mid = keys // 16 * 16
+    padded = tile_ref.shape[1]
     for k in range(0, whole, hd):
         block = key_ref[k : k + hd].astype(F32)
         tile_ref[:hd, k : k + hd] = block.T.astype(BF16)
@@ -203,29 +210,47 @@
     tile_ref[:hd, whole:] = block.T.astype(BF16)
     block = jnp.concatenate([value_ref[whole:mid].astype(F32), last_value], axis=0)
     tile_ref[hd:, whole:] = block.astype(BF16)
+
+
+def pack(keys, values, padded):
+    hd = keys.shape[1]
+    apart = pl.BlockSpec(memory_space=pl.ANY)
+    return pl.pallas_call(
+        pack_kernel,
+        out_shape=jax.ShapeDtypeStruct((2 * hd, padded), BF16),
+        in_specs=[apart] * 2,
+        out_specs=pl.BlockSpec(memory_space=pltpu.VMEM),
+        scratch_shapes=[
+            pltpu.VMEM(keys.shape, BF16),
+            pltpu.VMEM(values.shape, BF16),
+            pltpu.SemaphoreType.DMA((2,)),
+        ],
+        compiler_params=pltpu.CompilerParams(vmem_limit_bytes=60 << 20),
+        name="pack",
+    )(keys, values)
+
+
+def sort_kernel(q_ref, order_ref, extra_ref, payload_ref):
+    width = q_ref.shape[1]
     order = order_ref[...]
-    step = 2 * hd
+    step = 256
     for k in range(0, width, step):
         part = jnp.dot(order, q_ref[:, k : k + step], preferred_element_type=F32)
         payload_ref[:, k : k + step] = part.astype(BF16)
     payload_ref[:, width:] = extra_ref[...].astype(BF16)
 
 
-def prepare(keys, values, queries, order, extra, padded):
-    hd = keys.shape[1]
+def sort_tokens(queries, order, extra):
     tokens, width = queries.shape
     here = pl.BlockSpec(memory_space=pltpu.VMEM)
     return pl.pallas_call(
-        prepare_kernel,
-        out_shape=[
-            jax.ShapeDtypeStruct((2 * hd, padded), BF16),
-            jax.ShapeDtypeStruct((tokens, width + hd), BF16),
-        ],
-        in_specs=[here] * 5,
-        out_specs=[here] * 2,
+        sort_kernel,
+        out_shape=jax.ShapeDtypeStruct((tokens, width + extra.shape[1]), BF16),
+        in_specs=[here] * 3,
+        out_specs=here,
         compiler_params=pltpu.CompilerParams(vmem_limit_bytes=24 << 20),
-        name="prepare",
-    )(keys, values, queries, order, extra)
+        name="sort_tokens",
+    )(queries, order, extra)
 
 
 def work_list(wanted):
@@ -312,7 +337,7 @@
             ],
         ),
         cost_estimate=pl.CostEstimate(
-            flops=2 * tokens * depth, bytes_accessed=2 * tokens * depth, transcendentals=0
+            flops=2 * tokens * depth * width * total, bytes_accessed=4 * depth * width * total, transcendentals=0
         ),
         compiler_params=pltpu.CompilerParams(vmem_limit_bytes=50 << 20),
         name="project",
@@ -380,6 +405,9 @@
     nz, nyh = (lax.axis_size(n) for n in HEAD)
 
     padded = -(-keys // 128) * 128
+    own = pack(image_keys, image_values, padded)
+    across = shifted(own, "y", 1)
+    beside = shifted(own, "core", 1)
     low, high = image_range[0], image_range[1]
     grade = jnp.where(low < high, low * 16 + high, 1 << 10)
     place = jnp.arange(tokens, dtype=jnp.int32)
@@ -403,11 +431,10 @@
         ],
         axis=1,
     )
-    own, payload = prepare(image_keys, image_values, queries, order, extra, padded)
-    across = shifted(own, "y", 1)
+    payload = sort_tokens(queries, order, extra)
+    payload, beside = lax.optimization_barrier((payload, beside))
     payloads = {s: shifted(payload, "x", s) for s in (2, 1, 3)}
     payloads[0] = payload
-    beside = shifted(own, "core", 1)
     diagonal = shifted(across, "core", 1)
     tiles = (own, beside, across, diagonal)
 
@@ -420,6 +447,8 @@
 
     parts = {}
     for turns in GROUPS:
+        if parts:
+            images = lax.optimization_barrier((images, *parts.values()))[0]
         flags = jnp.concatenate([payloads[s][::CHUNK, width + 16 : width + 32] for s in turns], axis=0)
         wanted = jnp.sum(flags.astype(jnp.int32)[:, None, :] * mine[None, :, :], axis=2)
         items, count = work_list(wanted)
@@ -433,8 +462,8 @@
             tokens,
             hd,
         )
-        for s, part in zip(turns, got):
-            parts[s] = part if s == 0 else shifted(part, "x", nx - s)
+        parts.update(zip(turns, got))
+    parts = {s: part if s == 0 else shifted(part, "x", nx - s) for s, part in parts.items()}
 
     half = width // 2
 
@@ -442,12 +471,14 @@
         return ((z + dz) % nz * nyh + (yh + dy) % nyh) * 2
 
     sources = [order] + [parts[s] for s in (2, 1, 3, 0)]
+    over_y, attended = project(
+        sources, out_weight, [first(dz, 1) + 1 for dz in (1, 2, 3, 0)], (4,), half, hd
+    )
+    got_y = shifted(over_y, "yh", 1)
     far = [first(dz, dy) for dz in (2, 1) for dy in (1, 0)]
-    *over_z, attended = project(sources, out_weight, far, (2, 2), half, hd)
+    over_z = project([attended], out_weight, far, (2, 2), half, hd)
     got_z = [shifted(term, "z", dz) for dz, term in zip((2, 1), over_z)]
-    mixed = [first(3, 1), first(3, 0)] + [first(dz, 1) + 1 for dz in (1, 2, 3, 0)]
-    last_z, over_y = project([attended], out_weight, mixed, (2, 4), half, hd)
-    got_y = shifted(over_y, "yh", 1)
+    (last_z,) = project([attended], out_weight, [first(3, 1), first(3, 0)], (2,), half, hd)
     got_z.append(shifted(last_z, "z", 3))
     near = [first(0, 1), first(0, 0)] + [first(dz, 0) + 1 for dz in (1, 2, 3, 0)]
     own_z, own_y = project([attended], out_weight, near, (2, 4), half, hd)

time: 136 us -> 129 us (0.949)
  the two profiles are of different devices: /device:TPU:8 before, /device:TPU:63 now
where the time goes in v5:
time: 129 us; the launch traced here: 128 us
  Pallas kernels  52.7 us (41%)
  waiting for transfers between devices  45.6 us (35%)
  starting transfers between devices  19.7 us (15%)
  other arithmetic  4.56 us (4%)
  local copies, waits for them, and re-layouts  3.06 us (2%)
    ppermute x17, waiting for transfers between devices, shifted(): lax.ppermute(value, axis, [(s, (s + steps) % count) for s in range(count)])  45.6 us
    pallas_call x2, Pallas kernels, attend(): pl.pallas_call(lambda *refs: attend_kernel(*refs, scale=1.0 / math.sqrt(h...  32.6 us
    ppermute x17, starting transfers between devices, shifted(): lax.ppermute(value, axis, [(s, (s + steps) % count) for s in range(count)])  19.7 us
    pallas_call x4, Pallas kernels, project(): pl.pallas_call(lambda *refs: project_kernel(*refs, hd=hd, group=depth //...  16.2 us
  transfers between devices with their start and end apart: 17, of which 10 were waited for; matrix products, arithmetic and copies ran while one was open for 5% of the time, Pallas kernels for 18%

profile of v5, /device:TPU:63, one launch (start us, length us, event | category | flops | bytes accessed | tf_op | source)
XLA Modules:
  0.0 127.7 jit_solution(7580283730425201771)
XLA Ops:
  0.0 2.3 %pack.1.refs_6_.refs_4_ = bf16[256,1664]{1,0:T(8,128)(2,1)} custom-call(bf16[1601,128]{1,0:T(8,128)(2,1)} %key_hbm.1, bf16[1601,128]{1,0:T(8,128)(2,1)} %value_hbm.1), custom_call_target="tpu_custom_call" | custom-call | tf_op jit(solution)/shard_map/pack/pallas_call | solution.py:218
  9.6 1.8 %collective-permute-start.2 = (bf16[192,1152]{1,0:T(8,128)(2,1)S(1)}, bf16[192,1152]{1,0:T(8,128)(2,1)S(1)}, u32[]{:S(2)}, u32[]{:S(2)}) collective-permute-start(bf16[192,1152]{1,0:T(8,128)(2,1)S(1)} %sort_tokens.1.refs_3_), channel_id=1, source_target_pairs={{0,16},{16,32},{32,48},{48,0},{1,17},{17,33},{33,49},{49,1},{2,18}... | collective-permute-start | bytes 1327112 | tf_op jit(solution)/shard_map/ppermute | solution.py:23
  12.4 11.5 %collective-permute-done.4.refs_8_.refs_6_ = bf16[256,1664]{1,0:T(8,128)(2,1)} collective-permute-done((bf16[256,1664]{1,0:T(8,128)(2,1)}, bf16[256,1664]{1,0:T(8,128)(2,1)}, u32[]{:S(2)}, u32[]{:S(2)}) %collective-permute-start.4) | collective-permute-done | bytes 852000 | tf_op jit(solution)/shard_map/ppermute | solution.py:23
  25.0 3.7 %collective-permute-done.2.refs_4_ = bf16[192,1152]{1,0:T(8,128)(2,1)S(1)} collective-permute-done((bf16[192,1152]{1,0:T(8,128)(2,1)S(1)}, bf16[192,1152]{1,0:T(8,128)(2,1)S(1)}, u32[]{:S(2)}, u32[]{:S(2)}) %collective-permute-start.2) | collective-permute-done | bytes 442400 | tf_op jit(solution)/shard_map/ppermute | solution.py:23
  28.8 2.7 %collective-permute-done.3.refs_5_ = bf16[192,1152]{1,0:T(8,128)(2,1)S(1)} collective-permute-done((bf16[192,1152]{1,0:T(8,128)(2,1)S(1)}, bf16[192,1152]{1,0:T(8,128)(2,1)S(1)}, u32[]{:S(2)}, u32[]{:S(2)}) %collective-permute-start.3) | collective-permute-done | bytes 442400 | tf_op jit(solution)/shard_map/ppermute | solution.py:23
  33.0 1.1 copy-done
  34.1 21.6 %attend.2 = (bf16[192,1152]{1,0:T(8,128)(2,1)S(1)}, bf16[192,1152]{1,0:T(8,128)(2,1)S(1)}, bf16[192,1152]{1,0:T(8,128)(2,1)S(1)}) custom-call(s32[75]{0:T(128)S(1)} %compare_select_fusion.2.refs_0_, s32[1]{0:T(128)} %bitcast.17.refs_1_, s32[4]{0:T(128)S(1)} %select_reduce_fusion.3.refs_2_, bf16[192,1152]{1,0:T(8,128)(2,1)S(1)} %collective-permute-done.1.refs_3_, ...), custom_call_target="tpu_custom_call" | custom-call | flops 3925868544 | bytes 5767168 | tf_op jit(solution)/shard_map/attend/pallas_call | solution.py:149
  55.8 1.8 %collective-permute-start.7 = (bf16[192,1152]{1,0:T(8,128)(2,1)S(1)}, bf16[192,1152]{1,0:T(8,128)(2,1)S(1)}, u32[]{:S(2)}, u32[]{:S(2)}) collective-permute-start(bf16[192,1152]{1,0:T(8,128)(2,1)S(1)} %get-tuple-element.24), channel_id=1, source_target_pairs={{0,48},{16,0},{32,16},{48,32},{1,49},{17,1},{33,17},{49,33},{2,50}... | collective-permute-start | bytes 1327112 | tf_op jit(solution)/shard_map/ppermute | solution.py:23
  57.6 2.3 %collective-permute-start.8 = (bf16[192,1152]{1,0:T(8,128)(2,1)S(1)}, bf16[192,1152]{1,0:T(8,128)(2,1)S(1)}, u32[]{:S(2)}, u32[]{:S(2)}) collective-permute-start(bf16[192,1152]{1,0:T(8,128)(2,1)S(1)} %get-tuple-element.25), channel_id=1, source_target_pairs={{0,16},{16,32},{32,48},{48,0},{1,17},{17,33},{33,49},{49,1},{2,18}... | collective-permute-start | bytes 1327112 | tf_op jit(solution)/shard_map/ppermute | solution.py:23
  60.0 11.1 %attend.3.refs_5_ = bf16[192,1152]{1,0:T(8,128)(2,1)S(1)} custom-call(s32[27]{0:T(128)S(1)} %compare_select_fusion.1.refs_0_, s32[1]{0:T(128)} %bitcast.18.refs_1_, s32[4]{0:T(128)S(1)} %select_reduce_fusion.3.refs_2_, bf16[192,1152]{1,0:T(8,128)(2,1)S(1)} %sort_tokens.1.refs_3_, bf16[256,1664]{1,0:T(8,128)(2,1)S(1)} %copy-done, ...), custom_call_target="tpu_custom_call" | custom-call | flops 1308622848 | bytes 4194304 | tf_op jit(solution)/shard_map/attend/pallas_call | solution.py:149
  71.1 6.9 %collective-permute-done.7.refs_3_ = bf16[192,1152]{1,0:T(8,128)(2,1)S(1)} collective-permute-done((bf16[192,1152]{1,0:T(8,128)(2,1)S(1)}, bf16[192,1152]{1,0:T(8,128)(2,1)S(1)}, u32[]{:S(2)}, u32[]{:S(2)}) %collective-permute-start.7) | collective-permute-done | bytes 442400 | tf_op jit(solution)/shard_map/ppermute | solution.py:23
  78.0 5.5 %project.4 = (bf16[192,2048]{1,0:T(8,128)(2,1)}, bf16[192,1024]{1,0:T(8,128)(2,1)S(1)}) custom-call(s32[4]{0:T(128)S(1)} %pad_add_fusion.refs_0_, bf16[192,192]{1,0:T(8,128)(2,1)S(1)} %fusion.1.order_ref.refs_1_, bf16[192,1152]{1,0:T(8,128)(2,1)S(1)} %collective-permute-done.6.refs_2_, bf16[192,1152]{1,0:T(8,128)(2,1)S(1)} %collective-permute-done.7.refs_3_, ...), custom_call_target="tpu_custom_call" | custom-call | flops 805306368 | bytes 8388608 | tf_op jit(solution)/shard_map/project/pallas_call | solution.py:326
  84.4 4.1 %project.7 = (bf16[192,1024]{1,0:T(8,128)(2,1)}, bf16[192,1024]{1,0:T(8,128)(2,1)}) custom-call(s32[4]{0:T(128)S(1)} %pad_add_fusion.3.refs_0_, bf16[192,1024]{1,0:T(8,128)(2,1)S(1)} %get-tuple-element.27.refs_1_, bf16[1024,8192]{1,0:T(8,128)(2,1)} %refs_2_.5), custom_call_target="tpu_custom_call" | custom-call | flops 805306368 | bytes 8388608 | tf_op jit(solution)/shard_map/project/pallas_call | solution.py:326
  88.4 1.8 %collective-permute-start.10 = (bf16[192,1024]{1,0:T(8,128)(2,1)}, bf16[192,1024]{1,0:T(8,128)(2,1)S(1)}, u32[]{:S(2)}, u32[]{:S(2)}) collective-permute-start(bf16[192,1024]{1,0:T(8,128)(2,1)} %get-tuple-element.29), channel_id=1, source_target_pairs={{0,2},{2,4},{4,6},{6,0},{1,3},{3,5},{5,7},{7,1},{8,10},{10,12},{12... | collective-permute-start | bytes 1179656 | tf_op jit(solution)/shard_map/ppermute | solution.py:23
  91.3 2.5 %project.6 = bf16[192,1024]{1,0:T(8,128)(2,1)S(1)} custom-call(s32[2]{0:T(128)S(1)} %pad_add_fusion.2.refs_0_, bf16[192,1024]{1,0:T(8,128)(2,1)S(1)} %get-tuple-element.27.refs_1_, bf16[1024,8192]{1,0:T(8,128)(2,1)} %refs_2_.5), custom_call_target="tpu_custom_call" | custom-call | flops 402653184 | bytes 4194304 | tf_op jit(solution)/shard_map/project/pallas_call | solution.py:326
  93.9 2.0 %collective-permute-start.9 = (bf16[192,1024]{1,0:T(8,128)(2,1)S(1)}, bf16[192,1024]{1,0:T(8,128)(2,1)S(1)}, u32[]{:S(2)}, u32[]{:S(2)}) collective-permute-start(bf16[192,1024]{1,0:T(8,128)(2,1)S(1)} %project.6), channel_id=1, source_target_pairs={{0,6},{2,0},{4,2},{6,4},{1,7},{3,1},{5,3},{7,5},{8,14},{10,8},{12,... | collective-permute-start | bytes 1179656 | tf_op jit(solution)/shard_map/ppermute | solution.py:23
  96.0 4.1 %project.5 = (bf16[192,1024]{1,0:T(8,128)(2,1)S(1)}, bf16[192,2048]{1,0:T(8,128)(2,1)S(1)}) custom-call(s32[6]{0:T(128)S(1)} %stack.81.refs_0_, bf16[192,1024]{1,0:T(8,128)(2,1)S(1)} %get-tuple-element.27.refs_1_, bf16[1024,8192]{1,0:T(8,128)(2,1)} %refs_2_.5), custom_call_target="tpu_custom_call" | custom-call | flops 1207959552 | bytes 12582912 | tf_op jit(solution)/shard_map/project/pallas_call | solution.py:326
  100.6 10.8 %collective-permute-done.9.refs_1_ = bf16[192,1024]{1,0:T(8,128)(2,1)S(1)} collective-permute-done((bf16[192,1024]{1,0:T(8,128)(2,1)S(1)}, bf16[192,1024]{1,0:T(8,128)(2,1)S(1)}, u32[]{:S(2)}, u32[]{:S(2)}) %collective-permute-start.9) | collective-permute-done | bytes 393248 | tf_op jit(solution)/shard_map/ppermute | solution.py:23
  111.6 2.4 %collective-permute-start.12 = (bf16[192,512]{1,0:T(8,128)(2,1)S(1)}, bf16[192,512]{1,0:T(8,128)(2,1)S(1)}, u32[]{:S(2)}, u32[]{:S(2)}) collective-permute-start(bf16[192,512]{1,0:T(8,128)(2,1)S(1)} %get-tuple-element.32), channel_id=1, source_target_pairs={{0,1},{1,0},{2,3},{3,2},{4,5},{5,4},{6,7},{7,6},{8,9},{9,8},{10,11... | collective-permute-start | bytes 589832 | tf_op jit(solution)/shard_map/ppermute | solution.py:23
  115.2 1.5 %collective-permute-start.16 = (bf16[192,512]{1,0:T(8,128)(2,1)S(1)}, bf16[192,512]{1,0:T(8,128)(2,1)S(1)}, u32[]{:S(2)}, u32[]{:S(2)}) collective-permute-start(bf16[192,512]{1,0:T(8,128)(2,1)S(1)} %get-tuple-element.41), channel_id=1, source_target_pairs={{0,6},{2,0},{4,2},{6,4},{1,7},{3,1},{5,3},{7,5},{8,14},{10,8},{12,... | collective-permute-start | bytes 589832 | tf_op jit(solution)/shard_map/ppermute | solution.py:23
  117.4 1.8 %collective-permute-done.12.refs_1_ = bf16[192,512]{1,0:T(8,128)(2,1)S(1)} collective-permute-done((bf16[192,512]{1,0:T(8,128)(2,1)S(1)}, bf16[192,512]{1,0:T(8,128)(2,1)S(1)}, u32[]{:S(2)}, u32[]{:S(2)}) %collective-permute-start.12) | collective-permute-done | bytes 196640 | tf_op jit(solution)/shard_map/ppermute | solution.py:23
  119.2 2.3 %collective-permute-done.14.refs_3_ = bf16[192,512]{1,0:T(8,128)(2,1)S(1)} collective-permute-done((bf16[192,512]{1,0:T(8,128)(2,1)S(1)}, bf16[192,512]{1,0:T(8,128)(2,1)S(1)}, u32[]{:S(2)}, u32[]{:S(2)}) %collective-permute-start.14) | collective-permute-done | bytes 196640 | tf_op jit(solution)/shard_map/ppermute | solution.py:23
  121.5 2.4 %collective-permute-done.15.refs_4_ = bf16[192,512]{1,0:T(8,128)(2,1)S(1)} collective-permute-done((bf16[192,512]{1,0:T(8,128)(2,1)S(1)}, bf16[192,512]{1,0:T(8,128)(2,1)S(1)}, u32[]{:S(2)}, u32[]{:S(2)}) %collective-permute-start.15) | collective-permute-done | bytes 196640 | tf_op jit(solution)/shard_map/ppermute | solution.py:23
  123.9 2.9 %collective-permute-done.16.refs_5_ = bf16[192,512]{1,0:T(8,128)(2,1)S(1)} collective-permute-done((bf16[192,512]{1,0:T(8,128)(2,1)S(1)}, bf16[192,512]{1,0:T(8,128)(2,1)S(1)}, u32[]{:S(2)}, u32[]{:S(2)}) %collective-permute-start.16) | collective-permute-done | bytes 196640 | tf_op jit(solution)/shard_map/ppermute | solution.py:23
  (68 shorter events, 15.8 us)
Async XLA Ops:
  2.3 6.1 %collective-permute-start = (bf16[256,1664]{1,0:T(8,128)(2,1)}, bf16[256,1664]{1,0:T(8,128)(2,1)S(1)}, u32[]{:S(2)}, u32[]{:S(2)}) collective-permute-start(bf16[256,1664]{1,0:T(8,128)(2,1)} %pack.1.refs_6_.refs_4_), channel_id=1, source_target_pairs={{0,8},{8,0},{1,9},{9,1},{2,10},{10,2},{3,11},{11,3},{4,12},{12,4},... | collective-permute-start | bytes 2555912 | tf_op jit(solution)/shard_map/ppermute | solution.py:23
  3.1 20.8 %collective-permute-start.4 = (bf16[256,1664]{1,0:T(8,128)(2,1)}, bf16[256,1664]{1,0:T(8,128)(2,1)}, u32[]{:S(2)}, u32[]{:S(2)}) collective-permute-start(bf16[256,1664]{1,0:T(8,128)(2,1)} %pack.1.refs_6_.refs_4_), channel_id=1, source_target_pairs={{0,64},{64,0},{1,65},{65,1},{2,66},{66,2},{3,67},{67,3},{4,68},{68... | collective-permute-start | bytes 2555912 | tf_op jit(solution)/shard_map/ppermute | solution.py:23
  6.7 1.0 copy-start.2
  8.4 16.5 %collective-permute-start.1 = (bf16[192,1152]{1,0:T(8,128)(2,1)S(1)}, bf16[192,1152]{1,0:T(8,128)(2,1)S(1)}, u32[]{:S(2)}, u32[]{:S(2)}) collective-permute-start(bf16[192,1152]{1,0:T(8,128)(2,1)S(1)} %sort_tokens.1.refs_3_), channel_id=1, source_target_pairs={{0,32},{16,48},{32,0},{48,16},{1,33},{17,49},{33,1},{49,17},{2,34}... | collective-permute-start | bytes 1327112 | tf_op jit(solution)/shard_map/ppermute | solution.py:23
  9.6 19.1 %collective-permute-start.2 = (bf16[192,1152]{1,0:T(8,128)(2,1)S(1)}, bf16[192,1152]{1,0:T(8,128)(2,1)S(1)}, u32[]{:S(2)}, u32[]{:S(2)}) collective-permute-start(bf16[192,1152]{1,0:T(8,128)(2,1)S(1)} %sort_tokens.1.refs_3_), channel_id=1, source_target_pairs={{0,16},{16,32},{32,48},{48,0},{1,17},{17,33},{33,49},{49,1},{2,18}... | collective-permute-start | bytes 1327112 | tf_op jit(solution)/shard_map/ppermute | solution.py:23
  11.4 20.1 %collective-permute-start.3 = (bf16[192,1152]{1,0:T(8,128)(2,1)S(1)}, bf16[192,1152]{1,0:T(8,128)(2,1)S(1)}, u32[]{:S(2)}, u32[]{:S(2)}) collective-permute-start(bf16[192,1152]{1,0:T(8,128)(2,1)S(1)} %sort_tokens.1.refs_3_), channel_id=1, source_target_pairs={{0,48},{16,0},{32,16},{48,32},{1,49},{17,1},{33,17},{49,33},{2,50}... | collective-permute-start | bytes 1327112 | tf_op jit(solution)/shard_map/ppermute | solution.py:23
  23.9 9.0 %collective-permute-start.5 = (bf16[256,1664]{1,0:T(8,128)(2,1)}, bf16[256,1664]{1,0:T(8,128)(2,1)}, u32[]{:S(2)}, u32[]{:S(2)}) collective-permute-start(bf16[256,1664]{1,0:T(8,128)(2,1)} %collective-permute-done.4.refs_8_.refs_6_), channel_id=1, source_target_pairs={{0,8},{8,0},{1,9},{9,1},{2,10},{10,2},{3,11},{11,3},{4,12},{12,4},... | collective-permute-start | bytes 2555912 | tf_op jit(solution)/shard_map/ppermute | solution.py:23
  32.9 1.2 copy-start
  55.7 15.4 %collective-permute-start.6 = (bf16[192,1152]{1,0:T(8,128)(2,1)S(1)}, bf16[192,1152]{1,0:T(8,128)(2,1)S(1)}, u32[]{:S(2)}, u32[]{:S(2)}) collective-permute-start(bf16[192,1152]{1,0:T(8,128)(2,1)S(1)} %get-tuple-element.23), channel_id=1, source_target_pairs={{0,32},{16,48},{32,0},{48,16},{1,33},{17,49},{33,1},{49,17},{2,34}... | collective-permute-start | bytes 1327112 | tf_op jit(solution)/shard_map/ppermute | solution.py:23
  55.8 22.2 %collective-permute-start.7 = (bf16[192,1152]{1,0:T(8,128)(2,1)S(1)}, bf16[192,1152]{1,0:T(8,128)(2,1)S(1)}, u32[]{:S(2)}, u32[]{:S(2)}) collective-permute-start(bf16[192,1152]{1,0:T(8,128)(2,1)S(1)} %get-tuple-element.24), channel_id=1, source_target_pairs={{0,48},{16,0},{32,16},{48,32},{1,49},{17,1},{33,17},{49,33},{2,50}... | collective-permute-start | bytes 1327112 | tf_op jit(solution)/shard_map/ppermute | solution.py:23
  57.6 20.4 %collective-permute-start.8 = (bf16[192,1152]{1,0:T(8,128)(2,1)S(1)}, bf16[192,1152]{1,0:T(8,128)(2,1)S(1)}, u32[]{:S(2)}, u32[]{:S(2)}) collective-permute-start(bf16[192,1152]{1,0:T(8,128)(2,1)S(1)} %get-tuple-element.25), channel_id=1, source_target_pairs={{0,16},{16,32},{32,48},{48,0},{1,17},{17,33},{33,49},{49,1},{2,18}... | collective-permute-start | bytes 1327112 | tf_op jit(solution)/shard_map/ppermute | solution.py:23
  83.5 30.5 %collective-permute-start.13 = (bf16[192,2048]{1,0:T(8,128)(2,1)}, bf16[192,2048]{1,0:T(8,128)(2,1)S(1)}, u32[]{:S(2)}, u32[]{:S(2)}) collective-permute-start(bf16[192,2048]{1,0:T(8,128)(2,1)} %get-tuple-element.34), channel_id=1, source_target_pairs={{0,1},{1,0},{2,3},{3,2},{4,5},{5,4},{6,7},{7,6},{8,9},{9,8},{10,11... | collective-permute-start | bytes 2359304 | tf_op jit(solution)/shard_map/ppermute | solution.py:23
  88.4 11.6 %collective-permute-start.10 = (bf16[192,1024]{1,0:T(8,128)(2,1)}, bf16[192,1024]{1,0:T(8,128)(2,1)S(1)}, u32[]{:S(2)}, u32[]{:S(2)}) collective-permute-start(bf16[192,1024]{1,0:T(8,128)(2,1)} %get-tuple-element.29), channel_id=1, source_target_pairs={{0,2},{2,4},{4,6},{6,0},{1,3},{3,5},{5,7},{7,1},{8,10},{10,12},{12... | collective-permute-start | bytes 1179656 | tf_op jit(solution)/shard_map/ppermute | solution.py:23
  90.2 36.6 %copy-start.1 = (bf16[192,1024]{1,0:T(8,128)(2,1)S(1)}, bf16[192,1024]{1,0:T(8,128)(2,1)}, u32[]{:S(2)}) copy-start(bf16[192,1024]{1,0:T(8,128)(2,1)} %layer_ref.1) | copy-start | bytes 1179652
  90.2 10.4 %collective-permute-start.11 = (bf16[192,1024]{1,0:T(8,128)(2,1)}, bf16[192,1024]{1,0:T(8,128)(2,1)S(1)}, u32[]{:S(2)}, u32[]{:S(2)}) collective-permute-start(bf16[192,1024]{1,0:T(8,128)(2,1)} %get-tuple-element.30), channel_id=1, source_target_pairs={{0,4},{2,6},{4,0},{6,2},{1,5},{3,7},{5,1},{7,3},{8,12},{10,14},{12... | collective-permute-start | bytes 1179656 | tf_op jit(solution)/shard_map/ppermute | solution.py:23
  93.9 17.5 %collective-permute-start.9 = (bf16[192,1024]{1,0:T(8,128)(2,1)S(1)}, bf16[192,1024]{1,0:T(8,128)(2,1)S(1)}, u32[]{:S(2)}, u32[]{:S(2)}) collective-permute-start(bf16[192,1024]{1,0:T(8,128)(2,1)S(1)} %project.6), channel_id=1, source_target_pairs={{0,6},{2,0},{4,2},{6,4},{1,7},{3,1},{5,3},{7,5},{8,14},{10,8},{12,... | collective-permute-start | bytes 1179656 | tf_op jit(solution)/shard_map/ppermute | solution.py:23
  111.6 7.6 %collective-permute-start.12 = (bf16[192,512]{1,0:T(8,128)(2,1)S(1)}, bf16[192,512]{1,0:T(8,128)(2,1)S(1)}, u32[]{:S(2)}, u32[]{:S(2)}) collective-permute-start(bf16[192,512]{1,0:T(8,128)(2,1)S(1)} %get-tuple-element.32), channel_id=1, source_target_pairs={{0,1},{1,0},{2,3},{3,2},{4,5},{5,4},{6,7},{7,6},{8,9},{9,8},{10,11... | collective-permute-start | bytes 589832 | tf_op jit(solution)/shard_map/ppermute | solution.py:23
  114.2 7.3 %collective-permute-start.14 = (bf16[192,512]{1,0:T(8,128)(2,1)S(1)}, bf16[192,512]{1,0:T(8,128)(2,1)S(1)}, u32[]{:S(2)}, u32[]{:S(2)}) collective-permute-start(bf16[192,512]{1,0:T(8,128)(2,1)S(1)} %get-tuple-element.43), channel_id=1, source_target_pairs={{0,4},{2,6},{4,0},{6,2},{1,5},{3,7},{5,1},{7,3},{8,12},{10,14},{12... | collective-permute-start | bytes 589832 | tf_op jit(solution)/shard_map/ppermute | solution.py:23
  115.2 8.7 %collective-permute-start.15 = (bf16[192,512]{1,0:T(8,128)(2,1)S(1)}, bf16[192,512]{1,0:T(8,128)(2,1)S(1)}, u32[]{:S(2)}, u32[]{:S(2)}) collective-permute-start(bf16[192,512]{1,0:T(8,128)(2,1)S(1)} %get-tuple-element.42), channel_id=1, source_target_pairs={{0,2},{2,4},{4,6},{6,0},{1,3},{3,5},{5,7},{7,1},{8,10},{10,12},{12... | collective-permute-start | bytes 589832 | tf_op jit(solution)/shard_map/ppermute | solution.py:23
  115.2 11.6 %collective-permute-start.16 = (bf16[192,512]{1,0:T(8,128)(2,1)S(1)}, bf16[192,512]{1,0:T(8,128)(2,1)S(1)}, u32[]{:S(2)}, u32[]{:S(2)}) collective-permute-start(bf16[192,512]{1,0:T(8,128)(2,1)S(1)} %get-tuple-element.41), channel_id=1, source_target_pairs={{0,6},{2,0},{4,2},{6,4},{1,7},{3,1},{5,3},{7,5},{8,14},{10,8},{12,... | collective-permute-start | bytes 589832 | tf_op jit(solution)/shard_map/ppermute | solution.py:23

commit v6 on v5

--- a/solution.py
+++ b/solution.py
@@ -186,16 +186,55 @@
     )(items, count, images, *payloads, *tiles)
 
 
-def pack_kernel(key_hbm, value_hbm, tile_ref, key_ref, value_ref, sems):
+def prepare_kernel(
+    counts, range_ref, key_hbm, value_hbm, q_hbm, tile_ref, payload_ref, back_ref, key_ref, value_ref, q_ref, sems
+):
     copies = [
         pltpu.make_async_copy(key_hbm, key_ref, sems.at[0]),
         pltpu.make_async_copy(value_hbm, value_ref, sems.at[1]),
+        pltpu.make_async_copy(q_hbm, q_ref, sems.at[2]),
     ]
     for copy in copies:
         copy.start()
+    tokens, width = q_ref.shape
+    keys, hd = key_ref.shape
+    square = (tokens, tokens)
+    down = lax.broadcasted_iota(jnp.int32, square, 0)
+    along = lax.broadcasted_iota(jnp.int32, square, 1)
+    rows = range_ref[...].astype(F32)
+    low_row = jnp.broadcast_to(rows[0:1], square)
+    high_row = jnp.broadcast_to(rows[1:2], square)
+    same = down == along
+    low = jnp.sum(jnp.where(same, low_row, 0.0), axis=1, keepdims=True)
+    high = jnp.sum(jnp.where(same, high_row, 0.0), axis=1, keepdims=True)
+    grade_row = jnp.where(low_row < high_row, low_row * 16 + high_row, 1024.0)
+    grade = jnp.where(low < high, low * 16 + high, 1024.0)
+    equal = grade == grade_row
+    before = (grade < grade_row) | (equal & (down < along))
+    after = (grade_row < grade) | (equal & (along < down))
+    rank_row = jnp.sum(jnp.where(before, 1.0, 0.0), axis=0, keepdims=True)
+    rank = jnp.sum(jnp.where(after, 1.0, 0.0), axis=1, keepdims=True)
+    order = jnp.where(rank_row == down.astype(F32), 1.0, 0.0).astype(BF16)
+    back_ref[...] = jnp.where(rank == along.astype(F32), 1.0, 0.0).astype(BF16)
+    lane = lax.broadcasted_iota(jnp.int32, (tokens, hd), 1)
+    owner = jnp.zeros((tokens, hd), F32)
+    end = 0
+    for i in range(counts.shape[0]):
+        end = end + counts[i]
+        owner = owner + jnp.where(lane - 16 >= end, 1.0, 0.0)
+    hits = (low <= owner) & (owner < high) & (lane >= 16) & (lane < 32)
+    extra = jnp.where(lane == 0, low, jnp.where(lane == 1, high, jnp.where(hits, 1.0, 0.0)))
+    placed = jnp.dot(order, extra.astype(BF16), preferred_element_type=F32)
+    group = jnp.where(down // CHUNK == along // CHUNK, 1.0, 0.0).astype(BF16)
+    crowd = jnp.dot(group, placed.astype(BF16), preferred_element_type=F32)
+    live = jnp.where(crowd > 0, 1.0, 0.0)
+    payload_ref[:, width:] = jnp.where(lane < 2, placed, live).astype(BF16)
     for copy in copies:
         copy.wait()
-    keys, hd = key_ref.shape
+    step = 2 * hd
+    for k in range(0, width, step):
+        part = jnp.dot(order, q_ref[:, k : k + step], preferred_element_type=F32)
+        payload_ref[:, k : k + step] = part.astype(BF16)
     whole = keys // hd * hd
     mid = keys // 16 * 16
     padded = tile_ref.shape[1]
@@ -212,45 +251,29 @@
     tile_ref[hd:, whole:] = block.astype(BF16)
 
 
-def pack(keys, values, padded):
+def prepare(counts, image_range, keys, values, queries, padded):
     hd = keys.shape[1]
+    tokens, width = queries.shape
     apart = pl.BlockSpec(memory_space=pl.ANY)
+    here = pl.BlockSpec(memory_space=pltpu.VMEM)
     return pl.pallas_call(
-        pack_kernel,
-        out_shape=jax.ShapeDtypeStruct((2 * hd, padded), BF16),
-        in_specs=[apart] * 2,
-        out_specs=pl.BlockSpec(memory_space=pltpu.VMEM),
+        prepare_kernel,
+        out_shape=[
+            jax.ShapeDtypeStruct((2 * hd, padded), BF16),
+            jax.ShapeDtypeStruct((tokens, width + hd), BF16),
+            jax.ShapeDtypeStruct((tokens, tokens), BF16),
+        ],
+        in_specs=[pl.BlockSpec(memory_space=pltpu.SMEM), here] + [apart] * 3,
+        out_specs=[here] * 3,
         scratch_shapes=[
             pltpu.VMEM(keys.shape, BF16),
             pltpu.VMEM(values.shape, BF16),
-            pltpu.SemaphoreType.DMA((2,)),
+            pltpu.VMEM(queries.shape, BF16),
+            pltpu.SemaphoreType.DMA((3,)),
         ],
         compiler_params=pltpu.CompilerParams(vmem_limit_bytes=60 << 20),
-        name="pack",
-    )(keys, values)
-
-
-def sort_kernel(q_ref, order_ref, extra_ref, payload_ref):
-    width = q_ref.shape[1]
-    order = order_ref[...]
-    step = 256
-    for k in range(0, width, step):
-        part = jnp.dot(order, q_ref[:, k : k + step], preferred_element_type=F32)
-        payload_ref[:, k : k + step] = part.astype(BF16)
-    payload_ref[:, width:] = extra_ref[...].astype(BF16)
-
-
-def sort_tokens(queries, order, extra):
-    tokens, width = queries.shape
-    here = pl.BlockSpec(memory_space=pltpu.VMEM)
-    return pl.pallas_call(
-        sort_kernel,
-        out_shape=jax.ShapeDtypeStruct((tokens, width + extra.shape[1]), BF16),
-        in_specs=[here] * 3,
-        out_specs=here,
-        compiler_params=pltpu.CompilerParams(vmem_limit_bytes=24 << 20),
-        name="sort_tokens",
-    )(queries, order, extra)
+        name="prepare",
+    )(counts, image_range, keys, values, queries)
 
 
 def work_list(wanted):
@@ -268,7 +291,7 @@
     return items.astype(jnp.int32), count.reshape(1)
 
 
-def combined(order_ref, parts, out_ref, hd, group):
+def combined(back_ref, parts, out_ref, hd, group):
     width = group * hd
     sums = []
     for ref in parts:
@@ -283,10 +306,9 @@
         mixed = parts[0][:, at].astype(F32) * shares[0][:, h : h + 1]
         for ref, share in zip(parts[1:], shares[1:]):
             mixed = mixed + ref[:, at].astype(F32) * share[:, h : h + 1]
-        placed = lax.dot_general(
-            order_ref[...], mixed.astype(BF16), (((0,), (0,)), ((), ())), preferred_element_type=F32
-        )
-        out_ref[:, at] = placed.astype(BF16)
+        out_ref[:, at] = mixed.astype(BF16)
+    placed = jnp.dot(back_ref[...], out_ref[...], preferred_element_type=F32)
+    out_ref[...] = placed.astype(BF16)
 
 
 def project_kernel(columns, *refs, hd, group, pieces, merge):
@@ -405,36 +427,17 @@
     nz, nyh = (lax.axis_size(n) for n in HEAD)
 
     padded = -(-keys // 128) * 128
-    own = pack(image_keys, image_values, padded)
+    own, payload, back = prepare(
+        tile_counts, image_range, image_keys, image_values, queries, padded
+    )
     across = shifted(own, "y", 1)
-    beside = shifted(own, "core", 1)
-    low, high = image_range[0], image_range[1]
-    grade = jnp.where(low < high, low * 16 + high, 1 << 10)
-    place = jnp.arange(tokens, dtype=jnp.int32)
-    ahead = (grade[None, :] < grade[:, None]) | (
-        (grade[None, :] == grade[:, None]) & (place[None, :] < place[:, None])
-    )
-    rank = jnp.sum(ahead.astype(jnp.int32), axis=1)
-    order = (rank[None, :] == place[:, None]).astype(BF16)
     image = jnp.arange(tile_counts.shape[0])
     ends = jnp.sum(jnp.where(image[None, :] <= image[:, None], tile_counts[None, :], 0), axis=1)
     tile = jnp.arange(ny * nx * nc, dtype=jnp.int32)
     owner = jnp.sum((ends[None, :] <= tile[:, None]).astype(jnp.int32), axis=1)
-    hits = (low[:, None] <= owner[None, :]) & (owner[None, :] < high[:, None])
-    same = (place[:, None] // CHUNK == rank[None, :] // CHUNK).astype(BF16)
-    live = jnp.dot(same, hits.astype(BF16), preferred_element_type=F32) > 0
-    span = jnp.dot(order, image_range.astype(BF16).T, preferred_element_type=F32)
-    extra = jnp.concatenate(
-        [
-            jnp.pad(span, ((0, 0), (0, 14))),
-            jnp.pad(live.astype(F32), ((0, 0), (0, hd - 16 - tile.shape[0]))),
-        ],
-        axis=1,
-    )
-    payload = sort_tokens(queries, order, extra)
-    payload, beside = lax.optimization_barrier((payload, beside))
     payloads = {s: shifted(payload, "x", s) for s in (2, 1, 3)}
     payloads[0] = payload
+    beside = shifted(own, "core", 1)
     diagonal = shifted(across, "core", 1)
     tiles = (own, beside, across, diagonal)
 
@@ -470,7 +473,7 @@
     def first(dz, dy):
         return ((z + dz) % nz * nyh + (yh + dy) % nyh) * 2
 
-    sources = [order] + [parts[s] for s in (2, 1, 3, 0)]
+    sources = [back] + [parts[s] for s in (2, 1, 3, 0)]
     over_y, attended = project(
         sources, out_weight, [first(dz, 1) + 1 for dz in (1, 2, 3, 0)], (4,), half, hd
     )

time: 129 us -> 129 us (level)
  the two profiles are of different devices: /device:TPU:63 before, /device:TPU:49 now
where the time goes in v6:
time: 129 us; the launch traced here: 127 us
  waiting for transfers between devices  50.2 us (39%)
  Pallas kernels  46.8 us (36%)
  starting transfers between devices  23.1 us (18%)
  other arithmetic  3.57 us (3%)
  local copies, waits for them, and re-layouts  2.87 us (2%)
    ppermute x17, waiting for transfers between devices, shifted(): lax.ppermute(value, axis, [(s, (s + steps) % count) for s in range(count)])  50.2 us
    pallas_call x2, Pallas kernels, attend(): pl.pallas_call(lambda *refs: attend_kernel(*refs, scale=1.0 / math.sqrt(h...  25.9 us
    ppermute x17, starting transfers between devices, shifted(): lax.ppermute(value, axis, [(s, (s + steps) % count) for s in range(count)])  23.1 us
    pallas_call x4, Pallas kernels, project(): pl.pallas_call(lambda *refs: project_kernel(*refs, hd=hd, group=depth //...  16.2 us
    pallas_call x1, Pallas kernels, prepare(): pl.pallas_call(prepare_kernel, out_shape=[jax.ShapeDtypeStruct((2 * hd, p...  3.36 us
  transfers between devices with their start and end apart: 17, of which 13 were waited for; matrix products, arithmetic and copies ran while one was open for 4% of the time, Pallas kernels for 13%

profile of v6, /device:TPU:49, one launch (start us, length us, event | category | flops | bytes accessed | tf_op | source)
XLA Modules:
  0.0 127.3 jit_solution(303533621667842977)
XLA Ops:
  0.0 3.4 %prepare.1 = (bf16[256,1664]{1,0:T(8,128)(2,1)}, bf16[192,1152]{1,0:T(8,128)(2,1)}, bf16[192,192]{1,0:T(8,128)(2,1)}) custom-call(s32[8]{0:T(128)} %counts.1, s32[2,192]{1,0:T(2,128)} %range_ref.1, bf16[1601,128]{1,0:T(8,128)(2,1)} %key_hbm.1, bf16[1601,128]{1,0:T(8,128)(2,1)} %value_hbm.1, bf16[192,1024]{1,0:T(8,128)(2,1)} %q_hbm.1), custom_call_target="tpu_custom_call" | custom-call | tf_op jit(solution)/shard_map/prepare/pallas_call | solution.py:259
  3.4 2.8 %collective-permute-start = (bf16[192,1152]{1,0:T(8,128)(2,1)}, bf16[192,1152]{1,0:T(8,128)(2,1)S(1)}, u32[]{:S(2)}, u32[]{:S(2)}) collective-permute-start(bf16[192,1152]{1,0:T(8,128)(2,1)} %get-tuple-element.23.refs_3_), channel_id=1, source_target_pairs={{0,32},{16,48},{32,0},{48,16},{1,33},{17,49},{33,1},{49,17},{2,34}... | collective-permute-start | bytes 1327112 | tf_op jit(solution)/shard_map/ppermute | solution.py:23
  6.5 2.4 %collective-permute-start.2 = (bf16[192,1152]{1,0:T(8,128)(2,1)}, bf16[192,1152]{1,0:T(8,128)(2,1)S(1)}, u32[]{:S(2)}, u32[]{:S(2)}) collective-permute-start(bf16[192,1152]{1,0:T(8,128)(2,1)} %get-tuple-element.23.refs_3_), channel_id=1, source_target_pairs={{0,48},{16,0},{32,16},{48,32},{1,49},{17,1},{33,17},{49,33},{2,50}... | collective-permute-start | bytes 1327112 | tf_op jit(solution)/shard_map/ppermute | solution.py:23
  9.9 1.8 %collective-permute-start.3 = (bf16[256,1664]{1,0:T(8,128)(2,1)}, bf16[256,1664]{1,0:T(8,128)(2,1)S(1)}, u32[]{:S(2)}, u32[]{:S(2)}) collective-permute-start(bf16[256,1664]{1,0:T(8,128)(2,1)} %get-tuple-element.24.refs_6_.refs_4_), channel_id=1, source_target_pairs={{0,8},{8,0},{1,9},{9,1},{2,10},{10,2},{3,11},{11,3},{4,12},{12,4},... | collective-permute-start | bytes 2555912 | tf_op jit(solution)/shard_map/ppermute | solution.py:23
  16.4 10.4 %collective-permute-done.1.refs_4_ = bf16[192,1152]{1,0:T(8,128)(2,1)S(1)} collective-permute-done((bf16[192,1152]{1,0:T(8,128)(2,1)}, bf16[192,1152]{1,0:T(8,128)(2,1)S(1)}, u32[]{:S(2)}, u32[]{:S(2)}) %collective-permute-start.1) | collective-permute-done | bytes 442400 | tf_op jit(solution)/shard_map/ppermute | solution.py:23
  28.0 2.4 %collective-permute-start.5 = (bf16[256,1664]{1,0:T(8,128)(2,1)S(1)}, bf16[256,1664]{1,0:T(8,128)(2,1)}, u32[]{:S(2)}, u32[]{:S(2)}) collective-permute-start(bf16[256,1664]{1,0:T(8,128)(2,1)S(1)} %collective-permute-done.4.refs_8_.refs_6_), channel_id=1, source_target_pairs={{0,8},{8,0},{1,9},{9,1},{2,10},{10,2},{3,11},{11,3},{4,12},{12,4},... | collective-permute-start | bytes 2555912 | tf_op jit(solution)/shard_map/ppermute | solution.py:23
  33.7 20.9 %attend.2 = (bf16[192,1152]{1,0:T(8,128)(2,1)S(1)}, bf16[192,1152]{1,0:T(8,128)(2,1)S(1)}, bf16[192,1152]{1,0:T(8,128)(2,1)S(1)}) custom-call(s32[75]{0:T(128)S(1)} %compare_select_fusion.1.refs_0_, s32[1]{0:T(128)} %bitcast.14.refs_1_, s32[4]{0:T(128)S(1)} %select_reduce_fusion.3.refs_2_, bf16[192,1152]{1,0:T(8,128)(2,1)S(1)} %collective-permute-done.refs_3_, ...), custom_call_target="tpu_custom_call" | custom-call | flops 3925868544 | bytes 5767168 | tf_op jit(solution)/shard_map/attend/pallas_call | solution.py:149
  54.9 1.5 %collective-permute-start.8 = (bf16[192,1152]{1,0:T(8,128)(2,1)S(1)}, bf16[192,1152]{1,0:T(8,128)(2,1)S(1)}, u32[]{:S(2)}, u32[]{:S(2)}) collective-permute-start(bf16[192,1152]{1,0:T(8,128)(2,1)S(1)} %get-tuple-element.27), channel_id=1, source_target_pairs={{0,16},{16,32},{32,48},{48,0},{1,17},{17,33},{33,49},{49,1},{2,18}... | collective-permute-start | bytes 1327112 | tf_op jit(solution)/shard_map/ppermute | solution.py:23
  56.4 5.0 %attend.3.refs_5_ = bf16[192,1152]{1,0:T(8,128)(2,1)S(1)} custom-call(s32[27]{0:T(128)S(1)} %compare_select_fusion.refs_0_, s32[1]{0:T(128)} %bitcast.15.refs_1_, s32[4]{0:T(128)S(1)} %select_reduce_fusion.3.refs_2_, bf16[192,1152]{1,0:T(8,128)(2,1)S(1)} %copy-done.2, bf16[256,1664]{1,0:T(8,128)(2,1)S(1)} %copy-done.3, ...), custom_call_target="tpu_custom_call" | custom-call | flops 1308622848 | bytes 4194304 | tf_op jit(solution)/shard_map/attend/pallas_call | solution.py:149
  61.4 6.4 %collective-permute-done.6.refs_2_ = bf16[192,1152]{1,0:T(8,128)(2,1)S(1)} collective-permute-done((bf16[192,1152]{1,0:T(8,128)(2,1)S(1)}, bf16[192,1152]{1,0:T(8,128)(2,1)S(1)}, u32[]{:S(2)}, u32[]{:S(2)}) %collective-permute-start.6) | collective-permute-done | bytes 442400 | tf_op jit(solution)/shard_map/ppermute | solution.py:23
  67.8 1.3 %collective-permute-done.7.refs_3_ = bf16[192,1152]{1,0:T(8,128)(2,1)S(1)} collective-permute-done((bf16[192,1152]{1,0:T(8,128)(2,1)S(1)}, bf16[192,1152]{1,0:T(8,128)(2,1)S(1)}, u32[]{:S(2)}, u32[]{:S(2)}) %collective-permute-start.7) | collective-permute-done | bytes 442400 | tf_op jit(solution)/shard_map/ppermute | solution.py:23
  69.1 8.8 %collective-permute-done.8.refs_4_ = bf16[192,1152]{1,0:T(8,128)(2,1)S(1)} collective-permute-done((bf16[192,1152]{1,0:T(8,128)(2,1)S(1)}, bf16[192,1152]{1,0:T(8,128)(2,1)S(1)}, u32[]{:S(2)}, u32[]{:S(2)}) %collective-permute-start.8) | collective-permute-done | bytes 442400 | tf_op jit(solution)/shard_map/ppermute | solution.py:23
  77.8 5.5 %project.4 = (bf16[192,2048]{1,0:T(8,128)(2,1)}, bf16[192,1024]{1,0:T(8,128)(2,1)S(1)}) custom-call(s32[4]{0:T(128)S(1)} %pad_add_fusion.refs_0_, bf16[192,192]{1,0:T(8,128)(2,1)S(1)} %copy-done.1, bf16[192,1152]{1,0:T(8,128)(2,1)S(1)} %collective-permute-done.6.refs_2_, bf16[192,1152]{1,0:T(8,128)(2,1)S(1)} %collective-permute-done.7.refs_3_, ...), custom_call_target="tpu_custom_call" | custom-call | flops 805306368 | bytes 8388608 | tf_op jit(solution)/shard_map/project/pallas_call | solution.py:348
  83.6 4.1 %project.7 = (bf16[192,1024]{1,0:T(8,128)(2,1)S(1)}, bf16[192,1024]{1,0:T(8,128)(2,1)}) custom-call(s32[4]{0:T(128)S(1)} %pad_add_fusion.3.refs_0_, bf16[192,1024]{1,0:T(8,128)(2,1)S(1)} %get-tuple-element.29.refs_1_, bf16[1024,8192]{1,0:T(8,128)(2,1)} %refs_2_.5), custom_call_target="tpu_custom_call" | custom-call | flops 805306368 | bytes 8388608 | tf_op jit(solution)/shard_map/project/pallas_call | solution.py:348
  87.7 1.7 %collective-permute-start.10 = (bf16[192,1024]{1,0:T(8,128)(2,1)}, bf16[192,1024]{1,0:T(8,128)(2,1)S(1)}, u32[]{:S(2)}, u32[]{:S(2)}) collective-permute-start(bf16[192,1024]{1,0:T(8,128)(2,1)} %get-tuple-element.31), channel_id=1, source_target_pairs={{0,2},{2,4},{4,6},{6,0},{1,3},{3,5},{5,7},{7,1},{8,10},{10,12},{12... | collective-permute-start | bytes 1179656 | tf_op jit(solution)/shard_map/ppermute | solution.py:23
  90.6 2.6 %project.6 = bf16[192,1024]{1,0:T(8,128)(2,1)S(1)} custom-call(s32[2]{0:T(128)S(1)} %pad_add_fusion.2.refs_0_, bf16[192,1024]{1,0:T(8,128)(2,1)S(1)} %get-tuple-element.29.refs_1_, bf16[1024,8192]{1,0:T(8,128)(2,1)} %refs_2_.5), custom_call_target="tpu_custom_call" | custom-call | flops 402653184 | bytes 4194304 | tf_op jit(solution)/shard_map/project/pallas_call | solution.py:348
  93.1 2.0 %collective-permute-start.9 = (bf16[192,1024]{1,0:T(8,128)(2,1)S(1)}, bf16[192,1024]{1,0:T(8,128)(2,1)S(1)}, u32[]{:S(2)}, u32[]{:S(2)}) collective-permute-start(bf16[192,1024]{1,0:T(8,128)(2,1)S(1)} %project.6), channel_id=1, source_target_pairs={{0,6},{2,0},{4,2},{6,4},{1,7},{3,1},{5,3},{7,5},{8,14},{10,8},{12,... | collective-permute-start | bytes 1179656 | tf_op jit(solution)/shard_map/ppermute | solution.py:23
  95.3 4.1 %project.5 = (bf16[192,1024]{1,0:T(8,128)(2,1)S(1)}, bf16[192,2048]{1,0:T(8,128)(2,1)S(1)}) custom-call(s32[6]{0:T(128)S(1)} %stack.81.refs_0_, bf16[192,1024]{1,0:T(8,128)(2,1)S(1)} %get-tuple-element.29.refs_1_, bf16[1024,8192]{1,0:T(8,128)(2,1)} %refs_2_.5), custom_call_target="tpu_custom_call" | custom-call | flops 1207959552 | bytes 12582912 | tf_op jit(solution)/shard_map/project/pallas_call | solution.py:348
  100.6 9.8 %collective-permute-done.9.refs_1_ = bf16[192,1024]{1,0:T(8,128)(2,1)S(1)} collective-permute-done((bf16[192,1024]{1,0:T(8,128)(2,1)S(1)}, bf16[192,1024]{1,0:T(8,128)(2,1)S(1)}, u32[]{:S(2)}, u32[]{:S(2)}) %collective-permute-start.9) | collective-permute-done | bytes 393248 | tf_op jit(solution)/shard_map/ppermute | solution.py:23
  110.6 3.0 %collective-permute-start.12 = (bf16[192,512]{1,0:T(8,128)(2,1)S(1)}, bf16[192,512]{1,0:T(8,128)(2,1)S(1)}, u32[]{:S(2)}, u32[]{:S(2)}) collective-permute-start(bf16[192,512]{1,0:T(8,128)(2,1)S(1)} %get-tuple-element.34), channel_id=1, source_target_pairs={{0,1},{1,0},{2,3},{3,2},{4,5},{5,4},{6,7},{7,6},{8,9},{9,8},{10,11... | collective-permute-start | bytes 589832 | tf_op jit(solution)/shard_map/ppermute | solution.py:23
  115.0 1.5 %collective-permute-start.16 = (bf16[192,512]{1,0:T(8,128)(2,1)S(1)}, bf16[192,512]{1,0:T(8,128)(2,1)S(1)}, u32[]{:S(2)}, u32[]{:S(2)}) collective-permute-start(bf16[192,512]{1,0:T(8,128)(2,1)S(1)} %get-tuple-element.43), channel_id=1, source_target_pairs={{0,6},{2,0},{4,2},{6,4},{1,7},{3,1},{5,3},{7,5},{8,14},{10,8},{12,... | collective-permute-start | bytes 589832 | tf_op jit(solution)/shard_map/ppermute | solution.py:23
  118.1 2.9 %collective-permute-done.14.refs_3_ = bf16[192,512]{1,0:T(8,128)(2,1)S(1)} collective-permute-done((bf16[192,512]{1,0:T(8,128)(2,1)S(1)}, bf16[192,512]{1,0:T(8,128)(2,1)S(1)}, u32[]{:S(2)}, u32[]{:S(2)}) %collective-permute-start.14) | collective-permute-done | bytes 196640 | tf_op jit(solution)/shard_map/ppermute | solution.py:23
  121.1 2.3 %collective-permute-done.15.refs_4_ = bf16[192,512]{1,0:T(8,128)(2,1)S(1)} collective-permute-done((bf16[192,512]{1,0:T(8,128)(2,1)S(1)}, bf16[192,512]{1,0:T(8,128)(2,1)S(1)}, u32[]{:S(2)}, u32[]{:S(2)}) %collective-permute-start.15) | collective-permute-done | bytes 196640 | tf_op jit(solution)/shard_map/ppermute | solution.py:23
  123.4 3.0 %collective-permute-done.16.refs_5_ = bf16[192,512]{1,0:T(8,128)(2,1)S(1)} collective-permute-done((bf16[192,512]{1,0:T(8,128)(2,1)S(1)}, bf16[192,512]{1,0:T(8,128)(2,1)S(1)}, u32[]{:S(2)}, u32[]{:S(2)}) %collective-permute-start.16) | collective-permute-done | bytes 196640 | tf_op jit(solution)/shard_map/ppermute | solution.py:23
  (60 shorter events, 17.0 us)
Async XLA Ops:
  3.4 53.0 %copy-start.2 = (bf16[192,1152]{1,0:T(8,128)(2,1)S(1)}, bf16[192,1152]{1,0:T(8,128)(2,1)}, u32[]{:S(2)}) copy-start(bf16[192,1152]{1,0:T(8,128)(2,1)} %get-tuple-element.23.refs_3_) | copy-start | bytes 1327108
  3.4 12.9 %collective-permute-start = (bf16[192,1152]{1,0:T(8,128)(2,1)}, bf16[192,1152]{1,0:T(8,128)(2,1)S(1)}, u32[]{:S(2)}, u32[]{:S(2)}) collective-permute-start(bf16[192,1152]{1,0:T(8,128)(2,1)} %get-tuple-element.23.refs_3_), channel_id=1, source_target_pairs={{0,32},{16,48},{32,0},{48,16},{1,33},{17,49},{33,1},{49,17},{2,34}... | collective-permute-start | bytes 1327112 | tf_op jit(solution)/shard_map/ppermute | solution.py:23
  6.2 20.5 %collective-permute-start.1 = (bf16[192,1152]{1,0:T(8,128)(2,1)}, bf16[192,1152]{1,0:T(8,128)(2,1)S(1)}, u32[]{:S(2)}, u32[]{:S(2)}) collective-permute-start(bf16[192,1152]{1,0:T(8,128)(2,1)} %get-tuple-element.23.refs_3_), channel_id=1, source_target_pairs={{0,16},{16,32},{32,48},{48,0},{1,17},{17,33},{33,49},{49,1},{2,18}... | collective-permute-start | bytes 1327112 | tf_op jit(solution)/shard_map/ppermute | solution.py:23
  6.5 20.3 %collective-permute-start.2 = (bf16[192,1152]{1,0:T(8,128)(2,1)}, bf16[192,1152]{1,0:T(8,128)(2,1)S(1)}, u32[]{:S(2)}, u32[]{:S(2)}) collective-permute-start(bf16[192,1152]{1,0:T(8,128)(2,1)} %get-tuple-element.23.refs_3_), channel_id=1, source_target_pairs={{0,48},{16,0},{32,16},{48,32},{1,49},{17,1},{33,17},{49,33},{2,50}... | collective-permute-start | bytes 1327112 | tf_op jit(solution)/shard_map/ppermute | solution.py:23
  8.9 19.1 %collective-permute-start.4 = (bf16[256,1664]{1,0:T(8,128)(2,1)}, bf16[256,1664]{1,0:T(8,128)(2,1)S(1)}, u32[]{:S(2)}, u32[]{:S(2)}) collective-permute-start(bf16[256,1664]{1,0:T(8,128)(2,1)} %get-tuple-element.24.refs_6_.refs_4_), channel_id=1, source_target_pairs={{0,64},{64,0},{1,65},{65,1},{2,66},{66,2},{3,67},{67,3},{4,68},{68... | collective-permute-start | bytes 2555912 | tf_op jit(solution)/shard_map/ppermute | solution.py:23
  9.9 21.9 %collective-permute-start.3 = (bf16[256,1664]{1,0:T(8,128)(2,1)}, bf16[256,1664]{1,0:T(8,128)(2,1)S(1)}, u32[]{:S(2)}, u32[]{:S(2)}) collective-permute-start(bf16[256,1664]{1,0:T(8,128)(2,1)} %get-tuple-element.24.refs_6_.refs_4_), channel_id=1, source_target_pairs={{0,8},{8,0},{1,9},{9,1},{2,10},{10,2},{3,11},{11,3},{4,12},{12,4},... | collective-permute-start | bytes 2555912 | tf_op jit(solution)/shard_map/ppermute | solution.py:23
  28.0 4.6 %collective-permute-start.5 = (bf16[256,1664]{1,0:T(8,128)(2,1)S(1)}, bf16[256,1664]{1,0:T(8,128)(2,1)}, u32[]{:S(2)}, u32[]{:S(2)}) collective-permute-start(bf16[256,1664]{1,0:T(8,128)(2,1)S(1)} %collective-permute-done.4.refs_8_.refs_6_), channel_id=1, source_target_pairs={{0,8},{8,0},{1,9},{9,1},{2,10},{10,2},{3,11},{11,3},{4,12},{12,4},... | collective-permute-start | bytes 2555912 | tf_op jit(solution)/shard_map/ppermute | solution.py:23
  32.6 1.2 copy-start.3
  33.7 44.1 %copy-start.1 = (bf16[192,192]{1,0:T(8,128)(2,1)S(1)}, bf16[192,192]{1,0:T(8,128)(2,1)}, u32[]{:S(2)}) copy-start(bf16[192,192]{1,0:T(8,128)(2,1)} %get-tuple-element.22.refs_1_) | copy-start | bytes 221188
  54.7 13.1 %collective-permute-start.6 = (bf16[192,1152]{1,0:T(8,128)(2,1)S(1)}, bf16[192,1152]{1,0:T(8,128)(2,1)S(1)}, u32[]{:S(2)}, u32[]{:S(2)}) collective-permute-start(bf16[192,1152]{1,0:T(8,128)(2,1)S(1)} %get-tuple-element.25), channel_id=1, source_target_pairs={{0,32},{16,48},{32,0},{48,16},{1,33},{17,49},{33,1},{49,17},{2,34}... | collective-permute-start | bytes 1327112 | tf_op jit(solution)/shard_map/ppermute | solution.py:23
  54.8 14.3 %collective-permute-start.7 = (bf16[192,1152]{1,0:T(8,128)(2,1)S(1)}, bf16[192,1152]{1,0:T(8,128)(2,1)S(1)}, u32[]{:S(2)}, u32[]{:S(2)}) collective-permute-start(bf16[192,1152]{1,0:T(8,128)(2,1)S(1)} %get-tuple-element.26), channel_id=1, source_target_pairs={{0,48},{16,0},{32,16},{48,32},{1,49},{17,1},{33,17},{49,33},{2,50}... | collective-permute-start | bytes 1327112 | tf_op jit(solution)/shard_map/ppermute | solution.py:23
  54.9 23.0 %collective-permute-start.8 = (bf16[192,1152]{1,0:T(8,128)(2,1)S(1)}, bf16[192,1152]{1,0:T(8,128)(2,1)S(1)}, u32[]{:S(2)}, u32[]{:S(2)}) collective-permute-start(bf16[192,1152]{1,0:T(8,128)(2,1)S(1)} %get-tuple-element.27), channel_id=1, source_target_pairs={{0,16},{16,32},{32,48},{48,0},{1,17},{17,33},{33,49},{49,1},{2,18}... | collective-permute-start | bytes 1327112 | tf_op jit(solution)/shard_map/ppermute | solution.py:23
  83.3 30.2 %collective-permute-start.13 = (bf16[192,2048]{1,0:T(8,128)(2,1)}, bf16[192,2048]{1,0:T(8,128)(2,1)S(1)}, u32[]{:S(2)}, u32[]{:S(2)}) collective-permute-start(bf16[192,2048]{1,0:T(8,128)(2,1)} %get-tuple-element.36), channel_id=1, source_target_pairs={{0,1},{1,0},{2,3},{3,2},{4,5},{5,4},{6,7},{7,6},{8,9},{9,8},{10,11... | collective-permute-start | bytes 2359304 | tf_op jit(solution)/shard_map/ppermute | solution.py:23
  87.7 11.7 %collective-permute-start.10 = (bf16[192,1024]{1,0:T(8,128)(2,1)}, bf16[192,1024]{1,0:T(8,128)(2,1)S(1)}, u32[]{:S(2)}, u32[]{:S(2)}) collective-permute-start(bf16[192,1024]{1,0:T(8,128)(2,1)} %get-tuple-element.31), channel_id=1, source_target_pairs={{0,2},{2,4},{4,6},{6,0},{1,3},{3,5},{5,7},{7,1},{8,10},{10,12},{12... | collective-permute-start | bytes 1179656 | tf_op jit(solution)/shard_map/ppermute | solution.py:23
  89.4 37.0 %copy-start = (bf16[192,1024]{1,0:T(8,128)(2,1)S(1)}, bf16[192,1024]{1,0:T(8,128)(2,1)}, u32[]{:S(2)}) copy-start(bf16[192,1024]{1,0:T(8,128)(2,1)} %layer_ref.1) | copy-start | bytes 1179652
  89.4 11.2 %collective-permute-start.11 = (bf16[192,1024]{1,0:T(8,128)(2,1)S(1)}, bf16[192,1024]{1,0:T(8,128)(2,1)S(1)}, u32[]{:S(2)}, u32[]{:S(2)}) collective-permute-start(bf16[192,1024]{1,0:T(8,128)(2,1)S(1)} %get-tuple-element.32), channel_id=1, source_target_pairs={{0,4},{2,6},{4,0},{6,2},{1,5},{3,7},{5,1},{7,3},{8,12},{10,14},{12... | collective-permute-start | bytes 1179656 | tf_op jit(solution)/shard_map/ppermute | solution.py:23
  93.1 17.3 %collective-permute-start.9 = (bf16[192,1024]{1,0:T(8,128)(2,1)S(1)}, bf16[192,1024]{1,0:T(8,128)(2,1)S(1)}, u32[]{:S(2)}, u32[]{:S(2)}) collective-permute-start(bf16[192,1024]{1,0:T(8,128)(2,1)S(1)} %project.6), channel_id=1, source_target_pairs={{0,6},{2,0},{4,2},{6,4},{1,7},{3,1},{5,3},{7,5},{8,14},{10,8},{12,... | collective-permute-start | bytes 1179656 | tf_op jit(solution)/shard_map/ppermute | solution.py:23
  110.6 7.6 %collective-permute-start.12 = (bf16[192,512]{1,0:T(8,128)(2,1)S(1)}, bf16[192,512]{1,0:T(8,128)(2,1)S(1)}, u32[]{:S(2)}, u32[]{:S(2)}) collective-permute-start(bf16[192,512]{1,0:T(8,128)(2,1)S(1)} %get-tuple-element.34), channel_id=1, source_target_pairs={{0,1},{1,0},{2,3},{3,2},{4,5},{5,4},{6,7},{7,6},{8,9},{9,8},{10,11... | collective-permute-start | bytes 589832 | tf_op jit(solution)/shard_map/ppermute | solution.py:23
  113.8 7.3 %collective-permute-start.14 = (bf16[192,512]{1,0:T(8,128)(2,1)S(1)}, bf16[192,512]{1,0:T(8,128)(2,1)S(1)}, u32[]{:S(2)}, u32[]{:S(2)}) collective-permute-start(bf16[192,512]{1,0:T(8,128)(2,1)S(1)} %get-tuple-element.45), channel_id=1, source_target_pairs={{0,4},{2,6},{4,0},{6,2},{1,5},{3,7},{5,1},{7,3},{8,12},{10,14},{12... | collective-permute-start | bytes 589832 | tf_op jit(solution)/shard_map/ppermute | solution.py:23
  115.0 8.4 %collective-permute-start.15 = (bf16[192,512]{1,0:T(8,128)(2,1)S(1)}, bf16[192,512]{1,0:T(8,128)(2,1)S(1)}, u32[]{:S(2)}, u32[]{:S(2)}) collective-permute-start(bf16[192,512]{1,0:T(8,128)(2,1)S(1)} %get-tuple-element.44), channel_id=1, source_target_pairs={{0,2},{2,4},{4,6},{6,0},{1,3},{3,5},{5,7},{7,1},{8,10},{10,12},{12... | collective-permute-start | bytes 589832 | tf_op jit(solution)/shard_map/ppermute | solution.py:23
  115.0 11.4 %collective-permute-start.16 = (bf16[192,512]{1,0:T(8,128)(2,1)S(1)}, bf16[192,512]{1,0:T(8,128)(2,1)S(1)}, u32[]{:S(2)}, u32[]{:S(2)}) collective-permute-start(bf16[192,512]{1,0:T(8,128)(2,1)S(1)} %get-tuple-element.43), channel_id=1, source_target_pairs={{0,6},{2,0},{4,2},{6,4},{1,7},{3,1},{5,3},{7,5},{8,14},{10,8},{12,... | collective-permute-start | bytes 589832 | tf_op jit(solution)/shard_map/ppermute | solution.py:23

commit v7 on v6

--- a/solution.py
+++ b/solution.py
@@ -11,7 +11,7 @@
 SEQ = ("y", "x", "core")
 HEAD = ("z", "yh")
 CHUNK = 32
-GROUPS = ((2, 1, 3), (0,))
+GROUPS = ((2,), (1, 3), (0,))
 LOWEST = -1e30
 BLOCKED = 1e30
 BF16 = jnp.bfloat16
@@ -478,11 +478,9 @@
         sources, out_weight, [first(dz, 1) + 1 for dz in (1, 2, 3, 0)], (4,), half, hd
     )
     got_y = shifted(over_y, "yh", 1)
-    far = [first(dz, dy) for dz in (2, 1) for dy in (1, 0)]
-    over_z = project([attended], out_weight, far, (2, 2), half, hd)
-    got_z = [shifted(term, "z", dz) for dz, term in zip((2, 1), over_z)]
-    (last_z,) = project([attended], out_weight, [first(3, 1), first(3, 0)], (2,), half, hd)
-    got_z.append(shifted(last_z, "z", 3))
+    far = [first(dz, dy) for dz in (2, 1, 3) for dy in (1, 0)]
+    over_z = project([attended], out_weight, far, (2, 2, 2), half, hd)
+    got_z = [shifted(term, "z", dz) for dz, term in zip((2, 1, 3), over_z)]
     near = [first(0, 1), first(0, 0)] + [first(dz, 0) + 1 for dz in (1, 2, 3, 0)]
     own_z, own_y = project([attended], out_weight, near, (2, 4), half, hd)
     late_z, kept_b = add_up([own_y, got_y], half)

time: 129 us -> 127 us (0.984)
  the two profiles are of different devices: /device:TPU:49 before, /device:TPU:1 now
where the time goes in v7:
time: 127 us
  Pallas kernels  57.1 us (45%)
  waiting for transfers between devices  32.6 us (26%)
  starting transfers between devices  29.8 us (23%)
  other arithmetic  3.74 us (3%)
  local copies, waits for them, and re-layouts  2.84 us (2%)
    pallas_call x3, Pallas kernels, attend(): pl.pallas_call(lambda *refs: attend_kernel(*refs, scale=1.0 / math.sqrt(h...  38.8 us
    ppermute x17, waiting for transfers between devices, shifted(): lax.ppermute(value, axis, [(s, (s + steps) % count) for s in range(count)])  32.6 us
    ppermute x17, starting transfers between devices, shifted(): lax.ppermute(value, axis, [(s, (s + steps) % count) for s in range(count)])  29.8 us
    pallas_call x3, Pallas kernels, project(): pl.pallas_call(lambda *refs: project_kernel(*refs, hd=hd, group=depth //...  13.6 us
    pallas_call x1, Pallas kernels, prepare(): pl.pallas_call(prepare_kernel, out_shape=[jax.ShapeDtypeStruct((2 * hd, p...  3.36 us
  transfers between devices with their start and end apart: 17, of which 7 were waited for; matrix products, arithmetic and copies ran while one was open for 4% of the time, Pallas kernels for 28%

profile of v7, /device:TPU:1, one launch (start us, length us, event | category | flops | bytes accessed | tf_op | source)
XLA Modules:
  0.0 127.1 jit_solution(8334479111975325640)
XLA Ops:
  0.0 3.4 %prepare.1 = (bf16[256,1664]{1,0:T(8,128)(2,1)}, bf16[192,1152]{1,0:T(8,128)(2,1)}, bf16[192,192]{1,0:T(8,128)(2,1)}) custom-call(s32[8]{0:T(128)} %counts.1, s32[2,192]{1,0:T(2,128)} %range_ref.1, bf16[1601,128]{1,0:T(8,128)(2,1)} %key_hbm.1, bf16[1601,128]{1,0:T(8,128)(2,1)} %value_hbm.1, bf16[192,1024]{1,0:T(8,128)(2,1)} %q_hbm.1), custom_call_target="tpu_custom_call" | custom-call | tf_op jit(solution)/shard_map/prepare/pallas_call | solution.py:259
  3.4 2.1 %collective-permute-start.5 = (bf16[192,1152]{1,0:T(8,128)(2,1)}, bf16[192,1152]{1,0:T(8,128)(2,1)S(1)}, u32[]{:S(2)}, u32[]{:S(2)}) collective-permute-start(bf16[192,1152]{1,0:T(8,128)(2,1)} %get-tuple-element.24.refs_3_), channel_id=1, source_target_pairs={{0,16},{16,32},{32,48},{48,0},{1,17},{17,33},{33,49},{49,1},{2,18}... | collective-permute-start | bytes 1327112 | tf_op jit(solution)/shard_map/ppermute | solution.py:23
  5.5 1.4 %collective-permute-start.6 = (bf16[192,1152]{1,0:T(8,128)(2,1)}, bf16[192,1152]{1,0:T(8,128)(2,1)S(1)}, u32[]{:S(2)}, u32[]{:S(2)}) collective-permute-start(bf16[192,1152]{1,0:T(8,128)(2,1)} %get-tuple-element.24.refs_3_), channel_id=1, source_target_pairs={{0,48},{16,0},{32,16},{48,32},{1,49},{17,1},{33,17},{49,33},{2,50}... | collective-permute-start | bytes 1327112 | tf_op jit(solution)/shard_map/ppermute | solution.py:23
  6.8 1.6 %collective-permute-start = (bf16[192,1152]{1,0:T(8,128)(2,1)}, bf16[192,1152]{1,0:T(8,128)(2,1)S(1)}, u32[]{:S(2)}, u32[]{:S(2)}) collective-permute-start(bf16[192,1152]{1,0:T(8,128)(2,1)} %get-tuple-element.24.refs_3_), channel_id=1, source_target_pairs={{0,32},{16,48},{32,0},{48,16},{1,33},{17,49},{33,1},{49,17},{2,34}... | collective-permute-start | bytes 1327112 | tf_op jit(solution)/shard_map/ppermute | solution.py:23
  9.8 1.8 %collective-permute-start.1 = (bf16[256,1664]{1,0:T(8,128)(2,1)}, bf16[256,1664]{1,0:T(8,128)(2,1)S(1)}, u32[]{:S(2)}, u32[]{:S(2)}) collective-permute-start(bf16[256,1664]{1,0:T(8,128)(2,1)} %get-tuple-element.25.refs_4_.refs_5_), channel_id=1, source_target_pairs={{0,8},{8,0},{1,9},{9,1},{2,10},{10,2},{3,11},{11,3},{4,12},{12,4},... | collective-permute-start | bytes 2555912 | tf_op jit(solution)/shard_map/ppermute | solution.py:23
  13.7 13.5 %collective-permute-done.refs_3_ = bf16[192,1152]{1,0:T(8,128)(2,1)S(1)} collective-permute-done((bf16[192,1152]{1,0:T(8,128)(2,1)}, bf16[192,1152]{1,0:T(8,128)(2,1)S(1)}, u32[]{:S(2)}, u32[]{:S(2)}) %collective-permute-start) | collective-permute-done | bytes 442400 | tf_op jit(solution)/shard_map/ppermute | solution.py:23
  29.7 1.5 %collective-permute-start.3 = (bf16[256,1664]{1,0:T(8,128)(2,1)S(1)}, bf16[256,1664]{1,0:T(8,128)(2,1)}, u32[]{:S(2)}, u32[]{:S(2)}) collective-permute-start(bf16[256,1664]{1,0:T(8,128)(2,1)S(1)} %collective-permute-done.2.refs_6_.refs_7_), channel_id=1, source_target_pairs={{0,8},{8,0},{1,9},{9,1},{2,10},{10,2},{3,11},{11,3},{4,12},{12,4},... | collective-permute-start | bytes 2555912 | tf_op jit(solution)/shard_map/ppermute | solution.py:23
  31.8 1.6 %collective-permute-done.3.refs_7_.refs_8_ = bf16[256,1664]{1,0:T(8,128)(2,1)} collective-permute-done((bf16[256,1664]{1,0:T(8,128)(2,1)S(1)}, bf16[256,1664]{1,0:T(8,128)(2,1)}, u32[]{:S(2)}, u32[]{:S(2)}) %collective-permute-start.3) | collective-permute-done | bytes 852000 | tf_op jit(solution)/shard_map/ppermute | solution.py:23
  34.6 12.4 %attend.3 = bf16[192,1152]{1,0:T(8,128)(2,1)S(1)} custom-call(s32[27]{0:T(128)S(1)} %compare_select_fusion.2.refs_0_, s32[1]{0:T(128)} %bitcast.14.refs_1_, s32[4]{0:T(128)S(1)} %select_reduce_fusion.4.refs_2_, bf16[192,1152]{1,0:T(8,128)(2,1)S(1)} %collective-permute-done.refs_3_, bf16[256,1664]{1,0:T(8,128)(2,1)S(1)} %copy-done.3, ...), custom_call_target="tpu_custom_call" | custom-call | flops 1308622848 | bytes 4194304 | tf_op jit(solution)/shard_map/attend/pallas_call | solution.py:149
  47.1 15.1 %attend.4 = (bf16[192,1152]{1,0:T(8,128)(2,1)S(1)}, bf16[192,1152]{1,0:T(8,128)(2,1)S(1)}) custom-call(s32[51]{0:T(128)S(1)} %compare_select_fusion.1.refs_0_, s32[1]{0:T(128)} %bitcast.15.refs_1_, s32[4]{0:T(128)S(1)} %select_reduce_fusion.4.refs_2_, bf16[192,1152]{1,0:T(8,128)(2,1)S(1)} %collective-permute-done.5.refs_3_, ...), custom_call_target="tpu_custom_call" | custom-call | flops 2617245696 | bytes 4980736 | tf_op jit(solution)/shard_map/attend/pallas_call | solution.py:149
  62.3 6.1 %collective-permute-start.8 = (bf16[192,1152]{1,0:T(8,128)(2,1)S(1)}, bf16[192,1152]{1,0:T(8,128)(2,1)S(1)}, u32[]{:S(2)}, u32[]{:S(2)}) collective-permute-start(bf16[192,1152]{1,0:T(8,128)(2,1)S(1)} %get-tuple-element.28), channel_id=1, source_target_pairs={{0,16},{16,32},{32,48},{48,0},{1,17},{17,33},{33,49},{49,1},{2,18}... | collective-permute-start | bytes 1327112 | tf_op jit(solution)/shard_map/ppermute | solution.py:23
  68.4 11.3 %attend.5.refs_5_ = bf16[192,1152]{1,0:T(8,128)(2,1)S(1)} custom-call(s32[27]{0:T(128)S(1)} %compare_select_fusion.refs_0_, s32[1]{0:T(128)} %bitcast.16.refs_1_, s32[4]{0:T(128)S(1)} %select_reduce_fusion.4.refs_2_, bf16[192,1152]{1,0:T(8,128)(2,1)S(1)} %copy-done.2, bf16[256,1664]{1,0:T(8,128)(2,1)S(1)} %copy-done.3, ...), custom_call_target="tpu_custom_call" | custom-call | flops 1308622848 | bytes 4194304 | tf_op jit(solution)/shard_map/attend/pallas_call | solution.py:149
  79.8 4.6 %project.3 = (bf16[192,2048]{1,0:T(8,128)(2,1)S(1)}, bf16[192,1024]{1,0:T(8,128)(2,1)S(1)}) custom-call(s32[4]{0:T(128)S(1)} %pad_add_fusion.refs_0_, bf16[192,192]{1,0:T(8,128)(2,1)S(1)} %copy-done.1, bf16[192,1152]{1,0:T(8,128)(2,1)S(1)} %collective-permute-done.4.refs_2_, bf16[192,1152]{1,0:T(8,128)(2,1)S(1)} %collective-permute-done.7.refs_3_, ...), custom_call_target="tpu_custom_call" | custom-call | flops 805306368 | bytes 8388608 | tf_op jit(solution)/shard_map/project/pallas_call | solution.py:348
  84.4 3.0 %collective-permute-start.13 = (bf16[192,2048]{1,0:T(8,128)(2,1)S(1)}, bf16[192,2048]{1,0:T(8,128)(2,1)S(1)}, u32[]{:S(2)}, u32[]{:S(2)}) collective-permute-start(bf16[192,2048]{1,0:T(8,128)(2,1)S(1)} %get-tuple-element.38), channel_id=1, source_target_pairs={{0,1},{1,0},{2,3},{3,2},{4,5},{5,4},{6,7},{7,6},{8,9},{9,8},{10,11... | collective-permute-start | bytes 2359304 | tf_op jit(solution)/shard_map/ppermute | solution.py:23
  87.5 4.9 %project.5 = (bf16[192,1024]{1,0:T(8,128)(2,1)}, bf16[192,1024]{1,0:T(8,128)(2,1)}, bf16[192,1024]{1,0:T(8,128)(2,1)}) custom-call(s32[6]{0:T(128)S(1)} %stack.95.refs_0_, bf16[192,1024]{1,0:T(8,128)(2,1)S(1)} %get-tuple-element.30.refs_1_, bf16[1024,8192]{1,0:T(8,128)(2,1)} %refs_2_.3), custom_call_target="tpu_custom_call" | custom-call | flops 1207959552 | bytes 12582912 | tf_op jit(solution)/shard_map/project/pallas_call | solution.py:348
  92.4 1.7 %collective-permute-start.10 = (bf16[192,1024]{1,0:T(8,128)(2,1)}, bf16[192,1024]{1,0:T(8,128)(2,1)S(1)}, u32[]{:S(2)}, u32[]{:S(2)}) collective-permute-start(bf16[192,1024]{1,0:T(8,128)(2,1)} %get-tuple-element.33), channel_id=1, source_target_pairs={{0,2},{2,4},{4,6},{6,0},{1,3},{3,5},{5,7},{7,1},{8,10},{10,12},{12... | collective-permute-start | bytes 1179656 | tf_op jit(solution)/shard_map/ppermute | solution.py:23
  94.1 3.3 %collective-permute-start.11 = (bf16[192,1024]{1,0:T(8,128)(2,1)}, bf16[192,1024]{1,0:T(8,128)(2,1)S(1)}, u32[]{:S(2)}, u32[]{:S(2)}) collective-permute-start(bf16[192,1024]{1,0:T(8,128)(2,1)} %get-tuple-element.34), channel_id=1, source_target_pairs={{0,4},{2,6},{4,0},{6,2},{1,5},{3,7},{5,1},{7,3},{8,12},{10,14},{12... | collective-permute-start | bytes 1179656 | tf_op jit(solution)/shard_map/ppermute | solution.py:23
  98.2 4.1 %project.4 = (bf16[192,1024]{1,0:T(8,128)(2,1)S(1)}, bf16[192,2048]{1,0:T(8,128)(2,1)S(1)}) custom-call(s32[6]{0:T(128)S(1)} %stack.78.refs_0_, bf16[192,1024]{1,0:T(8,128)(2,1)S(1)} %get-tuple-element.30.refs_1_, bf16[1024,8192]{1,0:T(8,128)(2,1)} %refs_2_.3), custom_call_target="tpu_custom_call" | custom-call | flops 1207959552 | bytes 12582912 | tf_op jit(solution)/shard_map/project/pallas_call | solution.py:348
  102.3 2.1 %collective-permute-done.10.refs_2_ = bf16[192,1024]{1,0:T(8,128)(2,1)S(1)} collective-permute-done((bf16[192,1024]{1,0:T(8,128)(2,1)}, bf16[192,1024]{1,0:T(8,128)(2,1)S(1)}, u32[]{:S(2)}, u32[]{:S(2)}) %collective-permute-start.10) | collective-permute-done | bytes 393248 | tf_op jit(solution)/shard_map/ppermute | solution.py:23
  104.4 8.5 %collective-permute-done.11.refs_3_ = bf16[192,1024]{1,0:T(8,128)(2,1)S(1)} collective-permute-done((bf16[192,1024]{1,0:T(8,128)(2,1)}, bf16[192,1024]{1,0:T(8,128)(2,1)S(1)}, u32[]{:S(2)}, u32[]{:S(2)}) %collective-permute-start.11) | collective-permute-done | bytes 393248 | tf_op jit(solution)/shard_map/ppermute | solution.py:23
  113.5 2.3 %collective-permute-start.14 = (bf16[192,512]{1,0:T(8,128)(2,1)S(1)}, bf16[192,512]{1,0:T(8,128)(2,1)S(1)}, u32[]{:S(2)}, u32[]{:S(2)}) collective-permute-start(bf16[192,512]{1,0:T(8,128)(2,1)S(1)} %get-tuple-element.53), channel_id=1, source_target_pairs={{0,4},{2,6},{4,0},{6,2},{1,5},{3,7},{5,1},{7,3},{8,12},{10,14},{12... | collective-permute-start | bytes 589832 | tf_op jit(solution)/shard_map/ppermute | solution.py:23
  116.3 2.3 %collective-permute-start.16 = (bf16[192,512]{1,0:T(8,128)(2,1)S(1)}, bf16[192,512]{1,0:T(8,128)(2,1)S(1)}, u32[]{:S(2)}, u32[]{:S(2)}) collective-permute-start(bf16[192,512]{1,0:T(8,128)(2,1)S(1)} %get-tuple-element.51), channel_id=1, source_target_pairs={{0,6},{2,0},{4,2},{6,4},{1,7},{3,1},{5,3},{7,5},{8,14},{10,8},{12,... | collective-permute-start | bytes 589832 | tf_op jit(solution)/shard_map/ppermute | solution.py:23
  119.2 2.0 %collective-permute-done.12.refs_1_ = bf16[192,512]{1,0:T(8,128)(2,1)S(1)} collective-permute-done((bf16[192,512]{1,0:T(8,128)(2,1)S(1)}, bf16[192,512]{1,0:T(8,128)(2,1)S(1)}, u32[]{:S(2)}, u32[]{:S(2)}) %collective-permute-start.12) | collective-permute-done | bytes 196640 | tf_op jit(solution)/shard_map/ppermute | solution.py:23
  121.9 4.3 %collective-permute-done.15.refs_4_ = bf16[192,512]{1,0:T(8,128)(2,1)S(1)} collective-permute-done((bf16[192,512]{1,0:T(8,128)(2,1)S(1)}, bf16[192,512]{1,0:T(8,128)(2,1)S(1)}, u32[]{:S(2)}, u32[]{:S(2)}) %collective-permute-start.15) | collective-permute-done | bytes 196640 | tf_op jit(solution)/shard_map/ppermute | solution.py:23
  (61 shorter events, 11.3 us)
Async XLA Ops:
  3.4 65.0 %copy-start.2 = (bf16[192,1152]{1,0:T(8,128)(2,1)S(1)}, bf16[192,1152]{1,0:T(8,128)(2,1)}, u32[]{:S(2)}) copy-start(bf16[192,1152]{1,0:T(8,128)(2,1)} %get-tuple-element.24.refs_3_) | copy-start | bytes 1327108
  3.4 25.1 %collective-permute-start.5 = (bf16[192,1152]{1,0:T(8,128)(2,1)}, bf16[192,1152]{1,0:T(8,128)(2,1)S(1)}, u32[]{:S(2)}, u32[]{:S(2)}) collective-permute-start(bf16[192,1152]{1,0:T(8,128)(2,1)} %get-tuple-element.24.refs_3_), channel_id=1, source_target_pairs={{0,16},{16,32},{32,48},{48,0},{1,17},{17,33},{33,49},{49,1},{2,18}... | collective-permute-start | bytes 1327112 | tf_op jit(solution)/shard_map/ppermute | solution.py:23
  5.5 23.1 %collective-permute-start.6 = (bf16[192,1152]{1,0:T(8,128)(2,1)}, bf16[192,1152]{1,0:T(8,128)(2,1)S(1)}, u32[]{:S(2)}, u32[]{:S(2)}) collective-permute-start(bf16[192,1152]{1,0:T(8,128)(2,1)} %get-tuple-element.24.refs_3_), channel_id=1, source_target_pairs={{0,48},{16,0},{32,16},{48,32},{1,49},{17,1},{33,17},{49,33},{2,50}... | collective-permute-start | bytes 1327112 | tf_op jit(solution)/shard_map/ppermute | solution.py:23
  6.8 20.4 %collective-permute-start = (bf16[192,1152]{1,0:T(8,128)(2,1)}, bf16[192,1152]{1,0:T(8,128)(2,1)S(1)}, u32[]{:S(2)}, u32[]{:S(2)}) collective-permute-start(bf16[192,1152]{1,0:T(8,128)(2,1)} %get-tuple-element.24.refs_3_), channel_id=1, source_target_pairs={{0,32},{16,48},{32,0},{48,16},{1,33},{17,49},{33,1},{49,17},{2,34}... | collective-permute-start | bytes 1327112 | tf_op jit(solution)/shard_map/ppermute | solution.py:23
  8.5 21.2 %collective-permute-start.2 = (bf16[256,1664]{1,0:T(8,128)(2,1)}, bf16[256,1664]{1,0:T(8,128)(2,1)S(1)}, u32[]{:S(2)}, u32[]{:S(2)}) collective-permute-start(bf16[256,1664]{1,0:T(8,128)(2,1)} %get-tuple-element.25.refs_4_.refs_5_), channel_id=1, source_target_pairs={{0,64},{64,0},{1,65},{65,1},{2,66},{66,2},{3,67},{67,3},{4,68},{68... | collective-permute-start | bytes 2555912 | tf_op jit(solution)/shard_map/ppermute | solution.py:23
  9.8 22.1 %collective-permute-start.1 = (bf16[256,1664]{1,0:T(8,128)(2,1)}, bf16[256,1664]{1,0:T(8,128)(2,1)S(1)}, u32[]{:S(2)}, u32[]{:S(2)}) collective-permute-start(bf16[256,1664]{1,0:T(8,128)(2,1)} %get-tuple-element.25.refs_4_.refs_5_), channel_id=1, source_target_pairs={{0,8},{8,0},{1,9},{9,1},{2,10},{10,2},{3,11},{11,3},{4,12},{12,4},... | collective-permute-start | bytes 2555912 | tf_op jit(solution)/shard_map/ppermute | solution.py:23
  29.7 3.7 %collective-permute-start.3 = (bf16[256,1664]{1,0:T(8,128)(2,1)S(1)}, bf16[256,1664]{1,0:T(8,128)(2,1)}, u32[]{:S(2)}, u32[]{:S(2)}) collective-permute-start(bf16[256,1664]{1,0:T(8,128)(2,1)S(1)} %collective-permute-done.2.refs_6_.refs_7_), channel_id=1, source_target_pairs={{0,8},{8,0},{1,9},{9,1},{2,10},{10,2},{3,11},{11,3},{4,12},{12,4},... | collective-permute-start | bytes 2555912 | tf_op jit(solution)/shard_map/ppermute | solution.py:23
  33.4 1.2 copy-start.3
  47.0 32.8 %copy-start.1 = (bf16[192,192]{1,0:T(8,128)(2,1)S(1)}, bf16[192,192]{1,0:T(8,128)(2,1)}, u32[]{:S(2)}) copy-start(bf16[192,192]{1,0:T(8,128)(2,1)} %get-tuple-element.23.refs_1_) | copy-start | bytes 221188
  47.0 32.7 %collective-permute-start.4 = (bf16[192,1152]{1,0:T(8,128)(2,1)S(1)}, bf16[192,1152]{1,0:T(8,128)(2,1)S(1)}, u32[]{:S(2)}, u32[]{:S(2)}) collective-permute-start(bf16[192,1152]{1,0:T(8,128)(2,1)S(1)} %attend.3), channel_id=1, source_target_pairs={{0,32},{16,48},{32,0},{48,16},{1,33},{17,49},{33,1},{49,17},{2,34}... | collective-permute-start | bytes 1327112 | tf_op jit(solution)/shard_map/ppermute | solution.py:23
  62.2 17.6 %collective-permute-start.7 = (bf16[192,1152]{1,0:T(8,128)(2,1)S(1)}, bf16[192,1152]{1,0:T(8,128)(2,1)S(1)}, u32[]{:S(2)}, u32[]{:S(2)}) collective-permute-start(bf16[192,1152]{1,0:T(8,128)(2,1)S(1)} %get-tuple-element.27), channel_id=1, source_target_pairs={{0,48},{16,0},{32,16},{48,32},{1,49},{17,1},{33,17},{49,33},{2,50}... | collective-permute-start | bytes 1327112 | tf_op jit(solution)/shard_map/ppermute | solution.py:23
  62.3 17.5 %collective-permute-start.8 = (bf16[192,1152]{1,0:T(8,128)(2,1)S(1)}, bf16[192,1152]{1,0:T(8,128)(2,1)S(1)}, u32[]{:S(2)}, u32[]{:S(2)}) collective-permute-start(bf16[192,1152]{1,0:T(8,128)(2,1)S(1)} %get-tuple-element.28), channel_id=1, source_target_pairs={{0,16},{16,32},{32,48},{48,0},{1,17},{17,33},{33,49},{49,1},{2,18}... | collective-permute-start | bytes 1327112 | tf_op jit(solution)/shard_map/ppermute | solution.py:23
  84.4 28.9 %collective-permute-start.13 = (bf16[192,2048]{1,0:T(8,128)(2,1)S(1)}, bf16[192,2048]{1,0:T(8,128)(2,1)S(1)}, u32[]{:S(2)}, u32[]{:S(2)}) collective-permute-start(bf16[192,2048]{1,0:T(8,128)(2,1)S(1)} %get-tuple-element.38), channel_id=1, source_target_pairs={{0,1},{1,0},{2,3},{3,2},{4,5},{5,4},{6,7},{7,6},{8,9},{9,8},{10,11... | collective-permute-start | bytes 2359304 | tf_op jit(solution)/shard_map/ppermute | solution.py:23
  87.5 38.7 %copy-start = (bf16[192,1024]{1,0:T(8,128)(2,1)S(1)}, bf16[192,1024]{1,0:T(8,128)(2,1)}, u32[]{:S(2)}) copy-start(bf16[192,1024]{1,0:T(8,128)(2,1)} %layer_ref.1) | copy-start | bytes 1179652
  92.4 12.0 %collective-permute-start.10 = (bf16[192,1024]{1,0:T(8,128)(2,1)}, bf16[192,1024]{1,0:T(8,128)(2,1)S(1)}, u32[]{:S(2)}, u32[]{:S(2)}) collective-permute-start(bf16[192,1024]{1,0:T(8,128)(2,1)} %get-tuple-element.33), channel_id=1, source_target_pairs={{0,2},{2,4},{4,6},{6,0},{1,3},{3,5},{5,7},{7,1},{8,10},{10,12},{12... | collective-permute-start | bytes 1179656 | tf_op jit(solution)/shard_map/ppermute | solution.py:23
  94.1 18.8 %collective-permute-start.11 = (bf16[192,1024]{1,0:T(8,128)(2,1)}, bf16[192,1024]{1,0:T(8,128)(2,1)S(1)}, u32[]{:S(2)}, u32[]{:S(2)}) collective-permute-start(bf16[192,1024]{1,0:T(8,128)(2,1)} %get-tuple-element.34), channel_id=1, source_target_pairs={{0,4},{2,6},{4,0},{6,2},{1,5},{3,7},{5,1},{7,3},{8,12},{10,14},{12... | collective-permute-start | bytes 1179656 | tf_op jit(solution)/shard_map/ppermute | solution.py:23
  97.4 15.6 %collective-permute-start.9 = (bf16[192,1024]{1,0:T(8,128)(2,1)}, bf16[192,1024]{1,0:T(8,128)(2,1)S(1)}, u32[]{:S(2)}, u32[]{:S(2)}) collective-permute-start(bf16[192,1024]{1,0:T(8,128)(2,1)} %get-tuple-element.32), channel_id=1, source_target_pairs={{0,6},{2,0},{4,2},{6,4},{1,7},{3,1},{5,3},{7,5},{8,14},{10,8},{12,... | collective-permute-start | bytes 1179656 | tf_op jit(solution)/shard_map/ppermute | solution.py:23
  113.1 8.1 %collective-permute-start.12 = (bf16[192,512]{1,0:T(8,128)(2,1)S(1)}, bf16[192,512]{1,0:T(8,128)(2,1)S(1)}, u32[]{:S(2)}, u32[]{:S(2)}) collective-permute-start(bf16[192,512]{1,0:T(8,128)(2,1)S(1)} %get-tuple-element.36), channel_id=1, source_target_pairs={{0,1},{1,0},{2,3},{3,2},{4,5},{5,4},{6,7},{7,6},{8,9},{9,8},{10,11... | collective-permute-start | bytes 589832 | tf_op jit(solution)/shard_map/ppermute | solution.py:23
  113.5 8.3 %collective-permute-start.14 = (bf16[192,512]{1,0:T(8,128)(2,1)S(1)}, bf16[192,512]{1,0:T(8,128)(2,1)S(1)}, u32[]{:S(2)}, u32[]{:S(2)}) collective-permute-start(bf16[192,512]{1,0:T(8,128)(2,1)S(1)} %get-tuple-element.53), channel_id=1, source_target_pairs={{0,4},{2,6},{4,0},{6,2},{1,5},{3,7},{5,1},{7,3},{8,12},{10,14},{12... | collective-permute-start | bytes 589832 | tf_op jit(solution)/shard_map/ppermute | solution.py:23
  115.8 10.3 %collective-permute-start.15 = (bf16[192,512]{1,0:T(8,128)(2,1)S(1)}, bf16[192,512]{1,0:T(8,128)(2,1)S(1)}, u32[]{:S(2)}, u32[]{:S(2)}) collective-permute-start(bf16[192,512]{1,0:T(8,128)(2,1)S(1)} %get-tuple-element.52), channel_id=1, source_target_pairs={{0,2},{2,4},{4,6},{6,0},{1,3},{3,5},{5,7},{7,1},{8,10},{10,12},{12... | collective-permute-start | bytes 589832 | tf_op jit(solution)/shard_map/ppermute | solution.py:23
  116.3 9.9 %collective-permute-start.16 = (bf16[192,512]{1,0:T(8,128)(2,1)S(1)}, bf16[192,512]{1,0:T(8,128)(2,1)S(1)}, u32[]{:S(2)}, u32[]{:S(2)}) collective-permute-start(bf16[192,512]{1,0:T(8,128)(2,1)S(1)} %get-tuple-element.51), channel_id=1, source_target_pairs={{0,6},{2,0},{4,2},{6,4},{1,7},{3,1},{5,3},{7,5},{8,14},{10,8},{12,... | collective-permute-start | bytes 589832 | tf_op jit(solution)/shard_map/ppermute | solution.py:23

commit v8 on v7

--- a/solution.py
+++ b/solution.py
@@ -48,6 +48,7 @@
         copies.append(
             pltpu.make_async_copy(tile_refs[j].at[pl.ds(0, hd)], key_all.at[j], sems.at[2 * j])
         )
+    for j in range(4):
         copies.append(
             pltpu.make_async_copy(tile_refs[j].at[pl.ds(hd, hd)], value_in.at[j], sems.at[2 * j + 1])
         )
@@ -65,11 +66,8 @@
         value_all[j, :, hd:] = ones
     top_ref[...] = jnp.full(top_ref.shape, LOWEST, F32)
     acc_ref[...] = jnp.zeros(acc_ref.shape, F32)
-    for copy in copies:
+    for copy in copies[:4] + copies[8:]:
         copy.wait()
-    for j in range(4):
-        for k in range(0, padded, hd):
-            value_all[j, k : k + hd, :hd] = value_in[j, :, k : k + hd]
 
     def where_is(i):
         item = items[i]
@@ -113,6 +111,11 @@
         return carry
 
     score(0, first_s, first_b)
+    for copy in copies[4:8]:
+        copy.wait()
+    for j in range(4):
+        for k in range(0, padded, hd):
+            value_all[j, k : k + hd, :hd] = value_in[j, :, k : k + hd]
     lax.fori_loop(0, (count[0] + 1) // 2, pair, 0)
 
     lane = lax.broadcasted_iota(jnp.int32, (CHUNK, hd), 1)
@@ -316,33 +319,40 @@
     w_ref = refs[len(sources)]
     outs = refs[len(sources) + 1 : len(sources) + 1 + len(pieces)]
     held, sems = refs[-2:]
-    width = held.shape[2]
     copies = []
-    for i in range(sum(pieces)):
-        start = pl.multiple_of(columns[i] * width, width)
-        copies.append(pltpu.make_async_copy(w_ref.at[:, pl.ds(start, width)], held.at[i], sems.at[i]))
-        copies[-1].start()
+    for count, width in pieces:
+        for _ in range(count):
+            i = len(copies)
+            start = pl.multiple_of(columns[i] * hd, hd)
+            copies.append(
+                pltpu.make_async_copy(
+                    w_ref.at[:, pl.ds(start, width)], held.at[i, :, pl.ds(0, width)], sems.at[i]
+                )
+            )
+            copies[-1].start()
     if merge:
         attended = refs[len(sources) + 1 + len(pieces)]
         combined(sources[0], sources[1:], attended, hd, group)
     else:
         attended = sources[0]
     i = 0
-    for out_ref, count in zip(outs, pieces):
+    for out_ref, (count, width) in zip(outs, pieces):
         for c in range(count):
             copies[i].wait()
-            term = jnp.dot(attended[...], held[i], preferred_element_type=F32)
+            term = jnp.dot(attended[...], held[i, :, :width], preferred_element_type=F32)
             out_ref[:, c * width : (c + 1) * width] = term.astype(BF16)
             i += 1
 
 
-def project(sources, weight, columns, pieces, width, hd):
+def project(sources, weight, columns, pieces, hd):
     merge = len(sources) > 1
     tokens = sources[-1].shape[0]
     depth = weight.shape[0]
-    total = sum(pieces)
+    total = sum(count for count, _ in pieces)
+    widest = max(width for _, width in pieces)
+    area = sum(count * width for count, width in pieces)
     here = pl.BlockSpec(memory_space=pltpu.VMEM)
-    results = [jax.ShapeDtypeStruct((tokens, width * count), BF16) for count in pieces]
+    results = [jax.ShapeDtypeStruct((tokens, width * count), BF16) for count, width in pieces]
     if merge:
         results.append(jax.ShapeDtypeStruct((tokens, depth), BF16))
     return pl.pallas_call(
@@ -354,12 +364,12 @@
             in_specs=[here] * len(sources) + [pl.BlockSpec(memory_space=pl.ANY)],
             out_specs=[here] * len(results),
             scratch_shapes=[
-                pltpu.VMEM((total, depth, width), BF16),
+                pltpu.VMEM((total, depth, widest), BF16),
                 pltpu.SemaphoreType.DMA((total,)),
             ],
         ),
         cost_estimate=pl.CostEstimate(
-            flops=2 * tokens * depth * width * total, bytes_accessed=4 * depth * width * total, transcendentals=0
+            flops=2 * tokens * depth * area, bytes_accessed=4 * depth * area, transcendentals=0
         ),
         compiler_params=pltpu.CompilerParams(vmem_limit_bytes=50 << 20),
         name="project",
@@ -391,8 +401,8 @@
 
 def settle_kernel(gate_ref, layer_ref, *refs):
     parts, out_ref = refs[:-1], refs[-1]
-    half = out_ref.shape[1] // 2
-    for at, some in ((slice(0, half), parts[:2]), (slice(half, None), parts[2:])):
+    cut = parts[0].shape[1]
+    for at, some in ((slice(0, cut), parts[:2]), (slice(cut, None), parts[2:])):
         total = some[0][...]
         for ref in some[1:]:
             total = total + ref[...].astype(F32)
@@ -404,12 +414,12 @@
     cuts = 2
     rows = tokens // cuts
     wide = pl.BlockSpec((rows, width), lambda g: (g, 0))
-    part = pl.BlockSpec((rows, width // 2), lambda g: (g, 0))
+    each = [pl.BlockSpec((rows, part.shape[1]), lambda g: (g, 0)) for part in parts]
     return pl.pallas_call(
         settle_kernel,
         out_shape=jax.ShapeDtypeStruct((tokens, width), BF16),
         grid=(cuts,),
-        in_specs=[pl.BlockSpec(memory_space=pltpu.SMEM), wide] + [part] * len(parts),
+        in_specs=[pl.BlockSpec(memory_space=pltpu.SMEM), wide] + each,
         out_specs=wide,
         compiler_params=pltpu.CompilerParams(vmem_limit_bytes=24 << 20),
         name="settle",
@@ -468,24 +478,27 @@
         parts.update(zip(turns, got))
     parts = {s: part if s == 0 else shifted(part, "x", nx - s) for s, part in parts.items()}
 
-    half = width // 2
+    some, rest = width * 3 // 8, width * 5 // 8
 
     def first(dz, dy):
-        return ((z + dz) % nz * nyh + (yh + dy) % nyh) * 2
+        return ((z + dz) % nz * nyh + (yh + dy) % nyh) * (width // hd)
+
+    def second(dz, dy):
+        return first(dz, dy) + some // hd
 
     sources = [back] + [parts[s] for s in (2, 1, 3, 0)]
     over_y, attended = project(
-        sources, out_weight, [first(dz, 1) + 1 for dz in (1, 2, 3, 0)], (4,), half, hd
+        sources, out_weight, [second(dz, 1) for dz in (1, 2, 3, 0)], ((4, rest),), hd
     )
     got_y = shifted(over_y, "yh", 1)
     far = [first(dz, dy) for dz in (2, 1, 3) for dy in (1, 0)]
-    over_z = project([attended], out_weight, far, (2, 2, 2), half, hd)
+    over_z = project([attended], out_weight, far, ((2, some),) * 3, hd)
     got_z = [shifted(term, "z", dz) for dz, term in zip((2, 1, 3), over_z)]
-    near = [first(0, 1), first(0, 0)] + [first(dz, 0) + 1 for dz in (1, 2, 3, 0)]
-    own_z, own_y = project([attended], out_weight, near, (2, 4), half, hd)
-    late_z, kept_b = add_up([own_y, got_y], half)
-    ends_b = [shifted(late_z[:, i * half : (i + 1) * half], "z", i + 1) for i in (1, 0, 2)]
-    late_y, kept_a = add_up([own_z] + got_z[::-1], half)
+    near = [first(0, 1), first(0, 0)] + [second(dz, 0) for dz in (1, 2, 3, 0)]
+    own_z, own_y = project([attended], out_weight, near, ((2, some), (4, rest)), hd)
+    late_z, kept_b = add_up([own_y, got_y], rest)
+    ends_b = [shifted(late_z[:, i * rest : (i + 1) * rest], "z", i + 1) for i in (1, 0, 2)]
+    late_y, kept_a = add_up([own_z] + got_z[::-1], some)
     end_a = shifted(late_y, "yh", 1)
     return settle(jnp.tanh(attn_gate), layer_input, [kept_a, end_a, kept_b] + ends_b)
 

time: 127 us -> 119 us (0.937)
  the two profiles are of different devices: /device:TPU:1 before, /device:TPU:12 now
where the time goes in v8:
time: 119 us; the launch traced here: 121 us
  Pallas kernels  62.2 us (52%)
  starting transfers between devices  26.4 us (22%)
  waiting for transfers between devices  25.3 us (21%)
  other arithmetic  3.74 us (3%)
  local copies, waits for them, and re-layouts  2.87 us (2%)
    pallas_call x3, Pallas kernels, attend(): pl.pallas_call(lambda *refs: attend_kernel(*refs, scale=1.0 / math.sqrt(h...  44 us
    ppermute x17, starting transfers between devices, shifted(): lax.ppermute(value, axis, [(s, (s + steps) % count) for s in range(count)])  26.4 us
    ppermute x17, waiting for transfers between devices, shifted(): lax.ppermute(value, axis, [(s, (s + steps) % count) for s in range(count)])  25.3 us
    pallas_call x3, Pallas kernels, project(): pl.pallas_call(lambda *refs: project_kernel(*refs, hd=hd, group=depth //...  13.5 us
    pallas_call x1, Pallas kernels, prepare(): pl.pallas_call(prepare_kernel, out_shape=[jax.ShapeDtypeStruct((2 * hd, p...  3.36 us
  transfers between devices with their start and end apart: 17, of which 4 were waited for; matrix products, arithmetic and copies ran while one was open for 4% of the time, Pallas kernels for 34%

profile of v8, /device:TPU:12, one launch (start us, length us, event | category | flops | bytes accessed | tf_op | source)
XLA Modules:
  0.0 121.5 jit_solution(5344089356782982435)
XLA Ops:
  0.0 3.4 %prepare.1 = (bf16[256,1664]{1,0:T(8,128)(2,1)}, bf16[192,1152]{1,0:T(8,128)(2,1)}, bf16[192,192]{1,0:T(8,128)(2,1)}) custom-call(s32[8]{0:T(128)} %counts.1, s32[2,192]{1,0:T(2,128)} %range_ref.1, bf16[1601,128]{1,0:T(8,128)(2,1)} %key_hbm.1, bf16[1601,128]{1,0:T(8,128)(2,1)} %value_hbm.1, bf16[192,1024]{1,0:T(8,128)(2,1)} %q_hbm.1), custom_call_target="tpu_custom_call" | custom-call | tf_op jit(solution)/shard_map/prepare/pallas_call | solution.py:262
  3.4 1.3 %collective-permute-start.5 = (bf16[192,1152]{1,0:T(8,128)(2,1)}, bf16[192,1152]{1,0:T(8,128)(2,1)S(1)}, u32[]{:S(2)}, u32[]{:S(2)}) collective-permute-start(bf16[192,1152]{1,0:T(8,128)(2,1)} %get-tuple-element.24.refs_3_), channel_id=1, source_target_pairs={{0,16},{16,32},{32,48},{48,0},{1,17},{17,33},{33,49},{49,1},{2,18}... | collective-permute-start | bytes 1327112 | tf_op jit(solution)/shard_map/ppermute | solution.py:23
  5.5 1.7 %collective-permute-start = (bf16[192,1152]{1,0:T(8,128)(2,1)}, bf16[192,1152]{1,0:T(8,128)(2,1)S(1)}, u32[]{:S(2)}, u32[]{:S(2)}) collective-permute-start(bf16[192,1152]{1,0:T(8,128)(2,1)} %get-tuple-element.24.refs_3_), channel_id=1, source_target_pairs={{0,32},{16,48},{32,0},{48,16},{1,33},{17,49},{33,1},{49,17},{2,34}... | collective-permute-start | bytes 1327112 | tf_op jit(solution)/shard_map/ppermute | solution.py:23
  9.7 15.3 %collective-permute-done.refs_3_ = bf16[192,1152]{1,0:T(8,128)(2,1)S(1)} collective-permute-done((bf16[192,1152]{1,0:T(8,128)(2,1)}, bf16[192,1152]{1,0:T(8,128)(2,1)S(1)}, u32[]{:S(2)}, u32[]{:S(2)}) %collective-permute-start) | collective-permute-done | bytes 442400 | tf_op jit(solution)/shard_map/ppermute | solution.py:23
  28.1 1.9 %collective-permute-done.3.refs_7_.refs_8_ = bf16[256,1664]{1,0:T(8,128)(2,1)} collective-permute-done((bf16[256,1664]{1,0:T(8,128)(2,1)S(1)}, bf16[256,1664]{1,0:T(8,128)(2,1)}, u32[]{:S(2)}, u32[]{:S(2)}) %collective-permute-start.3) | collective-permute-done | bytes 852000 | tf_op jit(solution)/shard_map/ppermute | solution.py:23
  30.1 1.2 copy-done.3
  31.2 12.0 %attend.3 = bf16[192,1152]{1,0:T(8,128)(2,1)S(1)} custom-call(s32[27]{0:T(128)S(1)} %compare_select_fusion.2.refs_0_, s32[1]{0:T(128)} %bitcast.14.refs_1_, s32[4]{0:T(128)S(1)} %select_reduce_fusion.4.refs_2_, bf16[192,1152]{1,0:T(8,128)(2,1)S(1)} %collective-permute-done.refs_3_, bf16[256,1664]{1,0:T(8,128)(2,1)S(1)} %copy-done.3, ...), custom_call_target="tpu_custom_call" | custom-call | flops 1308622848 | bytes 4194304 | tf_op jit(solution)/shard_map/attend/pallas_call | solution.py:152
  43.2 1.5 %collective-permute-start.4 = (bf16[192,1152]{1,0:T(8,128)(2,1)S(1)}, bf16[192,1152]{1,0:T(8,128)(2,1)S(1)}, u32[]{:S(2)}, u32[]{:S(2)}) collective-permute-start(bf16[192,1152]{1,0:T(8,128)(2,1)S(1)} %attend.3), channel_id=1, source_target_pairs={{0,32},{16,48},{32,0},{48,16},{1,33},{17,49},{33,1},{49,17},{2,34}... | collective-permute-start | bytes 1327112 | tf_op jit(solution)/shard_map/ppermute | solution.py:23
  44.7 20.0 %attend.4 = (bf16[192,1152]{1,0:T(8,128)(2,1)S(1)}, bf16[192,1152]{1,0:T(8,128)(2,1)S(1)}) custom-call(s32[51]{0:T(128)S(1)} %compare_select_fusion.1.refs_0_, s32[1]{0:T(128)} %bitcast.15.refs_1_, s32[4]{0:T(128)S(1)} %select_reduce_fusion.4.refs_2_, bf16[192,1152]{1,0:T(8,128)(2,1)S(1)} %collective-permute-done.5.refs_3_, ...), custom_call_target="tpu_custom_call" | custom-call | flops 2617245696 | bytes 4980736 | tf_op jit(solution)/shard_map/attend/pallas_call | solution.py:152
  64.8 2.0 %collective-permute-start.8 = (bf16[192,1152]{1,0:T(8,128)(2,1)S(1)}, bf16[192,1152]{1,0:T(8,128)(2,1)S(1)}, u32[]{:S(2)}, u32[]{:S(2)}) collective-permute-start(bf16[192,1152]{1,0:T(8,128)(2,1)S(1)} %get-tuple-element.28), channel_id=1, source_target_pairs={{0,16},{16,32},{32,48},{48,0},{1,17},{17,33},{33,49},{49,1},{2,18}... | collective-permute-start | bytes 1327112 | tf_op jit(solution)/shard_map/ppermute | solution.py:23
  66.9 12.0 %attend.5.refs_5_ = bf16[192,1152]{1,0:T(8,128)(2,1)S(1)} custom-call(s32[27]{0:T(128)S(1)} %compare_select_fusion.refs_0_, s32[1]{0:T(128)} %bitcast.16.refs_1_, s32[4]{0:T(128)S(1)} %select_reduce_fusion.4.refs_2_, bf16[192,1152]{1,0:T(8,128)(2,1)S(1)} %copy-done.2, bf16[256,1664]{1,0:T(8,128)(2,1)S(1)} %copy-done.3, ...), custom_call_target="tpu_custom_call" | custom-call | flops 1308622848 | bytes 4194304 | tf_op jit(solution)/shard_map/attend/pallas_call | solution.py:152
  79.0 5.1 %project.3 = (bf16[192,2560]{1,0:T(8,128)(2,1)S(1)}, bf16[192,1024]{1,0:T(8,128)(2,1)S(1)}) custom-call(s32[4]{0:T(128)S(1)} %pad_add_fusion.refs_0_, bf16[192,192]{1,0:T(8,128)(2,1)S(1)} %copy-done.1, bf16[192,1152]{1,0:T(8,128)(2,1)S(1)} %collective-permute-done.4.refs_2_, bf16[192,1152]{1,0:T(8,128)(2,1)S(1)} %collective-permute-done.7.refs_3_, ...), custom_call_target="tpu_custom_call" | custom-call | flops 1006632960 | bytes 10485760 | tf_op jit(solution)/shard_map/project/pallas_call | solution.py:358
  84.1 2.4 %collective-permute-start.13 = (bf16[192,2560]{1,0:T(8,128)(2,1)S(1)}, bf16[192,2560]{1,0:T(8,128)(2,1)S(1)}, u32[]{:S(2)}, u32[]{:S(2)}) collective-permute-start(bf16[192,2560]{1,0:T(8,128)(2,1)S(1)} %get-tuple-element.38), channel_id=1, source_target_pairs={{0,1},{1,0},{2,3},{3,2},{4,5},{5,4},{6,7},{7,6},{8,9},{9,8},{10,11... | collective-permute-start | bytes 2949128 | tf_op jit(solution)/shard_map/ppermute | solution.py:23
  86.6 4.0 %project.5 = (bf16[192,768]{1,0:T(8,128)(2,1)S(1)}, bf16[192,768]{1,0:T(8,128)(2,1)S(1)}, bf16[192,768]{1,0:T(8,128)(2,1)S(1)}) custom-call(s32[6]{0:T(128)S(1)} %stack.95.refs_0_, bf16[192,1024]{1,0:T(8,128)(2,1)S(1)} %get-tuple-element.30.refs_1_, bf16[1024,8192]{1,0:T(8,128)(2,1)} %refs_2_.3), custom_call_target="tpu_custom_call" | custom-call | flops 905969664 | bytes 9437184 | tf_op jit(solution)/shard_map/project/pallas_call | solution.py:358
  90.6 2.0 %collective-permute-start.10 = (bf16[192,768]{1,0:T(8,128)(2,1)S(1)}, bf16[192,768]{1,0:T(8,128)(2,1)S(1)}, u32[]{:S(2)}, u32[]{:S(2)}) collective-permute-start(bf16[192,768]{1,0:T(8,128)(2,1)S(1)} %get-tuple-element.33), channel_id=1, source_target_pairs={{0,2},{2,4},{4,6},{6,0},{1,3},{3,5},{5,7},{7,1},{8,10},{10,12},{12... | collective-permute-start | bytes 884744 | tf_op jit(solution)/shard_map/ppermute | solution.py:23
  92.6 4.4 %project.4 = (bf16[192,768]{1,0:T(8,128)(2,1)S(1)}, bf16[192,2560]{1,0:T(8,128)(2,1)S(1)}) custom-call(s32[6]{0:T(128)S(1)} %stack.78.refs_0_, bf16[192,1024]{1,0:T(8,128)(2,1)S(1)} %get-tuple-element.30.refs_1_, bf16[1024,8192]{1,0:T(8,128)(2,1)} %refs_2_.3), custom_call_target="tpu_custom_call" | custom-call | flops 1308622848 | bytes 13631488 | tf_op jit(solution)/shard_map/project/pallas_call | solution.py:358
  97.0 3.7 %collective-permute-start.11 = (bf16[192,768]{1,0:T(8,128)(2,1)S(1)}, bf16[192,768]{1,0:T(8,128)(2,1)S(1)}, u32[]{:S(2)}, u32[]{:S(2)}) collective-permute-start(bf16[192,768]{1,0:T(8,128)(2,1)S(1)} %get-tuple-element.34), channel_id=1, source_target_pairs={{0,4},{2,6},{4,0},{6,2},{1,5},{3,7},{5,1},{7,3},{8,12},{10,14},{12... | collective-permute-start | bytes 884744 | tf_op jit(solution)/shard_map/ppermute | solution.py:23
  100.7 1.1 collective-permute-start.9
  101.7 4.3 %collective-permute-done.13.refs_1_ = bf16[192,2560]{1,0:T(8,128)(2,1)S(1)} collective-permute-done((bf16[192,2560]{1,0:T(8,128)(2,1)S(1)}, bf16[192,2560]{1,0:T(8,128)(2,1)S(1)}, u32[]{:S(2)}, u32[]{:S(2)}) %collective-permute-start.13) | collective-permute-done | bytes 983072 | tf_op jit(solution)/shard_map/ppermute | solution.py:23
  106.4 4.0 %collective-permute-start.14 = (bf16[192,640]{1,0:T(8,128)(2,1)S(1)}, bf16[192,640]{1,0:T(8,128)(2,1)S(1)}, u32[]{:S(2)}, u32[]{:S(2)}) collective-permute-start(bf16[192,640]{1,0:T(8,128)(2,1)S(1)} %get-tuple-element.53), channel_id=1, source_target_pairs={{0,4},{2,6},{4,0},{6,2},{1,5},{3,7},{5,1},{7,3},{8,12},{10,14},{12... | collective-permute-start | bytes 737288 | tf_op jit(solution)/shard_map/ppermute | solution.py:23
  110.4 1.0 collective-permute-start.15
  111.4 2.2 %collective-permute-start.16 = (bf16[192,640]{1,0:T(8,128)(2,1)S(1)}, bf16[192,640]{1,0:T(8,128)(2,1)S(1)}, u32[]{:S(2)}, u32[]{:S(2)}) collective-permute-start(bf16[192,640]{1,0:T(8,128)(2,1)S(1)} %get-tuple-element.51), channel_id=1, source_target_pairs={{0,6},{2,0},{4,2},{6,4},{1,7},{3,1},{5,3},{7,5},{8,14},{10,8},{12,... | collective-permute-start | bytes 737288 | tf_op jit(solution)/shard_map/ppermute | solution.py:23
  113.8 2.4 %collective-permute-start.12 = (bf16[192,384]{1,0:T(8,128)(2,1)S(1)}, bf16[192,384]{1,0:T(8,128)(2,1)S(1)}, u32[]{:S(2)}, u32[]{:S(2)}) collective-permute-start(bf16[192,384]{1,0:T(8,128)(2,1)S(1)} %get-tuple-element.36), channel_id=1, source_target_pairs={{0,1},{1,0},{2,3},{3,2},{4,5},{5,4},{6,7},{7,6},{8,9},{9,8},{10,11... | collective-permute-start | bytes 442376 | tf_op jit(solution)/shard_map/ppermute | solution.py:23
  116.8 3.7 %collective-permute-done.12.refs_1_ = bf16[192,384]{1,0:T(8,128)(2,1)S(1)} collective-permute-done((bf16[192,384]{1,0:T(8,128)(2,1)S(1)}, bf16[192,384]{1,0:T(8,128)(2,1)S(1)}, u32[]{:S(2)}, u32[]{:S(2)}) %collective-permute-start.12) | collective-permute-done | bytes 147488 | tf_op jit(solution)/shard_map/ppermute | solution.py:23
  (61 shorter events, 8.1 us)
Async XLA Ops:
  3.4 63.5 %copy-start.2 = (bf16[192,1152]{1,0:T(8,128)(2,1)S(1)}, bf16[192,1152]{1,0:T(8,128)(2,1)}, u32[]{:S(2)}) copy-start(bf16[192,1152]{1,0:T(8,128)(2,1)} %get-tuple-element.24.refs_3_) | copy-start | bytes 1327108
  3.4 22.9 %collective-permute-start.5 = (bf16[192,1152]{1,0:T(8,128)(2,1)}, bf16[192,1152]{1,0:T(8,128)(2,1)S(1)}, u32[]{:S(2)}, u32[]{:S(2)}) collective-permute-start(bf16[192,1152]{1,0:T(8,128)(2,1)} %get-tuple-element.24.refs_3_), channel_id=1, source_target_pairs={{0,16},{16,32},{32,48},{48,0},{1,17},{17,33},{33,49},{49,1},{2,18}... | collective-permute-start | bytes 1327112 | tf_op jit(solution)/shard_map/ppermute | solution.py:23
  4.6 21.8 %collective-permute-start.6 = (bf16[192,1152]{1,0:T(8,128)(2,1)}, bf16[192,1152]{1,0:T(8,128)(2,1)S(1)}, u32[]{:S(2)}, u32[]{:S(2)}) collective-permute-start(bf16[192,1152]{1,0:T(8,128)(2,1)} %get-tuple-element.24.refs_3_), channel_id=1, source_target_pairs={{0,48},{16,0},{32,16},{48,32},{1,49},{17,1},{33,17},{49,33},{2,50}... | collective-permute-start | bytes 1327112 | tf_op jit(solution)/shard_map/ppermute | solution.py:23
  5.5 19.6 %collective-permute-start = (bf16[192,1152]{1,0:T(8,128)(2,1)}, bf16[192,1152]{1,0:T(8,128)(2,1)S(1)}, u32[]{:S(2)}, u32[]{:S(2)}) collective-permute-start(bf16[192,1152]{1,0:T(8,128)(2,1)} %get-tuple-element.24.refs_3_), channel_id=1, source_target_pairs={{0,32},{16,48},{32,0},{48,16},{1,33},{17,49},{33,1},{49,17},{2,34}... | collective-permute-start | bytes 1327112 | tf_op jit(solution)/shard_map/ppermute | solution.py:23
  7.2 20.4 %collective-permute-start.2 = (bf16[256,1664]{1,0:T(8,128)(2,1)}, bf16[256,1664]{1,0:T(8,128)(2,1)S(1)}, u32[]{:S(2)}, u32[]{:S(2)}) collective-permute-start(bf16[256,1664]{1,0:T(8,128)(2,1)} %get-tuple-element.25.refs_4_.refs_5_), channel_id=1, source_target_pairs={{0,64},{64,0},{1,65},{65,1},{2,66},{66,2},{3,67},{67,3},{4,68},{68... | collective-permute-start | bytes 2555912 | tf_op jit(solution)/shard_map/ppermute | solution.py:23
  7.6 20.6 %collective-permute-start.1 = (bf16[256,1664]{1,0:T(8,128)(2,1)}, bf16[256,1664]{1,0:T(8,128)(2,1)S(1)}, u32[]{:S(2)}, u32[]{:S(2)}) collective-permute-start(bf16[256,1664]{1,0:T(8,128)(2,1)} %get-tuple-element.25.refs_4_.refs_5_), channel_id=1, source_target_pairs={{0,8},{8,0},{1,9},{9,1},{2,10},{10,2},{3,11},{11,3},{4,12},{12,4},... | collective-permute-start | bytes 2555912 | tf_op jit(solution)/shard_map/ppermute | solution.py:23
  27.6 2.5 %collective-permute-start.3 = (bf16[256,1664]{1,0:T(8,128)(2,1)S(1)}, bf16[256,1664]{1,0:T(8,128)(2,1)}, u32[]{:S(2)}, u32[]{:S(2)}) collective-permute-start(bf16[256,1664]{1,0:T(8,128)(2,1)S(1)} %collective-permute-done.2.refs_6_.refs_7_), channel_id=1, source_target_pairs={{0,8},{8,0},{1,9},{9,1},{2,10},{10,2},{3,11},{11,3},{4,12},{12,4},... | collective-permute-start | bytes 2555912 | tf_op jit(solution)/shard_map/ppermute | solution.py:23
  30.1 1.2 copy-start.3
  43.2 35.8 %copy-start.1 = (bf16[192,192]{1,0:T(8,128)(2,1)S(1)}, bf16[192,192]{1,0:T(8,128)(2,1)}, u32[]{:S(2)}) copy-start(bf16[192,192]{1,0:T(8,128)(2,1)} %get-tuple-element.23.refs_1_) | copy-start | bytes 221188
  43.2 35.7 %collective-permute-start.4 = (bf16[192,1152]{1,0:T(8,128)(2,1)S(1)}, bf16[192,1152]{1,0:T(8,128)(2,1)S(1)}, u32[]{:S(2)}, u32[]{:S(2)}) collective-permute-start(bf16[192,1152]{1,0:T(8,128)(2,1)S(1)} %attend.3), channel_id=1, source_target_pairs={{0,32},{16,48},{32,0},{48,16},{1,33},{17,49},{33,1},{49,17},{2,34}... | collective-permute-start | bytes 1327112 | tf_op jit(solution)/shard_map/ppermute | solution.py:23
  64.7 14.2 %collective-permute-start.7 = (bf16[192,1152]{1,0:T(8,128)(2,1)S(1)}, bf16[192,1152]{1,0:T(8,128)(2,1)S(1)}, u32[]{:S(2)}, u32[]{:S(2)}) collective-permute-start(bf16[192,1152]{1,0:T(8,128)(2,1)S(1)} %get-tuple-element.27), channel_id=1, source_target_pairs={{0,48},{16,0},{32,16},{48,32},{1,49},{17,1},{33,17},{49,33},{2,50}... | collective-permute-start | bytes 1327112 | tf_op jit(solution)/shard_map/ppermute | solution.py:23
  64.8 14.1 %collective-permute-start.8 = (bf16[192,1152]{1,0:T(8,128)(2,1)S(1)}, bf16[192,1152]{1,0:T(8,128)(2,1)S(1)}, u32[]{:S(2)}, u32[]{:S(2)}) collective-permute-start(bf16[192,1152]{1,0:T(8,128)(2,1)S(1)} %get-tuple-element.28), channel_id=1, source_target_pairs={{0,16},{16,32},{32,48},{48,0},{1,17},{17,33},{33,49},{49,1},{2,18}... | collective-permute-start | bytes 1327112 | tf_op jit(solution)/shard_map/ppermute | solution.py:23
  84.1 22.0 %collective-permute-start.13 = (bf16[192,2560]{1,0:T(8,128)(2,1)S(1)}, bf16[192,2560]{1,0:T(8,128)(2,1)S(1)}, u32[]{:S(2)}, u32[]{:S(2)}) collective-permute-start(bf16[192,2560]{1,0:T(8,128)(2,1)S(1)} %get-tuple-element.38), channel_id=1, source_target_pairs={{0,1},{1,0},{2,3},{3,2},{4,5},{5,4},{6,7},{7,6},{8,9},{9,8},{10,11... | collective-permute-start | bytes 2949128 | tf_op jit(solution)/shard_map/ppermute | solution.py:23
  86.6 33.9 %copy-start = (bf16[192,1024]{1,0:T(8,128)(2,1)S(1)}, bf16[192,1024]{1,0:T(8,128)(2,1)}, u32[]{:S(2)}) copy-start(bf16[192,1024]{1,0:T(8,128)(2,1)} %layer_ref.1) | copy-start | bytes 1179652
  90.6 20.8 %collective-permute-start.10 = (bf16[192,768]{1,0:T(8,128)(2,1)S(1)}, bf16[192,768]{1,0:T(8,128)(2,1)S(1)}, u32[]{:S(2)}, u32[]{:S(2)}) collective-permute-start(bf16[192,768]{1,0:T(8,128)(2,1)S(1)} %get-tuple-element.33), channel_id=1, source_target_pairs={{0,2},{2,4},{4,6},{6,0},{1,3},{3,5},{5,7},{7,1},{8,10},{10,12},{12... | collective-permute-start | bytes 884744 | tf_op jit(solution)/shard_map/ppermute | solution.py:23
  97.0 16.6 %collective-permute-start.11 = (bf16[192,768]{1,0:T(8,128)(2,1)S(1)}, bf16[192,768]{1,0:T(8,128)(2,1)S(1)}, u32[]{:S(2)}, u32[]{:S(2)}) collective-permute-start(bf16[192,768]{1,0:T(8,128)(2,1)S(1)} %get-tuple-element.34), channel_id=1, source_target_pairs={{0,4},{2,6},{4,0},{6,2},{1,5},{3,7},{5,1},{7,3},{8,12},{10,14},{12... | collective-permute-start | bytes 884744 | tf_op jit(solution)/shard_map/ppermute | solution.py:23
  100.7 12.9 %collective-permute-start.9 = (bf16[192,768]{1,0:T(8,128)(2,1)S(1)}, bf16[192,768]{1,0:T(8,128)(2,1)S(1)}, u32[]{:S(2)}, u32[]{:S(2)}) collective-permute-start(bf16[192,768]{1,0:T(8,128)(2,1)S(1)} %get-tuple-element.32), channel_id=1, source_target_pairs={{0,6},{2,0},{4,2},{6,4},{1,7},{3,1},{5,3},{7,5},{8,14},{10,8},{12,... | collective-permute-start | bytes 884744 | tf_op jit(solution)/shard_map/ppermute | solution.py:23
  106.4 14.1 %collective-permute-start.14 = (bf16[192,640]{1,0:T(8,128)(2,1)S(1)}, bf16[192,640]{1,0:T(8,128)(2,1)S(1)}, u32[]{:S(2)}, u32[]{:S(2)}) collective-permute-start(bf16[192,640]{1,0:T(8,128)(2,1)S(1)} %get-tuple-element.53), channel_id=1, source_target_pairs={{0,4},{2,6},{4,0},{6,2},{1,5},{3,7},{5,1},{7,3},{8,12},{10,14},{12... | collective-permute-start | bytes 737288 | tf_op jit(solution)/shard_map/ppermute | solution.py:23
  110.4 10.1 %collective-permute-start.15 = (bf16[192,640]{1,0:T(8,128)(2,1)S(1)}, bf16[192,640]{1,0:T(8,128)(2,1)S(1)}, u32[]{:S(2)}, u32[]{:S(2)}) collective-permute-start(bf16[192,640]{1,0:T(8,128)(2,1)S(1)} %get-tuple-element.52), channel_id=1, source_target_pairs={{0,2},{2,4},{4,6},{6,0},{1,3},{3,5},{5,7},{7,1},{8,10},{10,12},{12... | collective-permute-start | bytes 737288 | tf_op jit(solution)/shard_map/ppermute | solution.py:23
  111.4 9.1 %collective-permute-start.16 = (bf16[192,640]{1,0:T(8,128)(2,1)S(1)}, bf16[192,640]{1,0:T(8,128)(2,1)S(1)}, u32[]{:S(2)}, u32[]{:S(2)}) collective-permute-start(bf16[192,640]{1,0:T(8,128)(2,1)S(1)} %get-tuple-element.51), channel_id=1, source_target_pairs={{0,6},{2,0},{4,2},{6,4},{1,7},{3,1},{5,3},{7,5},{8,14},{10,8},{12,... | collective-permute-start | bytes 737288 | tf_op jit(solution)/shard_map/ppermute | solution.py:23
  113.8 6.7 %collective-permute-start.12 = (bf16[192,384]{1,0:T(8,128)(2,1)S(1)}, bf16[192,384]{1,0:T(8,128)(2,1)S(1)}, u32[]{:S(2)}, u32[]{:S(2)}) collective-permute-start(bf16[192,384]{1,0:T(8,128)(2,1)S(1)} %get-tuple-element.36), channel_id=1, source_target_pairs={{0,1},{1,0},{2,3},{3,2},{4,5},{5,4},{6,7},{7,6},{8,9},{9,8},{10,11... | collective-permute-start | bytes 442376 | tf_op jit(solution)/shard_map/ppermute | solution.py:23
